TPU v7x, 256 devices: a whole 4x4x8 slice. The times are simulated.
256 devices in a mesh: gx: 8 (over z_lo, core), gy: 4 (over x), sa: 8 (over z_hi, y).
Axes of the slice: x: 4, y: 4, z: 8 (z_hi: 2, z_lo: 4; z = z_hi * 4 + z_lo), core: 2. Of those that a mesh axis runs over, the one named last changes fastest.
Arguments:
- field_now: float32 [160, 256, 1024], P('sa', 'gy', 'gx'), may hold values from -1.5 to 1.5
- field_before: float32 [160, 256, 1024], P('sa', 'gy', 'gx'), may hold values from -1.5 to 1.5
- source: float32 [160, 256, 1024], P('sa', 'gy', 'gx'), may hold values from -0.06 to 0.06
- log_fields: float32 [9, 256, 1024], P(None, ('gy', 'sa'), 'gx'), may hold values from -0.15 to 0.15
- weights: float32 [1500], replicated, may hold values from 0.0002 to 0.002
- mean_perm: float32 [], replicated, may hold values from 0.5 to 2
- node_index: int32 [1500, 8], replicated, may hold values from 0 to 6
- mode_index: int32 [160, 8], replicated, may hold values from 0 to 3, as said below
Outputs:
- fresh: float32 [160, 256, 1024], P('sa', 'gy', 'gx')
- update: float32 [160, 256, 1024], P('sa', 'gy', 'gx')
Inputs may be any that keep to these rules, and one draw needn't show every extreme that they name: `node_index`: each entry numbers a point of the list in the first step. `mode_index`: the rows are distinct multi-indices of total degree at most 3.
All inputs are finite; a program needn't handle non-finite values.
Results may differ from a plain program's by a relative error of at most 0.0003.
Values sent between devices are 32-bit elements; how exact they have to be, the bound alone decides.
No kernel may reach another device: no remote copies, remote signals or barrier semaphores. Data moves between devices by JAX's collectives and lax.ppermute only.
A program may use at most 64 MiB of HBM per device.

v0:
```python
import functools
import math

import jax
import jax.numpy as jnp
import numpy as np
from jax import lax
from jax.experimental import pallas as pl
from jax.experimental.pallas import tpu as pltpu
from jax.sharding import PartitionSpec as P

HIGHEST = lax.Precision.HIGHEST
hermite_points = (
    0.0,
    -1.7320508075688772,
    1.7320508075688772,
    -1.355626179974266,
    1.355626179974266,
    -2.8569700138728056,
    2.8569700138728056,
)
storage_rate = 0.0004
relax_weight = 1.6
step_length = 0.3
QB = 256
LANES = 128


def halves(x):
    top = lax.reduce_precision(x, 8, 7)
    return top.astype(jnp.bfloat16), (x - top).astype(jnp.bfloat16)


def split(x):
    top = x.astype(jnp.bfloat16)
    return top, (x - top.astype(jnp.float32)).astype(jnp.bfloat16)


def cosine_matrix(length):
    k = np.arange(length)[:, None]
    m = np.arange(length)[None, :]
    phase = (k * (2 * m + 1)) % (4 * length)
    factor = np.where(k == 0, math.sqrt(1.0 / length), math.sqrt(2.0 / length))
    return factor * np.cos(phase * (math.pi / (2 * length)))


def eigen_values(count, length):
    return 4.0 * np.sin(np.arange(count) * (math.pi / (2 * length))) ** 2


def node_tables(node_index, mode_index, weights):
    q = node_index.shape[0]
    pad = -q % QB
    index = jnp.pad(node_index.T, ((0, 0), (0, pad)))
    germ = jnp.zeros(index.shape, jnp.float32)
    for level, point in enumerate(hermite_points):
        germ = jnp.where(index == level, jnp.float32(point), germ)
    square = germ * germ
    h2 = (square - 1.0) / math.sqrt(2.0)
    h3 = (square * germ - 3.0 * germ) / math.sqrt(6.0)
    basis = None
    for i in range(germ.shape[0]):
        degree = mode_index[:, i][:, None]
        factor = jnp.where(
            degree == 0,
            1.0,
            jnp.where(degree == 1, germ[i][None], jnp.where(degree == 2, h2[i][None], h3[i][None])),
        )
        basis = factor if basis is None else basis * factor
    weighted = basis * jnp.pad(weights, (0, pad))[None]
    mass = lax.dot_general(
        storage_rate * weighted, basis, (((1,), (1,)), ((), ())), precision=HIGHEST
    )
    b_top, b_low = halves(basis.T)
    basis_cat = jnp.concatenate([b_top, b_top, b_low], axis=1)
    weight_cat = jnp.concatenate(halves(2.0 * weighted), axis=0)
    germ_full = jnp.concatenate([jnp.ones((1, q + pad), jnp.float32), germ], axis=0)
    g_top, g_low = halves(germ_full)
    germ_cat = jnp.concatenate([g_top, g_top, g_low], axis=0)
    germ_cat = jnp.pad(germ_cat, ((0, 32 - germ_cat.shape[0]), (0, 0))).T
    return basis_cat, weight_cat, germ_cat, mass


def log_cat(logs):
    top, low = halves(logs * jnp.float32(-math.log2(math.e)))
    cat = jnp.concatenate([top, low, top], axis=0)
    return jnp.pad(cat, ((0, 32 - cat.shape[0]), (0, 0)))


def put_cat(du_ref, lanes, diff):
    p = diff.shape[0]
    top, low = split(diff)
    du_ref[0:p, lanes] = top
    du_ref[p : 2 * p, lanes] = low
    du_ref[2 * p : 3 * p, lanes] = top


def add_flux(f_ref, lanes, w_ref, flux):
    p = f_ref.shape[0]
    top, low = split(flux)
    both = jnp.dot(w_ref[...], top, preferred_element_type=jnp.float32)
    rest = jnp.dot(w_ref[0:p, :], low, preferred_element_type=jnp.float32)
    f_ref[:, lanes] += both[0:p] + both[p : 2 * p] + rest


def inner_kernel(rows, u_ref, log_ref, basis_ref, germ_ref, w_ref, mass_ref, g_ref, du_ref, r_ref, f_ref):
    p = mass_ref.shape[0]
    cols = LANES
    step = pl.program_id(0)

    @pl.when(step == 0)
    def _():
        lane = lax.broadcasted_iota(jnp.int32, (p, cols), 1)
        above = None
        for y in range(rows):
            here = u_ref[pl.ds(y, p, stride=rows), :]
            ahead = pltpu.roll(here, cols - 1, axis=1)
            put_cat(du_ref, pl.ds(y * cols, cols), jnp.where(lane == cols - 1, 0.0, ahead - here))
            if y > 0:
                put_cat(du_ref, pl.ds((rows + y - 1) * cols, cols), here - above)
            above = here
        f_ref[...] = jnp.zeros_like(f_ref)

    r_ref[...] = jnp.exp2(
        jnp.dot(germ_ref[...], log_ref[...], preferred_element_type=jnp.float32)
    )

    def values(lanes):
        return jnp.dot(basis_ref[...], du_ref[:, lanes], preferred_element_type=jnp.float32)

    for y in range(0, rows, 2):
        lanes = pl.ds(y * cols, 2 * cols)
        sums = []
        for k in range(2):
            r = r_ref[:, pl.ds((y + k) * cols, cols)]
            sums.append(r + pltpu.roll(r, cols - 1, axis=1))
        add_flux(f_ref, lanes, w_ref, values(lanes) / jnp.concatenate(sums, axis=1))
    for y in range(0, rows - 1, 2):
        n = min(2, rows - 1 - y)
        lanes = pl.ds((rows + y) * cols, n * cols)
        total = r_ref[:, pl.ds(y * cols, n * cols)] + r_ref[:, pl.ds((y + 1) * cols, n * cols)]
        add_flux(f_ref, lanes, w_ref, values(lanes) / total)

    @pl.when(step == pl.num_programs(0) - 1)
    def _():
        lane = lax.broadcasted_iota(jnp.int32, (p, cols), 1)
        for y in range(rows):
            out = jnp.dot(
                mass_ref[...],
                u_ref[pl.ds(y, p, stride=rows), :],
                precision=HIGHEST,
                preferred_element_type=jnp.float32,
            )
            later = f_ref[:, pl.ds(y * cols, cols)]
            earlier = jnp.where(lane == 0, 0.0, pltpu.roll(later, 1, axis=1))
            later = jnp.where(lane == cols - 1, 0.0, later)
            out = out - (later - earlier)
            if y < rows - 1:
                out = out - f_ref[:, pl.ds((rows + y) * cols, cols)]
            if y > 0:
                out = out + f_ref[:, pl.ds((rows + y - 1) * cols, cols)]
            g_ref[y] = out


def whole(shape):
    return pl.BlockSpec(shape, lambda *_: (0,) * len(shape))


def inner_fluxes(field, logs, basis_cat, weight_cat, germ_cat, mass):
    p, rows, cols = field.shape
    q = basis_cat.shape[0]
    faces = (2 * rows - 1) * cols
    return pl.pallas_call(
        functools.partial(inner_kernel, rows),
        grid=(q // QB,),
        in_specs=[
            whole((p * rows, cols)),
            whole(logs.shape),
            pl.BlockSpec((QB, basis_cat.shape[1]), lambda i: (i, 0)),
            pl.BlockSpec((QB, germ_cat.shape[1]), lambda i: (i, 0)),
            pl.BlockSpec((2 * p, QB), lambda i: (0, i)),
            whole((p, p)),
        ],
        out_specs=whole((rows, p, cols)),
        out_shape=jax.ShapeDtypeStruct((rows, p, cols), jnp.float32),
        scratch_shapes=[
            pltpu.VMEM((3 * p, faces), jnp.bfloat16),
            pltpu.VMEM((QB, rows * cols), jnp.float32),
            pltpu.VMEM((p, faces), jnp.float32),
        ],
        compiler_params=pltpu.CompilerParams(vmem_limit_bytes=40 << 20),
        cost_estimate=pl.CostEstimate(
            flops=2 * q * faces * p * 6, bytes_accessed=8 << 20, transcendentals=q * rows * cols
        ),
        name="inner_fluxes",
    )(field.reshape(p * rows, cols), logs, basis_cat, germ_cat, weight_cat, mass)


def rim_kernel(
    rows, open_ref, g_ref, u_ref, up_ref, down_ref, side_ref, le_ref, ll_ref, basis_ref, germ_ref,
    w_ref, out_ref, du_ref, f_ref,
):
    p = up_ref.shape[0]
    cols = LANES
    step = pl.program_id(0)

    @pl.when(step == 0)
    def _():
        lane = lax.broadcasted_iota(jnp.int32, (p, cols), 1)
        first = u_ref[pl.ds(0, p, stride=rows), :]
        last = u_ref[pl.ds(rows - 1, p, stride=rows), :]
        put_cat(du_ref, pl.ds(0, cols), (first - up_ref[...]) * open_ref[0])
        put_cat(du_ref, pl.ds(cols, cols), (down_ref[...] - last) * open_ref[1])
        near = jnp.zeros((p, cols), jnp.float32)
        for y in range(rows):
            here = u_ref[pl.ds(y, p, stride=rows), :]
            near = jnp.where(lane == y, here[:, 0:1], near)
            near = jnp.where(lane == rows + y, here[:, cols - 1 : cols], near)
        side = side_ref[...]
        diff = jnp.where(lane < rows, (near - side) * open_ref[2], (side - near) * open_ref[3])
        put_cat(du_ref, pl.ds(2 * cols, cols), jnp.where(lane < 2 * rows, diff, 0.0))
        f_ref[...] = jnp.zeros_like(f_ref)

    earlier = jnp.exp2(jnp.dot(germ_ref[...], le_ref[...], preferred_element_type=jnp.float32))
    later = jnp.exp2(jnp.dot(germ_ref[...], ll_ref[...], preferred_element_type=jnp.float32))
    values = jnp.dot(basis_ref[...], du_ref[...], preferred_element_type=jnp.float32)
    add_flux(f_ref, pl.ds(0, 3 * cols), w_ref, values / (earlier + later))

    @pl.when(step == pl.num_programs(0) - 1)
    def _():
        lane = lax.broadcasted_iota(jnp.int32, (p, cols), 1)
        side = f_ref[:, pl.ds(2 * cols, cols)]
        for y in range(rows):
            out = g_ref[y]
            if y == 0:
                out = out + f_ref[:, pl.ds(0, cols)]
            if y == rows - 1:
                out = out - f_ref[:, pl.ds(cols, cols)]
            out = out + jnp.where(lane == 0, side[:, y : y + 1], 0.0)
            out = out - jnp.where(lane == cols - 1, side[:, rows + y : rows + y + 1], 0.0)
            out_ref[pl.ds(y, p, stride=rows), :] = out


def rim_fluxes(opened, inner, field, up, down, side, log_e, log_l, basis_cat, weight_cat, germ_cat):
    p, rows, cols = field.shape
    q = basis_cat.shape[0]
    return pl.pallas_call(
        functools.partial(rim_kernel, rows),
        grid=(q // QB,),
        in_specs=[
            pl.BlockSpec(memory_space=pltpu.SMEM),
            whole(inner.shape),
            whole((p * rows, cols)),
            whole((p, cols)),
            whole((p, cols)),
            whole((p, cols)),
            whole(log_e.shape),
            whole(log_l.shape),
            pl.BlockSpec((QB, basis_cat.shape[1]), lambda i: (i, 0)),
            pl.BlockSpec((QB, germ_cat.shape[1]), lambda i: (i, 0)),
            pl.BlockSpec((2 * p, QB), lambda i: (0, i)),
        ],
        out_specs=whole((p * rows, cols)),
        out_shape=jax.ShapeDtypeStruct((p * rows, cols), jnp.float32),
        scratch_shapes=[
            pltpu.VMEM((3 * p, 3 * cols), jnp.bfloat16),
            pltpu.VMEM((p, 3 * cols), jnp.float32),
        ],
        compiler_params=pltpu.CompilerParams(vmem_limit_bytes=40 << 20),
        cost_estimate=pl.CostEstimate(
            flops=2 * q * 3 * cols * p * 6, bytes_accessed=8 << 20, transcendentals=q * 6 * cols
        ),
        name="rim_fluxes",
    )(opened, inner, field.reshape(p * rows, cols), up, down, side, log_e, log_l, basis_cat, germ_cat, weight_cat)


def local_kernel(nsa, part_ref, src_ref, cy_ref, cx_ref, cxt_ref, ends_of_ref, recip_ref, z_ref, ends_ref):
    ngy, modes, length, cols = src_ref.shape
    rows = part_ref.shape[2]
    ends_ref[...] = jnp.zeros_like(ends_ref)
    for m in range(modes):
        tiles = []
        for g in range(ngy):
            for s in range(nsa):
                tiles.append(src_ref[g, m, s * rows : (s + 1) * rows, :] - part_ref[s * ngy + g, m])
        residual = jnp.concatenate(tiles, axis=0)
        spectral = jnp.dot(cy_ref[...], residual, precision=HIGHEST, preferred_element_type=jnp.float32)
        scaled = recip_ref[...] * jnp.dot(
            spectral, cxt_ref[...], precision=HIGHEST, preferred_element_type=jnp.float32
        )
        z_ref[m] = jnp.dot(scaled, cx_ref[...], precision=HIGHEST, preferred_element_type=jnp.float32)
        both = lax.dot_general(
            ends_of_ref[...], scaled, (((1,), (1,)), ((), ())),
            precision=HIGHEST, preferred_element_type=jnp.float32,
        )
        ends_ref[m : m + 1, :] = both[0:1]
        ends_ref[8 + m : 9 + m, :] = both[1:2]


def joined_kernel(z_ref, ends_ref, coef_ref, g_first_ref, g_last_ref, cyt_ref, out_ref):
    modes, ny, cols = z_ref.shape
    blocks = ends_ref.shape[0]
    ngy = out_ref.shape[0]
    length = ny // ngy
    jump = []
    for side in range(2):
        total = jnp.zeros((8, ny), jnp.float32)
        for i in range(blocks):
            total = total + coef_ref[side, 0, i : i + 1, :] * ends_ref[i, 0:8, :]
            total = total + coef_ref[side, 1, i : i + 1, :] * ends_ref[i, 8:16, :]
        jump.append(total)
    both = jnp.concatenate(jump + [jnp.zeros((LANES - 16, ny), jnp.float32)], axis=0).T
    for m in range(modes):
        x = (
            z_ref[m]
            + g_first_ref[...] * both[:, m : m + 1]
            - g_last_ref[...] * both[:, 8 + m : 9 + m]
        )
        out = jnp.dot(cyt_ref[...], x, precision=HIGHEST, preferred_element_type=jnp.float32)
        for g in range(ngy):
            out_ref[g, m] = out[g * length : (g + 1) * length]


def solve_tables(mean_perm, ny, cols, blocks, position):
    cx = cosine_matrix(cols)
    lam_y = jnp.asarray(eigen_values(ny, ny), jnp.float32)
    lam_x = jnp.asarray(eigen_values(cols, cols), jnp.float32)
    recip = 1.0 / (storage_rate + mean_perm * (lam_y[:, None] + lam_x[None, :]))
    first = jnp.asarray(cx[:, 0][:, None] * cx, jnp.float32)
    last = jnp.asarray(cx[:, -1][:, None] * cx, jnp.float32)
    g_first = jnp.dot(recip, first, precision=HIGHEST)
    g_last = jnp.dot(recip, last, precision=HIGHEST)
    k = np.arange(1, blocks)
    sine = math.sqrt(2.0 / blocks) * np.sin(np.pi * np.outer(np.arange(0, blocks + 1), k) / blocks)
    sine[0] = 0.0
    sine[blocks] = 0.0
    theta = jnp.asarray(2.0 * np.cos(np.pi * k / blocks), jnp.float32)
    spread = 1.0 / (
        1.0 / mean_perm + g_first[:, 0:1] + g_last[:, cols - 1 : cols] - g_first[:, cols - 1 : cols] * theta
    )
    table = jnp.asarray(sine, jnp.float32)
    coef = []
    for side in range(2):
        mine = lax.dynamic_slice_in_dim(table, position + side, 1, axis=0)
        inverse = jnp.einsum("ik,jk->ij", table, spread * mine, precision=HIGHEST)
        coef.append(jnp.stack([-inverse[:blocks], inverse[1:]]))
    return recip, g_first, g_last, jnp.stack(coef)


def shifted(last, leading, axis):
    count = lax.axis_size(axis)
    up = [(i, i + 1) for i in range(count - 1)]
    return lax.ppermute(last, axis, up), lax.ppermute(leading, axis, [(b, a) for a, b in up])


def on_device(
    field_now, field_before, source, log_fields, weights, mean_perm, node_index, mode_index
):
    nsa, ngy, ngx = (lax.axis_size(a) for a in ("sa", "gy", "gx"))
    modes, length, cols = field_now.shape
    rows = length // nsa
    p = modes * nsa
    ny = length * ngy
    sub = modes // ngy

    outgoing = field_now.reshape(modes, nsa, rows, cols).transpose(1, 0, 2, 3)
    field = lax.all_to_all(outgoing, "sa", 0, 0, tiled=True).reshape(p, rows, cols)
    src = lax.all_to_all(source.reshape(ngy, sub, length, cols), "gy", 0, 0, tiled=True)

    basis_cat, weight_cat, germ_cat, mass = node_tables(node_index, mode_index, weights)
    recip, g_first, g_last, coef = solve_tables(mean_perm, ny, cols, ngx, lax.axis_index("gx"))

    row_axis = ("gy", "sa")
    row_index = lax.axis_index(row_axis)
    col_index = lax.axis_index("gx")
    opened = jnp.stack(
        [row_index > 0, row_index < ngy * nsa - 1, col_index > 0, col_index < ngx - 1]
    ).astype(jnp.float32)
    log_up, log_down = shifted(log_fields[:, -1], log_fields[:, 0], row_axis)
    log_left, log_right = shifted(log_fields[:, :, -1], log_fields[:, :, 0], "gx")
    spare = jnp.zeros((log_fields.shape[0], LANES - 2 * rows), jnp.float32)
    log_e = log_cat(
        jnp.concatenate([log_up, log_fields[:, -1], log_left, log_fields[:, :, -1], spare], axis=1)
    )
    log_l = log_cat(
        jnp.concatenate([log_fields[:, 0], log_down, log_fields[:, :, 0], log_right, spare], axis=1)
    )
    logs = log_cat(log_fields.reshape(log_fields.shape[0], rows * cols))

    up, down = shifted(field[:, -1], field[:, 0], row_axis)
    left, right = shifted(field[:, :, -1], field[:, :, 0], "gx")
    side = jnp.concatenate([left, right, jnp.zeros((p, LANES - 2 * rows), jnp.float32)], axis=1)

    inner = inner_fluxes(field, logs, basis_cat, weight_cat, germ_cat, mass)
    galerkin = rim_fluxes(
        opened, inner, field, up, down, side, log_e, log_l, basis_cat, weight_cat, germ_cat
    )
    part = lax.all_to_all(
        galerkin.reshape(nsa * ngy, sub, rows, cols), ("sa", "gy"), 0, 0, tiled=True
    )

    cy = cosine_matrix(ny)
    cx = cosine_matrix(cols)
    ends_of = np.zeros((8, cols))
    ends_of[0], ends_of[1] = cx[:, 0], cx[:, -1]
    f32 = functools.partial(jnp.asarray, dtype=jnp.float32)
    params = pltpu.CompilerParams(vmem_limit_bytes=40 << 20)
    z, ends = pl.pallas_call(
        functools.partial(local_kernel, nsa),
        out_shape=(
            jax.ShapeDtypeStruct((sub, ny, cols), jnp.float32),
            jax.ShapeDtypeStruct((16, ny), jnp.float32),
        ),
        compiler_params=params,
        name="local_solve",
    )(part, src, f32(cy), f32(cx), f32(cx.T), f32(ends_of), recip)
    all_ends = lax.all_gather(ends, "gx", axis=0, tiled=False)
    columns = pl.pallas_call(
        joined_kernel,
        out_shape=jax.ShapeDtypeStruct((ngy, sub, length, cols), jnp.float32),
        compiler_params=params,
        name="joined_solve",
    )(z, all_ends, coef, g_first, g_last, f32(cy.T))
    update = lax.all_to_all(columns, "gy", 0, 0, tiled=True).reshape(modes, length, cols)
    fresh = field_before + relax_weight * (field_now - field_before + step_length * update)
    return (fresh, update)


def solution(mesh):
    block = P("sa", "gy", "gx")
    in_specs = (block, block, block, P(None, ("gy", "sa"), "gx"), P(), P(), P(), P())
    return jax.shard_map(
        on_device, mesh=mesh, in_specs=in_specs, out_specs=(block, block), check_vma=False
    )
```

profile of v0, /device:TPU:32, one launch (start us, length us, event | category | flops | bytes accessed | tf_op | source)
XLA Modules:
  0.0 185.7 jit_solution(15498030612103064638)
XLA Ops:
  0.7 2.0 %copy.78 = f32[8,20,8,128]{3,2,1,0:T(8,128)} copy(f32[8,20,8,128]{3,2,0,1:T(8,128)} %bitcast.64) | data formatting | bytes 1310720 | tf_op jit(solution)/shard_map/transpose | solution.py:366
  2.7 10.2 %all-to-all-start = ((f32[8,20,8,128]{3,2,1,0:T(8,128)}), f32[8,20,8,128]{3,2,1,0:T(8,128)S(1)}, u32[]{:S(2)}, u32[]{:S(2)}) async-start(f32[8,20,8,128]{3,2,1,0:T(8,128)} %copy.78), calls=%async_computation | async-start | bytes 1310720 | tf_op jit(solution)/shard_map/all_to_all | solution.py:367
  12.9 0.1 fusion.56
  12.9 0.8 copy.99
  13.7 2.1 %collective-permute-start.7 = (f32[9,8]{1,0:T(8,128)}, f32[9,8]{1,0:T(8,128)}, u32[]{:S(2)}, u32[]{:S(2)}) collective-permute-start(f32[9,8]{1,0:T(8,128)} %bitcast.34), channel_id=1, source_target_pairs={{32,0},{64,32},{96,64},{128,96},{160,128},{192,160},{224,192},{33,... | collective-permute-start | bytes 872 | tf_op jit(solution)/shard_map/ppermute | solution.py:353
  15.8 1.3 collective-permute-start.6
  17.1 0.8 copy.98
  17.9 2.2 %collective-permute-start.5 = (f32[9,8]{1,0:T(8,128)}, f32[9,8]{1,0:T(8,128)}, u32[]{:S(2)}, u32[]{:S(2)}) collective-permute-start(f32[9,8]{1,0:T(8,128)} %bitcast.33), channel_id=1, source_target_pairs={{0,32},{32,64},{64,96},{96,128},{128,160},{160,192},{192,224},{1,3... | collective-permute-start | bytes 872 | tf_op jit(solution)/shard_map/ppermute | solution.py:353
  20.1 0.6 copy.104
  20.7 5.1 %collective-permute-start.4 = (f32[9,128]{1,0:T(8,128)}, f32[9,128]{1,0:T(8,128)}, u32[]{:S(2)}, u32[]{:S(2)}) collective-permute-start(f32[9,128]{1,0:T(8,128)} %bitcast.56), channel_id=1, source_target_pairs={{0,1},{1,2},{2,3},{3,4},{4,5},{5,6},{6,7},{7,8},{8,9},{9,10},{10,1... | collective-permute-start | bytes 13832 | tf_op jit(solution)/shard_map/ppermute | solution.py:353
  25.9 0.1 slice_reduce_fusion.23
  26.1 0.1 compare_reduce_fusion.20
  26.2 0.3 slice_reduce_fusion.21
  26.5 5.9 %reduce-precision_convert_fusion = (bf16[1536,160]{1,0:T(8,128)(2,1)}, f32[1536,160]{1,0:T(8,128)S(1)}) fusion(f32[1536]{0:T(1024)S(1)} %get-tuple-element.23, f32[1536]{0:T(1024)S(1)} %get-tuple-element.110, pred[160]{0:T(512)(128)(4,1)S(1)} %get-tuple-element.87, f32[1536]{0:T(1024)S(1)} %get-tuple-element.13, pred[160]{0:T(512)(128)(4,1)S(1)} %get-tuple-element.88, ...), kind=kLoop, calls=%fused_computation.1 | loop fusion | flops 8110080 | bytes 1625856 | tf_op jit(solution)/shard_map/convert_element_type | solution.py:31
  32.4 5.7 %reduce-precision_convert_fusion.1 = (bf16[160,1536]{1,0:T(8,128)(2,1)S(1)}, f32[160,1536]{1,0:T(8,128)S(1)}) fusion(f32[1536]{0:T(1024)S(1)} %pad.27, f32[1536]{0:T(1024)S(1)} %get-tuple-element.23, f32[1536]{0:T(1024)S(1)} %get-tuple-element.110, pred[160]{0:T(512)(128)(4,1)S(1)} %get-tuple-element.87, f32[1536]{0:T(1024)S(1)} %get-tuple-element.13, ...), kind=kLoop, calls=%fused_computation.6 | loop fusion | flops 8601600 | bytes 1632000 | tf_op jit(solution)/shard_map/convert_element_type | solution.py:31
  38.1 0.9 copy-done.10
  39.0 0.2 fusion.1
  39.2 0.0 copy-start.18
  39.2 0.0 copy-start.20
  39.2 1.1 fusion
  40.4 0.2 copy.79
  40.6 0.8 pad_bitcast_fusion.germ_ref
  42.2 0.4 fusion.14
  42.6 0.4 fusion.15
  43.0 0.1 pad_maximum_fusion.1.w_ref
  43.1 2.5 %pad_maximum_fusion.basis_ref = bf16[1536,480]{1,0:T(8,128)(2,1)S(1)} fusion(bf16[1536,160]{1,0:T(8,128)(2,1)} %fusion, bf16[1536,160]{1,0:T(8,128)(2,1)} %get-tuple-element.56), kind=kLoop, calls=%fused_computation.3 | loop fusion | flops 4423680 | bytes 2457600 | tf_op jit(solution)/shard_map/concatenate | solution.py:75
  45.7 0.7 fusion.13.log_ref
  46.3 1.3 dynamic-slice_bitcast_fusion.1
  47.6 3.2 %fusion.2.mass_ref = f32[160,160]{1,0:T(8,128)} fusion(f32[160,1536]{1,0:T(8,128)} %copy-done.10, f32[1536]{0:T(1024)S(1)} %pad.27), kind=kOutput, calls=%fused_computation.9 | convolution fusion | flops 472350720 | bytes 1091584 | tf_op jit(solution)/shard_map/dot_general | solution.py:71
  50.8 0.1 add_convert_fusion.open_ref
  50.9 0.1 copy.90.g_first_ref
  51.0 1.0 copy.91.g_last_ref
  52.0 0.1 pad.44.clone
  52.1 0.8 concatenate.38
  52.9 0.8 concatenate.36
  53.8 9.5 %all-to-all-start.2 = ((f32[4,5,64,128]{3,2,1,0:T(8,128)}), f32[4,5,64,128]{3,2,1,0:T(8,128)}, u32[]{:S(2)}, u32[]{:S(2)}) async-start(f32[4,5,64,128]{3,2,1,0:T(8,128)} %bitcast.65), calls=%async_computation.2 | async-start | bytes 1310720 | tf_op jit(solution)/shard_map/all_to_all | solution.py:368
  63.3 1.2 fusion.54
  64.5 0.8 fusion.55
  65.3 2.7 %copy.92 = f32[160,8,1]{1,0,2:T(8,128)} copy(f32[160,8,1]{2,1,0:T(8,128)} %get-tuple-element.58) | data formatting | bytes 10240
  68.0 2.5 %collective-permute-start.2 = (f32[160,8]{1,0:T(8,128)}, f32[160,8]{1,0:T(8,128)}, u32[]{:S(2)}, u32[]{:S(2)}) collective-permute-start(f32[160,8]{1,0:T(8,128)} %bitcast.70), channel_id=1, source_target_pairs={{0,32},{32,64},{64,96},{96,128},{128,160},{160,192},{192,224},{1,3... | collective-permute-start | bytes 15368 | tf_op jit(solution)/shard_map/ppermute | solution.py:353
  70.5 2.7 %copy.93 = f32[160,8,1]{1,0,2:T(8,128)} copy(f32[160,8,1]{2,1,0:T(8,128)} %get-tuple-element.59) | data formatting | bytes 10240
  73.3 3.0 %collective-permute-start.3 = (f32[160,8]{1,0:T(8,128)}, f32[160,8]{1,0:T(8,128)S(1)}, u32[]{:S(2)}, u32[]{:S(2)}) collective-permute-start(f32[160,8]{1,0:T(8,128)} %bitcast.71), channel_id=1, source_target_pairs={{32,0},{64,32},{96,64},{128,96},{160,128},{192,160},{224,192},{33,... | collective-permute-start | bytes 15368 | tf_op jit(solution)/shard_map/ppermute | solution.py:353
  76.3 1.3 collective-permute-start
  77.6 1.3 collective-permute-start.1
  78.9 1.0 copy-done.1
  79.9 0.9 copy-done.5
  80.8 0.8 copy-done.8
  81.6 21.2 %inner_fluxes.1.g_ref = f32[8,160,128]{2,1,0:T(8,128)S(1)} custom-call(f32[1280,128]{1,0:T(8,128)S(1)} %bitcast.59, bf16[32,1024]{1,0:T(8,128)(2,1)S(1)} %copy-done.8, bf16[1536,480]{1,0:T(8,128)(2,1)S(1)} %pad_maximum_fusion.basis_ref, bf16[1536,32]{1,0:T(8,128)(2,1)S(1)} %copy-done.1, bf16[320,1536]{1,0:T(8,128)(2,1)S(1)} %pad_maximum_fusion.1.w_ref, ...), custom_call_target="tpu_custom_call" | custom-call | flops 5662310400 | bytes 8388608 | tf_op jit(solution)/shard_map/inner_fluxes/pallas_call | solution.py:173
  102.9 1.0 maximum_maximum_fusion.side_ref
  103.9 0.0 copy-start.24
  103.9 0.0 copy-start.27
  104.0 5.5 %rim_fluxes.1 = f32[1280,128]{1,0:T(8,128)S(1)} custom-call(f32[4]{0:T(128)S(1)} %add_convert_fusion.open_ref, f32[8,160,128]{2,1,0:T(8,128)S(1)} %inner_fluxes.1.g_ref, f32[1280,128]{1,0:T(8,128)S(1)} %bitcast.60, f32[160,128]{1,0:T(8,128)S(1)} %collective-permute-done.up_ref, f32[160,128]{1,0:T(8,128)S(1)} %collective-permute-done.1.down_ref, ...), custom_call_target="tpu_custom_call" | custom-call | flops 1132462080 | bytes 8388608 | tf_op jit(solution)/shard_map/rim_fluxes/pallas_call | solution.py:247
  109.5 0.8 copy-done
  110.4 17.0 %all-to-all-start.1 = ((f32[32,5,8,128]{3,2,1,0:T(8,128)}), f32[32,5,8,128]{3,2,1,0:T(8,128)S(1)}, u32[]{:S(2)}, u32[]{:S(2)}) async-start(f32[32,5,8,128]{3,2,1,0:T(8,128)} %bitcast.61), calls=%async_computation.1 | async-start | bytes 1310720 | tf_op jit(solution)/shard_map/all_to_all | solution.py:398
  127.4 0.2 fusion.35
  127.6 0.2 fusion.33
  127.9 0.1 add_divide_fusion.recip_ref
  128.0 22.1 %all-to-all-done.1.part_ref = f32[32,5,8,128]{3,2,1,0:T(8,128)S(1)} async-done(((f32[32,5,8,128]{3,2,1,0:T(8,128)}), f32[32,5,8,128]{3,2,1,0:T(8,128)S(1)}, u32[]{:S(2)}, u32[]{:S(2)}) %all-to-all-start.1) | async-done | bytes 655392 | tf_op jit(solution)/shard_map/all_to_all | solution.py:398
  150.1 5.8 %local_solve.1 = (f32[5,256,128]{2,1,0:T(8,128)S(1)}, f32[16,256]{1,0:T(8,128)S(1)}) custom-call(f32[32,5,8,128]{3,2,1,0:T(8,128)S(1)} %all-to-all-done.1.part_ref, f32[4,5,64,128]{3,2,1,0:T(8,128)} %all-to-all-done.2.src_ref, f32[256,256]{1,0:T(8,128)S(1)} %copy-done.4, f32[128,128]{1,0:T(8,128)S(1)} %copy-done.6, f32[128,128]{1,0:T(8,128)S(1)} %copy-done.7, ...), custom_call_target="tpu_custom_call" | custom-call | tf_op jit(solution)/shard_map/local_solve/pallas_call | solution.py:408
  155.9 12.2 %all-gather = f32[128,256]{1,0:T(8,128)S(1)} all-gather(f32[16,256]{1,0:T(8,128)S(1)} %get-tuple-element.5), channel_id=2, replica_groups=mesh['gx'=8,'gy'=4,'sa'=8] {'gx'}, dimensions={0}, use_global_device_ids=true | all-gather | bytes 147456 | tf_op jit(solution)/shard_map/all_gather | solution.py:417
  168.1 1.4 joined_solve.1
  169.6 14.3 %all_to_all.20 = f32[4,5,64,128]{3,2,1,0:T(8,128)S(1)} all-to-all(f32[4,5,64,128]{3,2,1,0:T(8,128)S(1)} %joined_solve.1), channel_id=1, replica_groups=mesh['gx'=8,'gy'=4,'sa'=8] {'gy'}, dimensions={0} | all-to-all | bytes 1310720 | tf_op jit(solution)/shard_map/all_to_all | solution.py:424
  183.9 1.0 multiply_add_fusion
  184.9 0.8 copy.107
  (77 shorter events, 0.4 us)
Async XLA Ops:
  0.6 12.2 %copy-start.13 = (f32[9,8,128]{2,1,0:T(8,128)S(1)}, f32[9,8,128]{2,1,0:T(8,128)}, u32[]{:S(2)}) copy-start(f32[9,8,128]{2,1,0:T(8,128)} %param.22) | copy-start | bytes 110596
  0.6 25.2 %copy-start.15 = (s32[1500,8]{0,1:T(8,128)S(1)}, s32[1500,8]{0,1:T(8,128)}, u32[]{:S(2)}) copy-start(s32[1500,8]{0,1:T(8,128)} %param.25) | copy-start | bytes 144004
  0.7 25.4 %copy-start.16 = (s32[160,8]{0,1:T(8,128)S(1)}, s32[160,8]{0,1:T(8,128)}, u32[]{:S(2)}) copy-start(s32[160,8]{0,1:T(8,128)} %param.26) | copy-start | bytes 15364
  0.7 25.8 %copy-start.17 = (f32[1500]{0:T(1024)S(1)}, f32[1500]{0:T(1024)}, u32[]{:S(2)}) copy-start(f32[1500]{0:T(1024)} %param.23) | copy-start | bytes 18004
  2.7 51.1 %all-to-all-start = ((f32[8,20,8,128]{3,2,1,0:T(8,128)}), f32[8,20,8,128]{3,2,1,0:T(8,128)S(1)}, u32[]{:S(2)}, u32[]{:S(2)}) async-start(f32[8,20,8,128]{3,2,1,0:T(8,128)} %copy.78), calls=%async_computation | async-start | bytes 1310720 | tf_op jit(solution)/shard_map/all_to_all | solution.py:367
  13.7 38.4 %collective-permute-start.7 = (f32[9,8]{1,0:T(8,128)}, f32[9,8]{1,0:T(8,128)}, u32[]{:S(2)}, u32[]{:S(2)}) collective-permute-start(f32[9,8]{1,0:T(8,128)} %bitcast.34), channel_id=1, source_target_pairs={{32,0},{64,32},{96,64},{128,96},{160,128},{192,160},{224,192},{33,... | collective-permute-start | bytes 872 | tf_op jit(solution)/shard_map/ppermute | solution.py:353
  15.8 36.3 %collective-permute-start.6 = (f32[9,128]{1,0:T(8,128)S(1)}, f32[9,128]{1,0:T(8,128)}, u32[]{:S(2)}, u32[]{:S(2)}) collective-permute-start(f32[9,128]{1,0:T(8,128)S(1)} %bitcast.73), channel_id=1, source_target_pairs={{1,0},{2,1},{3,2},{4,3},{5,4},{6,5},{7,6},{8,7},{9,8},{10,9},{11,1... | collective-permute-start | bytes 13832 | tf_op jit(solution)/shard_map/ppermute | solution.py:353
  17.9 35.0 %collective-permute-start.5 = (f32[9,8]{1,0:T(8,128)}, f32[9,8]{1,0:T(8,128)}, u32[]{:S(2)}, u32[]{:S(2)}) collective-permute-start(f32[9,8]{1,0:T(8,128)} %bitcast.33), channel_id=1, source_target_pairs={{0,32},{32,64},{64,96},{96,128},{128,160},{160,192},{192,224},{1,3... | collective-permute-start | bytes 872 | tf_op jit(solution)/shard_map/ppermute | solution.py:353
  20.7 32.2 %collective-permute-start.4 = (f32[9,128]{1,0:T(8,128)}, f32[9,128]{1,0:T(8,128)}, u32[]{:S(2)}, u32[]{:S(2)}) collective-permute-start(f32[9,128]{1,0:T(8,128)} %bitcast.56), channel_id=1, source_target_pairs={{0,1},{1,2},{2,3},{3,4},{4,5},{5,6},{6,7},{7,8},{8,9},{9,10},{10,1... | collective-permute-start | bytes 13832 | tf_op jit(solution)/shard_map/ppermute | solution.py:353
  38.1 1.0 copy-start.10
  39.2 3.0 %copy-start.18 = (f32[256]{0:T(256)S(1)}, f32[256]{0:T(256)}, u32[]{:S(2)}) copy-start(f32[256]{0:T(256)} %constant.43.clone) | copy-start | bytes 3076
  39.2 3.0 %copy-start.20 = (f32[128]{0:T(128)S(1)}, f32[128]{0:T(128)}, u32[]{:S(2)}) copy-start(f32[128]{0:T(128)} %constant.112.clone) | copy-start | bytes 1540
  39.2 3.0 %copy-start.26 = (f32[128,128]{1,0:T(8,128)S(1)}, f32[128,128]{1,0:T(8,128)}, u32[]{:S(2)}) copy-start(f32[128,128]{1,0:T(8,128)} %constant.114.clone) | copy-start | bytes 196612
  40.3 2.2 %copy-start.25 = (f32[128,128]{1,0:T(8,128)S(1)}, f32[128,128]{1,0:T(8,128)}, u32[]{:S(2)}) copy-start(f32[128,128]{1,0:T(8,128)} %constant.113.clone) | copy-start | bytes 196612
  42.6 5.0 %copy-start.14 = (f32[256,128]{0,1:T(8,128)}, f32[256,128]{0,1:T(8,128)S(1)}, u32[]{:S(2)}) copy-start(f32[256,128]{0,1:T(8,128)S(1)} %fusion.14) | copy-start | bytes 393220
  53.8 56.6 %all-to-all-start.2 = ((f32[4,5,64,128]{3,2,1,0:T(8,128)}), f32[4,5,64,128]{3,2,1,0:T(8,128)}, u32[]{:S(2)}, u32[]{:S(2)}) async-start(f32[4,5,64,128]{3,2,1,0:T(8,128)} %bitcast.65), calls=%async_computation.2 | async-start | bytes 1310720 | tf_op jit(solution)/shard_map/all_to_all | solution.py:368
  68.0 34.9 %collective-permute-start.2 = (f32[160,8]{1,0:T(8,128)}, f32[160,8]{1,0:T(8,128)}, u32[]{:S(2)}, u32[]{:S(2)}) collective-permute-start(f32[160,8]{1,0:T(8,128)} %bitcast.70), channel_id=1, source_target_pairs={{0,32},{32,64},{64,96},{96,128},{128,160},{160,192},{192,224},{1,3... | collective-permute-start | bytes 15368 | tf_op jit(solution)/shard_map/ppermute | solution.py:353
  73.3 29.6 %collective-permute-start.3 = (f32[160,8]{1,0:T(8,128)}, f32[160,8]{1,0:T(8,128)S(1)}, u32[]{:S(2)}, u32[]{:S(2)}) collective-permute-start(f32[160,8]{1,0:T(8,128)} %bitcast.71), channel_id=1, source_target_pairs={{32,0},{64,32},{96,64},{128,96},{160,128},{192,160},{224,192},{33,... | collective-permute-start | bytes 15368 | tf_op jit(solution)/shard_map/ppermute | solution.py:353
  76.3 27.6 %collective-permute-start = (f32[160,128]{1,0:T(8,128)}, f32[160,128]{1,0:T(8,128)S(1)}, u32[]{:S(2)}, u32[]{:S(2)}) collective-permute-start(f32[160,128]{1,0:T(8,128)} %bitcast.69), channel_id=1, source_target_pairs={{0,1},{1,2},{2,3},{3,4},{4,5},{5,6},{6,7},{7,8},{8,9},{9,10},{10,1... | collective-permute-start | bytes 245768 | tf_op jit(solution)/shard_map/ppermute | solution.py:353
  77.6 26.3 %collective-permute-start.1 = (f32[160,128]{1,0:T(8,128)}, f32[160,128]{1,0:T(8,128)S(1)}, u32[]{:S(2)}, u32[]{:S(2)}) collective-permute-start(f32[160,128]{1,0:T(8,128)} %bitcast.68), channel_id=1, source_target_pairs={{1,0},{2,1},{3,2},{4,3},{5,4},{6,5},{7,6},{8,7},{9,8},{10,9},{11,1... | collective-permute-start | bytes 245768 | tf_op jit(solution)/shard_map/ppermute | solution.py:353
  78.9 1.0 copy-start.1
  79.9 0.9 copy-start.5
  80.8 0.8 copy-start.8
  81.6 22.3 %copy-start.2 = (bf16[1536,32]{1,0:T(8,128)(2,1)S(1)}, bf16[1536,32]{1,0:T(8,128)(2,1)}, u32[]{:S(2)}) copy-start(bf16[1536,32]{1,0:T(8,128)(2,1)} %pad_bitcast_fusion.germ_ref) | copy-start | bytes 294916
  103.9 23.4 %copy-start.23 = (f32[7]{0:T(128)S(1)}, f32[7]{0:T(128)}, u32[]{:S(2)}) copy-start(f32[7]{0:T(128)} %get-tuple-element.83) | copy-start | bytes 88
  103.9 23.4 %copy-start.24 = (f32[9,7]{1,0:T(8,128)S(1)}, f32[9,7]{1,0:T(8,128)}, u32[]{:S(2)}) copy-start(f32[9,7]{1,0:T(8,128)} %constant.116.clone) | copy-start | bytes 760
  103.9 23.4 %copy-start.27 = (f32[7]{0:T(128)S(1)}, f32[7]{0:T(128)}, u32[]{:S(2)}) copy-start(f32[7]{0:T(128)} %constant.115.clone) | copy-start | bytes 88
  104.0 23.7 %copy-start.22 = (f32[7]{0:T(128)S(1)}, f32[7]{0:T(128)}, u32[]{:S(2)}) copy-start(f32[7]{0:T(128)} %get-tuple-element.84) | copy-start | bytes 88
  109.5 0.8 copy-start
  110.3 17.5 %copy-start.19 = (f32[256]{0:T(256)S(1)}, f32[256]{0:T(256)}, u32[]{:S(2)}) copy-start(f32[256]{0:T(256)} %constant.43.clone) | copy-start | bytes 3076
  110.3 17.5 %copy-start.21 = (f32[128]{0:T(128)S(1)}, f32[128]{0:T(128)}, u32[]{:S(2)}) copy-start(f32[128]{0:T(128)} %constant.112.clone) | copy-start | bytes 1540
  110.3 39.8 %copy-start.4 = (f32[256,256]{1,0:T(8,128)S(1)}, f32[256,256]{1,0:T(8,128)}, u32[]{:S(2)}) copy-start(f32[256,256]{1,0:T(8,128)} %constant.117.clone.cy_ref) | copy-start | bytes 786436
  110.3 39.8 %copy-start.6 = (f32[128,128]{1,0:T(8,128)S(1)}, f32[128,128]{1,0:T(8,128)}, u32[]{:S(2)}) copy-start(f32[128,128]{1,0:T(8,128)} %constant.118.clone.cx_ref) | copy-start | bytes 196612
  110.4 39.8 %copy-start.7 = (f32[128,128]{1,0:T(8,128)S(1)}, f32[128,128]{1,0:T(8,128)}, u32[]{:S(2)}) copy-start(f32[128,128]{1,0:T(8,128)} %constant.119.clone.cxt_ref) | copy-start | bytes 196612
  110.4 39.8 %copy-start.9 = (f32[8,128]{1,0:T(8,128)S(1)}, f32[8,128]{1,0:T(8,128)}, u32[]{:S(2)}) copy-start(f32[8,128]{1,0:T(8,128)} %constant.120.clone.ends_of_ref) | copy-start | bytes 12292
  110.4 39.7 %all-to-all-start.1 = ((f32[32,5,8,128]{3,2,1,0:T(8,128)}), f32[32,5,8,128]{3,2,1,0:T(8,128)S(1)}, u32[]{:S(2)}, u32[]{:S(2)}) async-start(f32[32,5,8,128]{3,2,1,0:T(8,128)} %bitcast.61), calls=%async_computation.1 | async-start | bytes 1310720 | tf_op jit(solution)/shard_map/all_to_all | solution.py:398
  127.3 40.8 %copy-start.3 = (f32[256,256]{1,0:T(8,128)S(1)}, f32[256,256]{1,0:T(8,128)}, u32[]{:S(2)}) copy-start(f32[256,256]{1,0:T(8,128)} %constant.121.clone.cyt_ref) | copy-start | bytes 786436
  168.1 15.8 %copy-start.11 = (f32[20,64,128]{2,1,0:T(8,128)S(1)}, f32[20,64,128]{2,1,0:T(8,128)}, u32[]{:S(2)}) copy-start(f32[20,64,128]{2,1,0:T(8,128)} %param.19) | copy-start | bytes 1966084
  168.1 15.8 %copy-start.12 = (f32[20,64,128]{2,1,0:T(8,128)S(1)}, f32[20,64,128]{2,1,0:T(8,128)}, u32[]{:S(2)}) copy-start(f32[20,64,128]{2,1,0:T(8,128)} %param.20) | copy-start | bytes 1966084
where the time goes:
time: 189 us; the launch traced here: 186 us
  starting transfers between devices  55.5 us (29%)
  Pallas kernels  34 us (18%)
  blocking collectives  26.5 us (14%)
  local copies, waits for them, and re-layouts  22.7 us (12%)
  waiting for transfers between devices  22.1 us (12%)
  other arithmetic  18.6 us (10%)
  matrix products  4.33 us (2%)
  between operations  1.99 us (1%)
    all_to_all x1, waiting for transfers between devices, on_device(): lax.all_to_all(galerkin.reshape(nsa * ngy, sub, rows, cols), ('sa', 'gy')...  22.1 us
    pallas_call x1, Pallas kernels, inner_fluxes(): pl.pallas_call(functools.partial(inner_kernel, rows), grid=(q // QB,), in...  21.2 us
    all_to_all x1, starting transfers between devices, on_device(): lax.all_to_all(galerkin.reshape(nsa * ngy, sub, rows, cols), ('sa', 'gy')...  17 us
    all_to_all x1, blocking collectives, on_device(): lax.all_to_all(columns, 'gy', 0, 0, tiled=True).reshape(modes, length, cols)  14.3 us
    convert_element_type x8, other arithmetic, halves(): return (top.astype(jnp.bfloat16), (x - top).astype(jnp.bfloat16))  12.9 us
    all_gather x1, blocking collectives, on_device(): all_ends = lax.all_gather(ends, 'gx', axis=0, tiled=False)  12.2 us
    unnamed x63, local copies, waits for them, and re-layouts  11.5 us
    ppermute x4, starting transfers between devices, shifted(): lax.ppermute(last, axis, up)  11.2 us
  transfers between devices with their start and end apart: 11, of which 1 were waited for; matrix products, arithmetic and copies ran while one was open for 20% of the time, Pallas kernels for 14%

commit v1 on v0

v1 whole, which is shorter than its diff:
```python
import functools
import math

import jax
import jax.numpy as jnp
import numpy as np
from jax import lax
from jax.experimental import pallas as pl
from jax.experimental.pallas import tpu as pltpu
from jax.sharding import PartitionSpec as P

HIGHEST = lax.Precision.HIGHEST
hermite_points = (
    0.0,
    -1.7320508075688772,
    1.7320508075688772,
    -1.355626179974266,
    1.355626179974266,
    -2.8569700138728056,
    2.8569700138728056,
)
storage_rate = 0.0004
relax_weight = 1.6
step_length = 0.3
QB = 256
LANES = 128


def halves(x):
    top = lax.reduce_precision(x, 8, 7)
    return top.astype(jnp.bfloat16), (x - top).astype(jnp.bfloat16)


def split(x):
    top = x.astype(jnp.bfloat16)
    return top, (x - top.astype(jnp.float32)).astype(jnp.bfloat16)


def cosine_matrix(length):
    k = np.arange(length)[:, None]
    m = np.arange(length)[None, :]
    phase = (k * (2 * m + 1)) % (4 * length)
    factor = np.where(k == 0, math.sqrt(1.0 / length), math.sqrt(2.0 / length))
    return factor * np.cos(phase * (math.pi / (2 * length)))


def eigen_values(count, length):
    return 4.0 * np.sin(np.arange(count) * (math.pi / (2 * length))) ** 2


SLOT = 16


def tables_kernel(index_ref, mode_ref, weight_ref, basis_ref, w_ref, germ_ref, mass_ref, sum_ref):
    germs, q = index_ref.shape
    p = mode_ref.shape[0]
    step = pl.program_id(0)
    index = index_ref[...]
    germ = jnp.zeros((germs, q), jnp.float32)
    for level, point in enumerate(hermite_points):
        germ = jnp.where(index == level, jnp.float32(point), germ)
    square = germ * germ
    h2 = (square - 1.0) / math.sqrt(2.0)
    h3 = (square * germ - 3.0 * germ) / math.sqrt(6.0)
    basis = jnp.ones((p, q), jnp.float32)
    for i in range(germs):
        degree = mode_ref[:, i : i + 1]
        factor = jnp.where(
            degree == 1,
            germ[i : i + 1],
            jnp.where(degree == 2, h2[i : i + 1], jnp.where(degree == 3, h3[i : i + 1], 1.0)),
        )
        basis = basis * factor
    weighted = basis * weight_ref[...]
    w_ref[0:p, :], w_ref[p : 2 * p, :] = split(2.0 * weighted)
    top, low = split(basis.T)
    basis_ref[:, 0:p] = top
    basis_ref[:, p : 2 * p] = top
    basis_ref[:, 2 * p : 3 * p] = low
    full = jnp.concatenate(
        [jnp.ones((8, q), jnp.float32), germ, jnp.zeros((LANES - 16, q), jnp.float32)], axis=0
    )
    top, low = split(full.T[:, 7 : 7 + SLOT])
    lane = lax.broadcasted_iota(jnp.int32, (q, SLOT), 1)
    keep = lane < germs + 1
    top = jnp.where(keep, top.astype(jnp.float32), 0.0).astype(jnp.bfloat16)
    low = jnp.where(keep, low.astype(jnp.float32), 0.0).astype(jnp.bfloat16)
    germ_ref[:, 0:SLOT] = top
    germ_ref[:, SLOT : 2 * SLOT] = top
    germ_ref[:, 2 * SLOT : 3 * SLOT] = low

    @pl.when(step == 0)
    def _():
        sum_ref[...] = jnp.zeros_like(sum_ref)

    sum_ref[...] += lax.dot_general(
        storage_rate * weighted, basis, (((1,), (1,)), ((), ())),
        precision=HIGHEST, preferred_element_type=jnp.float32,
    )

    @pl.when(step == pl.num_programs(0) - 1)
    def _():
        top, low = split(sum_ref[...])
        mass_ref[:, 0:p] = top
        mass_ref[:, p : 2 * p] = top
        mass_ref[:, 2 * p : 3 * p] = low


def node_tables(node_index, mode_index, weights):
    q, germs = node_index.shape
    p = mode_index.shape[0]
    pad = -q % QB
    index = jnp.pad(node_index.T, ((0, 0), (0, pad)))
    weights = jnp.pad(weights, (0, pad))[None]
    return pl.pallas_call(
        tables_kernel,
        grid=((q + pad) // QB,),
        in_specs=[
            pl.BlockSpec((germs, QB), lambda i: (0, i)),
            whole((p, germs)),
            pl.BlockSpec((1, QB), lambda i: (0, i)),
        ],
        out_specs=[
            pl.BlockSpec((QB, 3 * p), lambda i: (i, 0)),
            pl.BlockSpec((2 * p, QB), lambda i: (0, i)),
            pl.BlockSpec((QB, 3 * SLOT), lambda i: (i, 0)),
            whole((p, 3 * p)),
        ],
        out_shape=[
            jax.ShapeDtypeStruct((q + pad, 3 * p), jnp.bfloat16),
            jax.ShapeDtypeStruct((2 * p, q + pad), jnp.bfloat16),
            jax.ShapeDtypeStruct((q + pad, 3 * SLOT), jnp.bfloat16),
            jax.ShapeDtypeStruct((p, 3 * p), jnp.bfloat16),
        ],
        scratch_shapes=[pltpu.VMEM((p, p), jnp.float32)],
        compiler_params=pltpu.CompilerParams(vmem_limit_bytes=20 << 20),
        name="node_tables",
    )(index, mode_index, weights)


def whole(shape):
    return pl.BlockSpec(shape, lambda *_: (0,) * len(shape))


def rim_kernel(rows, u_ref, log_ref, first_ref, last_ref, near_ref):
    start = 0
    for ref in (u_ref, log_ref):
        n = ref.shape[0] // rows
        span = slice(start, start + n)
        lane = lax.broadcasted_iota(jnp.int32, (n, LANES), 1)
        near = jnp.zeros((n, LANES), jnp.float32)
        for y in range(rows):
            here = ref[pl.ds(y, n, stride=rows), :]
            if y == 0:
                first_ref[span] = here
            if y == rows - 1:
                last_ref[span] = here
            near = jnp.where(lane == y, here[:, 0:1], near)
            near = jnp.where(lane == rows + y, here[:, LANES - 1 : LANES], near)
        near_ref[span] = near
        start += n


def rim_of(rows, field, logs):
    n = (field.shape[0] + logs.shape[0]) // rows
    return pl.pallas_call(
        functools.partial(rim_kernel, rows),
        out_shape=[jax.ShapeDtypeStruct((n, LANES), jnp.float32)] * 3,
        compiler_params=pltpu.CompilerParams(vmem_limit_bytes=20 << 20),
        name="rim_of",
    )(field, logs)


def put_cat(ref, lanes, x):
    p = x.shape[0]
    top, low = split(x)
    ref[0:p, lanes] = top
    ref[p : 2 * p, lanes] = low
    ref[2 * p : 3 * p, lanes] = top


def projected(w_ref, parts):
    p = w_ref.shape[0] // 2
    top, low = parts
    both = jnp.dot(w_ref[...], top, preferred_element_type=jnp.float32)
    rest = jnp.dot(w_ref[0:p, :], low, preferred_element_type=jnp.float32)
    return both[0:p] + both[p : 2 * p] + rest


def resistance(germ_ref, log):
    return jnp.exp2(jnp.dot(germ_ref[...], log, preferred_element_type=jnp.float32))


def inner_kernel(rows, u_ref, log_ref, basis_ref, germ_ref, w_ref, mass_ref, g_ref, u_cat_ref, du_ref, r_ref, f_ref):
    p = mass_ref.shape[0]
    cols = LANES
    lane = lax.broadcasted_iota(jnp.int32, (p, cols), 1)
    above = None
    for y in range(rows):
        here = u_ref[pl.ds(y, p, stride=rows), :]
        put_cat(u_cat_ref, pl.ds(y * cols, cols), here)
        ahead = pltpu.roll(here, cols - 1, axis=1)
        put_cat(du_ref, pl.ds(y * cols, cols), jnp.where(lane == cols - 1, 0.0, ahead - here))
        if y > 0:
            put_cat(du_ref, pl.ds((rows + y - 1) * cols, cols), here - above)
        above = here

    chunks = [("x", y, 2) for y in range(0, rows, 2)]
    chunks += [("y", y, min(2, rows - 1 - y)) for y in range(0, rows - 1, 2)]

    def lanes(chunk):
        kind, y, n = chunk
        return pl.ds((y if kind == "x" else rows + y) * cols, n * cols)

    def values(chunk):
        return jnp.dot(basis_ref[...], du_ref[:, lanes(chunk)], preferred_element_type=jnp.float32)

    def total(chunk):
        kind, y, n = chunk
        if kind == "y":
            return r_ref[:, pl.ds(y * cols, n * cols)] + r_ref[:, pl.ds((y + 1) * cols, n * cols)]
        sums = []
        for k in range(n):
            r = r_ref[:, pl.ds((y + k) * cols, cols)]
            sums.append(r + pltpu.roll(r, cols - 1, axis=1))
        return jnp.concatenate(sums, axis=1)

    def fill(y):
        span = pl.ds(y * cols, 2 * cols)
        r_ref[:, span] = resistance(germ_ref, log_ref[:, span])

    fill(0)
    value = values(chunks[0])
    waiting = None
    for i, chunk in enumerate(chunks):
        later = values(chunks[i + 1]) if i + 1 < len(chunks) else None
        if 2 * (i + 1) < rows:
            fill(2 * (i + 1))
        parts = split(value / total(chunk))
        if waiting is not None:
            f_ref[:, lanes(waiting[0])] = projected(w_ref, waiting[1])
        waiting = (chunk, parts)
        value = later
    stored = [
        jnp.dot(mass_ref[...], u_cat_ref[:, pl.ds(y * cols, 2 * cols)], preferred_element_type=jnp.float32)
        for y in range(0, rows, 2)
    ]
    f_ref[:, lanes(waiting[0])] = projected(w_ref, waiting[1])

    for y in range(rows):
        out = stored[y // 2][:, (y % 2) * cols : (y % 2 + 1) * cols]
        later = f_ref[:, pl.ds(y * cols, cols)]
        earlier = jnp.where(lane == 0, 0.0, pltpu.roll(later, 1, axis=1))
        later = jnp.where(lane == cols - 1, 0.0, later)
        out = out - (later - earlier)
        if y < rows - 1:
            out = out - f_ref[:, pl.ds((rows + y) * cols, cols)]
        if y > 0:
            out = out + f_ref[:, pl.ds((rows + y - 1) * cols, cols)]
        g_ref[y] = out


def inner_fluxes(rows, field, logs, basis_cat, weight_cat, germ_cat, mass_cat):
    p, cols = field.shape[0] // rows, field.shape[1]
    q = basis_cat.shape[0]
    faces = (2 * rows - 1) * cols
    return pl.pallas_call(
        functools.partial(inner_kernel, rows),
        out_shape=jax.ShapeDtypeStruct((rows, p, cols), jnp.float32),
        scratch_shapes=[
            pltpu.VMEM((3 * p, rows * cols), jnp.bfloat16),
            pltpu.VMEM((3 * p, faces), jnp.bfloat16),
            pltpu.VMEM((q, rows * cols), jnp.float32),
            pltpu.VMEM((p, faces), jnp.float32),
        ],
        compiler_params=pltpu.CompilerParams(vmem_limit_bytes=50 << 20),
        cost_estimate=pl.CostEstimate(
            flops=2 * q * faces * p * 6, bytes_accessed=8 << 20, transcendentals=q * rows * cols
        ),
        name="inner_fluxes",
    )(field, logs, basis_cat, germ_cat, weight_cat, mass_cat)


def outer_kernel(
    rows, open_ref, g_ref, first_ref, last_ref, near_ref, up_ref, down_ref, left_ref, right_ref,
    basis_ref, germ_ref, w_ref, out_ref, du_ref, le_ref, ll_ref,
):
    p = w_ref.shape[0] // 2
    cols = LANES
    near = near_ref[...]
    left = pltpu.roll(left_ref[...], cols - rows, axis=1)
    right = pltpu.roll(right_ref[...], rows, axis=1)
    lane = lax.broadcasted_iota(jnp.int32, near.shape, 1)
    earlier = jnp.where(lane < rows, left, near)
    later = jnp.where(lane < rows, near, right)
    pairs = ((up_ref[...], first_ref[...]), (last_ref[...], down_ref[...]), (earlier, later))
    for k, (e, l) in enumerate(pairs):
        span = pl.ds(k * cols, cols)
        diff = l[0:p] - e[0:p]
        if k < 2:
            diff = diff * open_ref[k]
        else:
            low = lane[0:p] < rows
            diff = jnp.where(low, diff * open_ref[2], diff * open_ref[3])
            diff = jnp.where(lane[0:p] < 2 * rows, diff, 0.0)
        put_cat(du_ref, span, diff)
        put_cat(le_ref, span, e[p : p + SLOT])
        put_cat(ll_ref, span, l[p : p + SLOT])

    def values(span):
        return jnp.dot(basis_ref[...], du_ref[:, span], preferred_element_type=jnp.float32)

    def total(span):
        return resistance(germ_ref, le_ref[:, span]) + resistance(germ_ref, ll_ref[:, span])

    one, two = pl.ds(0, 2 * cols), pl.ds(2 * cols, cols)
    v1 = values(one)
    v2 = values(two)
    t1 = total(one)
    t2 = total(two)
    p1 = split(v1 / t1)
    p2 = split(v2 / t2)
    f1 = projected(w_ref, p1)
    side = projected(w_ref, p2)
    lane = lax.broadcasted_iota(jnp.int32, (p, cols), 1)
    for y in range(rows):
        out = g_ref[y]
        if y == 0:
            out = out + f1[:, 0:cols]
        if y == rows - 1:
            out = out - f1[:, cols : 2 * cols]
        out = out + jnp.where(lane == 0, side[:, y : y + 1], 0.0)
        out = out - jnp.where(lane == cols - 1, side[:, rows + y : rows + y + 1], 0.0)
        out_ref[pl.ds(y, p, stride=rows), :] = out


def outer_fluxes(rows, opened, inner, rims, halos, basis_cat, weight_cat, germ_cat):
    p, cols = inner.shape[1:]
    q = basis_cat.shape[0]
    vmem = pl.BlockSpec(memory_space=pltpu.VMEM)
    return pl.pallas_call(
        functools.partial(outer_kernel, rows),
        in_specs=[pl.BlockSpec(memory_space=pltpu.SMEM)] + [vmem] * 11,
        out_shape=jax.ShapeDtypeStruct((p * rows, cols), jnp.float32),
        scratch_shapes=[
            pltpu.VMEM((3 * p, 3 * cols), jnp.bfloat16),
            pltpu.VMEM((3 * SLOT, 3 * cols), jnp.bfloat16),
            pltpu.VMEM((3 * SLOT, 3 * cols), jnp.bfloat16),
        ],
        compiler_params=pltpu.CompilerParams(vmem_limit_bytes=50 << 20),
        cost_estimate=pl.CostEstimate(
            flops=2 * q * 3 * cols * p * 6, bytes_accessed=8 << 20, transcendentals=q * 6 * cols
        ),
        name="outer_fluxes",
    )(opened, inner, *rims, *halos, basis_cat, germ_cat, weight_cat)


def local_kernel(
    nsa, place_ref, part_ref, s0_ref, s1_ref, s2_ref, s3_ref, cy_ref, cx_ref, cxt_ref, ends_of_ref,
    recip_ref, coef_ref, z_ref, jump_ref, res_ref,
):
    modes, length, cols = s0_ref.shape
    rows = part_ref.shape[2]
    ngy = 4
    ny = ngy * length
    for d, src_ref in enumerate((s0_ref, s1_ref, s2_ref, s3_ref)):
        g = lax.rem(place_ref[0] + ngy - d, ngy)
        for s in range(nsa):
            span = pl.ds(pl.multiple_of(g * length + s * rows, 8), rows)
            for m in range(modes):
                res_ref[span, pl.ds(m * cols, cols)] = (
                    src_ref[m, pl.ds(s * rows, rows), :] - part_ref[s * ngy + g, m]
                )
    spectral = jnp.dot(cy_ref[...], res_ref[...], precision=HIGHEST, preferred_element_type=jnp.float32)
    spectral = jnp.concatenate([spectral[:, m * cols : (m + 1) * cols] for m in range(modes)], axis=0)
    spectral = jnp.dot(spectral, cxt_ref[...], precision=HIGHEST, preferred_element_type=jnp.float32)
    recip = recip_ref[...]
    scaled = jnp.concatenate(
        [recip * spectral[m * ny : (m + 1) * ny] for m in range(modes)], axis=0
    )
    both = lax.dot_general(
        ends_of_ref[...], scaled, (((1,), (1,)), ((), ())),
        precision=HIGHEST, preferred_element_type=jnp.float32,
    )
    pad = [jnp.zeros((8 - modes, ny), jnp.float32)]
    first = jnp.concatenate([both[0:1, m * ny : (m + 1) * ny] for m in range(modes)] + pad, axis=0)
    last = jnp.concatenate([both[1:2, m * ny : (m + 1) * ny] for m in range(modes)] + pad, axis=0)
    blocks = jump_ref.shape[0]
    for i in range(blocks + 1):
        term = coef_ref[0, i : i + 1, :] * first + coef_ref[1, i : i + 1, :] * last
        if i < blocks:
            jump_ref[i, 0:8, :] = term
        if i > 0:
            jump_ref[i - 1, 8:16, :] = term
    z = jnp.dot(scaled, cx_ref[...], precision=HIGHEST, preferred_element_type=jnp.float32)
    for m in range(modes):
        z_ref[m] = z[m * ny : (m + 1) * ny]


def joined_kernel(z_ref, jump_ref, g_first_ref, g_last_ref, cyt_ref, out_ref):
    modes, ny, cols = z_ref.shape
    blocks = jump_ref.shape[0]
    ngy = out_ref.shape[0]
    length = ny // ngy
    total = jump_ref[0]
    for i in range(1, blocks):
        total = total + jump_ref[i]
    both = jnp.concatenate([total, jnp.zeros((LANES - 16, ny), jnp.float32)], axis=0).T
    x = jnp.concatenate(
        [
            z_ref[m]
            + g_first_ref[...] * both[:, m : m + 1]
            - g_last_ref[...] * both[:, 8 + m : 9 + m]
            for m in range(modes)
        ],
        axis=1,
    )
    out = jnp.dot(cyt_ref[...], x, precision=HIGHEST, preferred_element_type=jnp.float32)
    for g in range(ngy):
        for m in range(modes):
            out_ref[g, m] = out[g * length : (g + 1) * length, m * cols : (m + 1) * cols]


def solve_tables(mean_perm, ny, cols, blocks, position):
    cx = cosine_matrix(cols)
    lam_y = jnp.asarray(eigen_values(ny, ny), jnp.float32)
    lam_x = jnp.asarray(eigen_values(cols, cols), jnp.float32)
    recip = 1.0 / (storage_rate + mean_perm * (lam_y[:, None] + lam_x[None, :]))
    first = jnp.asarray(cx[:, 0][:, None] * cx, jnp.float32)
    last = jnp.asarray(cx[:, -1][:, None] * cx, jnp.float32)
    g_first = jnp.dot(recip, first, precision=HIGHEST)
    g_last = jnp.dot(recip, last, precision=HIGHEST)
    k = np.arange(1, blocks)
    sine = math.sqrt(2.0 / blocks) * np.sin(np.pi * np.outer(np.arange(0, blocks + 1), k) / blocks)
    sine[0] = 0.0
    sine[blocks] = 0.0
    theta = jnp.asarray(2.0 * np.cos(np.pi * k / blocks), jnp.float32)
    spread = 1.0 / (
        1.0 / mean_perm + g_first[:, 0:1] + g_last[:, cols - 1 : cols] - g_first[:, cols - 1 : cols] * theta
    )
    table = jnp.asarray(sine, jnp.float32)
    coef = []
    for end, sign in ((0, -1.0), (1, 1.0)):
        mine = sign * lax.dynamic_slice_in_dim(table, position + end, 1, axis=0)
        coef.append(jnp.einsum("ik,jk->ij", table, spread * mine, precision=HIGHEST))
    return recip, g_first, g_last, jnp.stack(coef)


def rotated(x, axis, by):
    count = lax.axis_size(axis)
    return lax.ppermute(x, axis, [(i, (i + by) % count) for i in range(count)])


def on_device(
    field_now, field_before, source, log_fields, weights, mean_perm, node_index, mode_index
):
    nsa, ngy, ngx = (lax.axis_size(a) for a in ("sa", "gy", "gx"))
    modes, length, cols = field_now.shape
    rows = length // nsa
    p = modes * nsa
    ny = length * ngy
    sub = modes // ngy
    fields = log_fields.shape[0]

    outgoing = field_now.reshape(modes, nsa, rows, cols).transpose(1, 0, 2, 3)
    field = lax.all_to_all(outgoing, "sa", 0, 0, tiled=True).reshape(p * rows, cols)

    place = lax.axis_index("gy")
    blocks = source.reshape(ngy, sub, length, cols)
    pieces = [lax.dynamic_index_in_dim(blocks, (place + d) % ngy, 0, keepdims=False) for d in range(ngy)]
    pieces = pieces[:1] + [rotated(pieces[d], "gy", d) for d in range(1, ngy)]

    basis_cat, weight_cat, germ_cat, mass_cat = node_tables(node_index, mode_index, weights)
    recip, g_first, g_last, coef = solve_tables(mean_perm, ny, cols, ngx, lax.axis_index("gx"))

    row_axis = ("gy", "sa")
    row_index = lax.axis_index(row_axis)
    col_index = lax.axis_index("gx")
    opened = jnp.stack(
        [row_index > 0, row_index < ngy * nsa - 1, col_index > 0, col_index < ngx - 1]
    ).astype(jnp.float32)
    scaled_logs = jnp.pad(
        log_fields * jnp.float32(-math.log2(math.e)), ((0, SLOT - fields), (0, 0), (0, 0))
    )
    top, low = halves(scaled_logs.reshape(SLOT, rows * cols))
    logs = jnp.concatenate([top, low, top], axis=0)

    rims = rim_of(rows, field, scaled_logs.reshape(SLOT * rows, cols))
    first, last, near = rims
    halos = (
        rotated(last, row_axis, 1),
        rotated(first, row_axis, -1),
        rotated(near, "gx", 1),
        rotated(near, "gx", -1),
    )
    inner = inner_fluxes(rows, field, logs, basis_cat, weight_cat, germ_cat, mass_cat)
    galerkin = outer_fluxes(rows, opened, inner, rims, halos, basis_cat, weight_cat, germ_cat)
    part = lax.all_to_all(
        galerkin.reshape(nsa * ngy, sub, rows, cols), ("sa", "gy"), 0, 0, tiled=True
    )

    cy = cosine_matrix(ny)
    cx = cosine_matrix(cols)
    ends_of = np.zeros((8, cols))
    ends_of[0], ends_of[1] = cx[:, 0], cx[:, -1]
    f32 = functools.partial(jnp.asarray, dtype=jnp.float32)
    params = pltpu.CompilerParams(vmem_limit_bytes=40 << 20)
    vmem = pl.BlockSpec(memory_space=pltpu.VMEM)
    z, jumps = pl.pallas_call(
        functools.partial(local_kernel, nsa),
        in_specs=[pl.BlockSpec(memory_space=pltpu.SMEM)] + [vmem] * 11,
        out_shape=(
            jax.ShapeDtypeStruct((sub, ny, cols), jnp.float32),
            jax.ShapeDtypeStruct((ngx, 16, ny), jnp.float32),
        ),
        scratch_shapes=[pltpu.VMEM((ny, sub * cols), jnp.float32)],
        compiler_params=params,
        name="local_solve",
    )(place[None], part, *pieces, f32(cy), f32(cx), f32(cx.T), f32(ends_of), recip, coef)
    jumps = lax.all_to_all(jumps, "gx", 0, 0, tiled=True)
    columns = pl.pallas_call(
        joined_kernel,
        out_shape=jax.ShapeDtypeStruct((ngy, sub, length, cols), jnp.float32),
        compiler_params=params,
        name="joined_solve",
    )(z, jumps, g_first, g_last, f32(cy.T))
    update = lax.all_to_all(columns, "gy", 0, 0, tiled=True).reshape(modes, length, cols)
    fresh = field_before + relax_weight * (field_now - field_before + step_length * update)
    return (fresh, update)


def solution(mesh):
    block = P("sa", "gy", "gx")
    in_specs = (block, block, block, P(None, ("gy", "sa"), "gx"), P(), P(), P(), P())
    return jax.shard_map(
        on_device, mesh=mesh, in_specs=in_specs, out_specs=(block, block), check_vma=False
    )
```

time: 189 us -> 122 us (0.65); the launches traced: 186 us -> 121 us
  starting transfers between devices: 55.5 us -> 34.8 us
  local copies, waits for them, and re-layouts: 22.7 us -> 4.5 us
  other arithmetic: 18.6 us -> 1.26 us
  waiting for transfers between devices: 22.1 us -> 36 us
  blocking collectives: 26.5 us -> 13.5 us
  Pallas kernels: 34 us -> 28.1 us
  matrix products: 4.33 us -> 1.15 us
    all_to_all x2, waiting for transfers between devices: 0.01 us -> 16 us  [the longest x1 10.5 us: on_device(): lax.all_to_all(outgoing, 'sa', 0, 0, tiled=True).reshape(p * rows, cols)]
    all_to_all x1, starting transfers between devices: 17 us -> 4.04 us  [on_device(): lax.all_to_all(galerkin.reshape(nsa * ngy, sub, rows, cols), ('sa', 'gy')...]
    convert_element_type x8 -> x1, other arithmetic: 12.9 us -> 0.02 us  [halves(): return (top.astype(jnp.bfloat16), (x - top).astype(jnp.bfloat16))]
    all_gather x1 -> x0, blocking collectives: 12.2 us -> none  [on_device(): all_ends = lax.all_gather(ends, 'gx', axis=0, tiled=False)]
    unnamed x63 -> x44, local copies, waits for them, and re-layouts: 11.5 us -> 2.2 us
    pallas_call x3 -> x5, Pallas kernels: 32.6 us -> 26.8 us  [the longest x1 9.49 us: inner_fluxes(): pl.pallas_call(functools.partial(inner_kernel, rows), out_shape=jax.Shape...]
    all_to_all x2, starting transfers between devices: 19.7 us -> 13.9 us  [the longest x1 10.3 us: on_device(): lax.all_to_all(outgoing, 'sa', 0, 0, tiled=True).reshape(p * rows, cols)]
    concatenate x6 -> x1, other arithmetic: 4.31 us -> 0.01 us  [on_device(): logs = jnp.concatenate([top, low, top], axis=0)]
  transfers between devices with their start and end apart: 11 -> 10, of which waited for: 1 -> 3; matrix products, arithmetic and copies ran while one was open for 20% -> 1% of each run, Pallas kernels for 14% -> 19%
where the time goes in v1:
time: 122 us; the launch traced here: 121 us
  waiting for transfers between devices  36 us (30%)
  starting transfers between devices  34.8 us (29%)
  Pallas kernels  28.1 us (23%)
  blocking collectives  13.5 us (11%)
  local copies, waits for them, and re-layouts  4.5 us (4%)
  between operations  1.71 us (1%)
  other arithmetic  1.26 us (1%)
    all_to_all x1, waiting for transfers between devices, on_device(): lax.all_to_all(galerkin.reshape(nsa * ngy, sub, rows, cols), ('sa', 'gy')...  20 us
    ppermute x7, starting transfers between devices, rotated(): return lax.ppermute(x, axis, [(i, (i + by) % count) for i in range(count)])  16.9 us
    all_to_all x1, blocking collectives, on_device(): lax.all_to_all(columns, 'gy', 0, 0, tiled=True).reshape(modes, length, cols)  13.5 us
    all_to_all x1, waiting for transfers between devices, on_device(): lax.all_to_all(outgoing, 'sa', 0, 0, tiled=True).reshape(p * rows, cols)  10.5 us
    all_to_all x1, starting transfers between devices, on_device(): lax.all_to_all(outgoing, 'sa', 0, 0, tiled=True).reshape(p * rows, cols)  10.3 us
    pallas_call x1, Pallas kernels, inner_fluxes(): pl.pallas_call(functools.partial(inner_kernel, rows), out_shape=jax.Shape...  9.49 us
    pallas_call x1, Pallas kernels, node_tables(): pl.pallas_call(tables_kernel, grid=((q + pad) // QB,), in_specs=[pl.Block...  7.88 us
    all_to_all x1, waiting for transfers between devices, on_device(): jumps = lax.all_to_all(jumps, 'gx', 0, 0, tiled=True)  5.47 us
  transfers between devices with their start and end apart: 10, of which 3 were waited for; matrix products, arithmetic and copies ran while one was open for 1% of the time, Pallas kernels for 19%

profile of v1, /device:TPU:32, one launch (start us, length us, event | category | flops | bytes accessed | tf_op | source)
XLA Modules:
  0.0 121.1 jit_solution(17597825301218681436)
XLA Ops:
  0.6 0.0 copy-start.8
  0.6 2.0 %copy_bitcast_fusion = f32[8,20,8,128]{3,2,1,0:T(8,128)} fusion(f32[20,64,128]{2,1,0:T(8,128)} %param.19), kind=kLoop, calls=%fused_computation.2 | loop fusion | bytes 1310720 | tf_op jit(solution)/shard_map/transpose | solution.py:465
  2.7 10.3 %all-to-all-start = ((f32[8,20,8,128]{3,2,1,0:T(8,128)}), f32[8,20,8,128]{3,2,1,0:T(8,128)S(1)}, u32[]{:S(2)}, u32[]{:S(2)}) async-start(f32[8,20,8,128]{3,2,1,0:T(8,128)} %copy_bitcast_fusion), calls=%async_computation | async-start | bytes 1310720 | tf_op jit(solution)/shard_map/all_to_all | solution.py:466
  13.0 0.0 copy-done.8
  13.0 0.1 dynamic-slice_bitcast_fusion
  13.1 1.6 %collective-permute-start.4 = (f32[5,64,128]{2,1,0:T(8,128)S(1)}, f32[5,64,128]{2,1,0:T(8,128)S(1)}, u32[]{:S(2)}, u32[]{:S(2)}) collective-permute-start(f32[5,64,128]{2,1,0:T(8,128)S(1)} %get-tuple-element.22), channel_id=1, source_target_pairs={{0,8},{8,16},{16,24},{24,0},{1,9},{9,17},{17,25},{25,1},{2,10},{10... | collective-permute-start | bytes 491528 | tf_op jit(solution)/shard_map/ppermute | solution.py:451
  14.7 0.0 copy-done.11
  14.7 0.0 copy-done.14
  14.7 0.1 copy.26.mode_ref
  14.8 0.0 copy-done.13
  14.8 7.9 %node_tables.1 = (bf16[1536,480]{1,0:T(8,128)(2,1)S(1)}, bf16[320,1536]{1,0:T(8,128)(2,1)S(1)}, bf16[1536,48]{1,0:T(8,128)(2,1)S(1)}, bf16[160,480]{1,0:T(8,128)(2,1)S(1)}) custom-call(s32[8,1536]{1,0:T(8,128)S(1)} %pad.13.index_ref, s32[160,8]{1,0:T(8,128)S(1)} %copy.26.mode_ref, f32[1,1536]{1,0:T(1,128)S(1)} %broadcast_in_dim.10.weight_ref), custom_call_target="tpu_custom_call" | custom-call | tf_op jit(solution)/shard_map/node_tables/pallas_call | solution.py:115
  22.7 0.0 copy-start
  22.7 1.2 copy-done
  23.9 0.1 add_convert_fusion.open_ref
  24.0 0.0 copy-done.12
  24.0 10.5 %all-to-all-done = f32[8,20,8,128]{3,2,1,0:T(8,128)S(1)} async-done(((f32[8,20,8,128]{3,2,1,0:T(8,128)}), f32[8,20,8,128]{3,2,1,0:T(8,128)S(1)}, u32[]{:S(2)}, u32[]{:S(2)}) %all-to-all-start) | async-done | bytes 655392 | tf_op jit(solution)/shard_map/all_to_all | solution.py:466
  34.6 0.5 rim_of.1
  35.0 0.1 collective-permute-start.2
  35.1 1.7 %collective-permute-start.3 = (f32[176,128]{1,0:T(8,128)S(1)}, f32[176,128]{1,0:T(8,128)S(1)}, u32[]{:S(2)}, u32[]{:S(2)}) collective-permute-start(f32[176,128]{1,0:T(8,128)S(1)} %get-tuple-element.17.near_ref), channel_id=1, source_target_pairs={{0,224},{32,0},{64,32},{96,64},{128,96},{160,128},{192,160},{224,1... | collective-permute-start | bytes 270344 | tf_op jit(solution)/shard_map/ppermute | solution.py:451
  36.9 0.3 collective-permute-start
  37.2 9.8 %collective-permute-start.1 = (f32[176,128]{1,0:T(8,128)S(1)}, f32[176,128]{1,0:T(8,128)S(1)}, u32[]{:S(2)}, u32[]{:S(2)}) collective-permute-start(f32[176,128]{1,0:T(8,128)S(1)} %get-tuple-element.15.first_ref), channel_id=1, source_target_pairs={{0,31},{1,0},{2,1},{3,2},{4,3},{5,4},{6,5},{7,6},{8,7},{9,8},{10,9... | collective-permute-start | bytes 270344 | tf_op jit(solution)/shard_map/ppermute | solution.py:451
  47.0 9.5 %inner_fluxes.1.g_ref = f32[8,160,128]{2,1,0:T(8,128)S(1)} custom-call(f32[1280,128]{1,0:T(8,128)S(1)} %bitcast.45, bf16[48,1024]{1,0:T(8,128)(2,1)S(1)} %pad_maximum_fusion.log_ref, bf16[1536,480]{1,0:T(8,128)(2,1)} %copy-done, bf16[1536,48]{1,0:T(8,128)(2,1)S(1)} %get-tuple-element.12.germ_ref, bf16[320,1536]{1,0:T(8,128)(2,1)S(1)} %get-tuple-element.13.w_ref, ...), custom_call_target="tpu_custom_call" | custom-call | flops 5662310400 | bytes 8388608 | tf_op jit(solution)/shard_map/inner_fluxes/pallas_call | solution.py:267
  56.5 0.0 collective-permute-done.up_ref
  56.5 1.9 %collective-permute-start.5 = (f32[5,64,128]{2,1,0:T(8,128)S(1)}, f32[5,64,128]{2,1,0:T(8,128)S(1)}, u32[]{:S(2)}, u32[]{:S(2)}) collective-permute-start(f32[5,64,128]{2,1,0:T(8,128)S(1)} %get-tuple-element.21), channel_id=1, source_target_pairs={{0,16},{8,24},{16,0},{24,8},{1,17},{9,25},{17,1},{25,9},{2,18},{10... | collective-permute-start | bytes 491528 | tf_op jit(solution)/shard_map/ppermute | solution.py:451
  58.4 0.0 collective-permute-done.1.down_ref
  58.4 0.0 copy-start.19
  58.4 1.4 %collective-permute-start.6 = (f32[5,64,128]{2,1,0:T(8,128)S(1)}, f32[5,64,128]{2,1,0:T(8,128)S(1)}, u32[]{:S(2)}, u32[]{:S(2)}) collective-permute-start(f32[5,64,128]{2,1,0:T(8,128)S(1)} %get-tuple-element.20), channel_id=1, source_target_pairs={{0,24},{8,0},{16,8},{24,16},{1,25},{9,1},{17,9},{25,17},{2,26},{10... | collective-permute-start | bytes 491528 | tf_op jit(solution)/shard_map/ppermute | solution.py:451
  59.9 0.0 collective-permute-done.2.left_ref
  59.9 0.0 collective-permute-done.3.right_ref
  59.9 5.4 %outer_fluxes.1 = f32[1280,128]{1,0:T(8,128)} custom-call(f32[4]{0:T(128)S(1)} %add_convert_fusion.open_ref, f32[8,160,128]{2,1,0:T(8,128)S(1)} %inner_fluxes.1.g_ref, f32[176,128]{1,0:T(8,128)S(1)} %get-tuple-element.15.first_ref, f32[176,128]{1,0:T(8,128)S(1)} %get-tuple-element.16.last_ref, f32[176,128]{1,0:T(8,128)S(1)} %get-tuple-element.17.near_ref, ...), custom_call_target="tpu_custom_call" | custom-call | flops 1132462080 | bytes 8388608 | tf_op jit(solution)/shard_map/outer_fluxes/pallas_call | solution.py:341
  65.3 0.0 copy-start.4
  65.3 0.0 copy-start.5
  65.3 4.0 %all-to-all-start.1 = ((f32[32,5,8,128]{3,2,1,0:T(8,128)}), f32[32,5,8,128]{3,2,1,0:T(8,128)S(1)}, u32[]{:S(2)}, u32[]{:S(2)}) async-start(f32[32,5,8,128]{3,2,1,0:T(8,128)} %bitcast.10), calls=%async_computation.1 | async-start | bytes 1310720 | tf_op jit(solution)/shard_map/all_to_all | solution.py:498
  69.4 0.0 copy-done.17
  70.1 0.0 copy-done.15
  70.1 0.0 copy-done.16
  70.1 0.0 copy-done.19
  70.1 0.4 fusion.1
  70.5 0.0 copy-done.18
  70.5 0.0 copy-start.9
  70.5 0.4 fusion.2
  70.9 0.0 copy-start.1
  70.9 0.0 copy-done.20
  70.9 0.2 convolution_bitcast_fusion
  71.1 0.1 add_divide_fusion.recip_ref
  71.3 0.2 convolution_bitcast_fusion.1
  71.5 0.0 collective-permute-done.4.s1_ref
  71.5 0.0 collective-permute-done.5.s2_ref
  71.5 0.0 collective-permute-done.6.s3_ref
  71.5 20.0 %all-to-all-done.1.part_ref = f32[32,5,8,128]{3,2,1,0:T(8,128)S(1)} async-done(((f32[32,5,8,128]{3,2,1,0:T(8,128)}), f32[32,5,8,128]{3,2,1,0:T(8,128)S(1)}, u32[]{:S(2)}, u32[]{:S(2)}) %all-to-all-start.1) | async-done | bytes 655392 | tf_op jit(solution)/shard_map/all_to_all | solution.py:498
  91.5 0.0 copy-done.9
  91.5 0.0 copy-done.2
  91.5 0.0 copy-done.3
  91.5 0.0 copy-start.10
  91.6 3.6 %local_solve.1 = (f32[5,256,128]{2,1,0:T(8,128)S(1)}, f32[8,16,256]{2,1,0:T(8,128)}) custom-call(s32[1]{0:T(128)} %bitcast.place_ref, f32[32,5,8,128]{3,2,1,0:T(8,128)S(1)} %all-to-all-done.1.part_ref, f32[5,64,128]{2,1,0:T(8,128)S(1)} %get-tuple-element.23.s0_ref, f32[5,64,128]{2,1,0:T(8,128)S(1)} %collective-permute-done.4.s1_ref, ...), custom_call_target="tpu_custom_call" | custom-call | tf_op jit(solution)/shard_map/local_solve/pallas_call | solution.py:509
  95.2 3.6 %all-to-all-start.2 = ((f32[8,16,256]{2,1,0:T(8,128)}), f32[8,16,256]{2,1,0:T(8,128)S(1)}, u32[]{:S(2)}, u32[]{:S(2)}) async-start(f32[8,16,256]{2,1,0:T(8,128)} %get-tuple-element.19), calls=%async_computation.2 | async-start | bytes 262144 | tf_op jit(solution)/shard_map/all_to_all | solution.py:520
  98.7 0.1 copy.27.g_first_ref
  98.8 0.1 copy.28.g_last_ref
  98.9 5.5 %all-to-all-done.2.jump_ref = f32[8,16,256]{2,1,0:T(8,128)S(1)} async-done(((f32[8,16,256]{2,1,0:T(8,128)}), f32[8,16,256]{2,1,0:T(8,128)S(1)}, u32[]{:S(2)}, u32[]{:S(2)}) %all-to-all-start.2) | async-done | bytes 131104 | tf_op jit(solution)/shard_map/all_to_all | solution.py:520
  104.4 0.0 copy-done.1
  104.4 1.3 %joined_solve.1 = f32[4,5,64,128]{3,2,1,0:T(8,128)S(1)} custom-call(f32[5,256,128]{2,1,0:T(8,128)S(1)} %get-tuple-element.18.z_ref, f32[8,16,256]{2,1,0:T(8,128)S(1)} %all-to-all-done.2.jump_ref, f32[256,128]{1,0:T(8,128)S(1)} %copy.27.g_first_ref, f32[256,128]{1,0:T(8,128)S(1)} %copy.28.g_last_ref, f32[256,256]{1,0:T(8,128)S(1)} %copy-done.1), custom_call_target="tpu_custom_call" | custom-call | tf_op jit(solution)/shard_map/joined_solve/pallas_call | solution.py:521
  105.7 13.5 %all_to_all.20 = f32[4,5,64,128]{3,2,1,0:T(8,128)S(1)} all-to-all(f32[4,5,64,128]{3,2,1,0:T(8,128)S(1)} %joined_solve.1), channel_id=1, replica_groups=mesh['gx'=8,'gy'=4,'sa'=8] {'gy'}, dimensions={0} | all-to-all | bytes 1310720 | tf_op jit(solution)/shard_map/all_to_all | solution.py:527
  119.2 1.0 multiply_add_fusion
  120.3 0.8 copy.35
  (28 shorter events, 0.1 us)
Async XLA Ops:
  0.6 12.4 %copy-start.8 = (f32[20,64,128]{2,1,0:T(8,128)S(1)}, f32[20,64,128]{2,1,0:T(8,128)}, u32[]{:S(2)}) copy-start(f32[20,64,128]{2,1,0:T(8,128)} %param.21) | copy-start | bytes 1966084
  2.7 12.0 %copy-start.11 = (s32[1500,8]{0,1:T(8,128)S(1)}, s32[1500,8]{0,1:T(8,128)}, u32[]{:S(2)}) copy-start(s32[1500,8]{0,1:T(8,128)} %param.25) | copy-start | bytes 144004
  2.7 12.0 %copy-start.14 = (s32[160,8]{0,1:T(8,128)S(1)}, s32[160,8]{0,1:T(8,128)}, u32[]{:S(2)}) copy-start(s32[160,8]{0,1:T(8,128)} %param.26) | copy-start | bytes 15364
  2.7 12.1 %copy-start.13 = (f32[1500]{0:T(1024)S(1)}, f32[1500]{0:T(1024)}, u32[]{:S(2)}) copy-start(f32[1500]{0:T(1024)} %param.23) | copy-start | bytes 18004
  2.7 21.3 %copy-start.12 = (f32[9,8,128]{2,1,0:T(8,128)S(1)}, f32[9,8,128]{2,1,0:T(8,128)}, u32[]{:S(2)}) copy-start(f32[9,8,128]{2,1,0:T(8,128)} %param.22) | copy-start | bytes 110596
  2.7 31.9 %all-to-all-start = ((f32[8,20,8,128]{3,2,1,0:T(8,128)}), f32[8,20,8,128]{3,2,1,0:T(8,128)S(1)}, u32[]{:S(2)}, u32[]{:S(2)}) async-start(f32[8,20,8,128]{3,2,1,0:T(8,128)} %copy_bitcast_fusion), calls=%async_computation | async-start | bytes 1310720 | tf_op jit(solution)/shard_map/all_to_all | solution.py:466
  13.1 58.4 %collective-permute-start.4 = (f32[5,64,128]{2,1,0:T(8,128)S(1)}, f32[5,64,128]{2,1,0:T(8,128)S(1)}, u32[]{:S(2)}, u32[]{:S(2)}) collective-permute-start(f32[5,64,128]{2,1,0:T(8,128)S(1)} %get-tuple-element.22), channel_id=1, source_target_pairs={{0,8},{8,16},{16,24},{24,0},{1,9},{9,17},{17,25},{25,1},{2,10},{10... | collective-permute-start | bytes 491528 | tf_op jit(solution)/shard_map/ppermute | solution.py:451
  22.7 1.2 copy-start
  35.0 24.8 %collective-permute-start.2 = (f32[176,128]{1,0:T(8,128)S(1)}, f32[176,128]{1,0:T(8,128)S(1)}, u32[]{:S(2)}, u32[]{:S(2)}) collective-permute-start(f32[176,128]{1,0:T(8,128)S(1)} %get-tuple-element.17.near_ref), channel_id=1, source_target_pairs={{0,32},{32,64},{64,96},{96,128},{128,160},{160,192},{192,224},{224... | collective-permute-start | bytes 270344 | tf_op jit(solution)/shard_map/ppermute | solution.py:451
  35.1 24.8 %collective-permute-start.3 = (f32[176,128]{1,0:T(8,128)S(1)}, f32[176,128]{1,0:T(8,128)S(1)}, u32[]{:S(2)}, u32[]{:S(2)}) collective-permute-start(f32[176,128]{1,0:T(8,128)S(1)} %get-tuple-element.17.near_ref), channel_id=1, source_target_pairs={{0,224},{32,0},{64,32},{96,64},{128,96},{160,128},{192,160},{224,1... | collective-permute-start | bytes 270344 | tf_op jit(solution)/shard_map/ppermute | solution.py:451
  36.9 19.6 %collective-permute-start = (f32[176,128]{1,0:T(8,128)S(1)}, f32[176,128]{1,0:T(8,128)S(1)}, u32[]{:S(2)}, u32[]{:S(2)}) collective-permute-start(f32[176,128]{1,0:T(8,128)S(1)} %get-tuple-element.16.last_ref), channel_id=1, source_target_pairs={{0,1},{1,2},{2,3},{3,4},{4,5},{5,6},{6,7},{7,8},{8,9},{9,10},{10,1... | collective-permute-start | bytes 270344 | tf_op jit(solution)/shard_map/ppermute | solution.py:451
  37.2 21.2 %collective-permute-start.1 = (f32[176,128]{1,0:T(8,128)S(1)}, f32[176,128]{1,0:T(8,128)S(1)}, u32[]{:S(2)}, u32[]{:S(2)}) collective-permute-start(f32[176,128]{1,0:T(8,128)S(1)} %get-tuple-element.15.first_ref), channel_id=1, source_target_pairs={{0,31},{1,0},{2,1},{3,2},{4,3},{5,4},{6,5},{7,6},{8,7},{9,8},{10,9... | collective-permute-start | bytes 270344 | tf_op jit(solution)/shard_map/ppermute | solution.py:451
  56.5 15.0 %collective-permute-start.5 = (f32[5,64,128]{2,1,0:T(8,128)S(1)}, f32[5,64,128]{2,1,0:T(8,128)S(1)}, u32[]{:S(2)}, u32[]{:S(2)}) collective-permute-start(f32[5,64,128]{2,1,0:T(8,128)S(1)} %get-tuple-element.21), channel_id=1, source_target_pairs={{0,16},{8,24},{16,0},{24,8},{1,17},{9,25},{17,1},{25,9},{2,18},{10... | collective-permute-start | bytes 491528 | tf_op jit(solution)/shard_map/ppermute | solution.py:451
  58.4 10.9 %copy-start.17 = (f32[9,7]{1,0:T(8,128)S(1)}, f32[9,7]{1,0:T(8,128)}, u32[]{:S(2)}) copy-start(f32[9,7]{1,0:T(8,128)} %constant.106.clone) | copy-start | bytes 760
  58.4 11.7 %copy-start.15 = (f32[256]{0:T(256)S(1)}, f32[256]{0:T(256)}, u32[]{:S(2)}) copy-start(f32[256]{0:T(256)} %constant.101.clone) | copy-start | bytes 3076
  58.4 11.7 %copy-start.16 = (f32[128]{0:T(128)S(1)}, f32[128]{0:T(128)}, u32[]{:S(2)}) copy-start(f32[128]{0:T(128)} %constant.102.clone) | copy-start | bytes 1540
  58.4 11.7 %copy-start.19 = (f32[128,128]{1,0:T(8,128)S(1)}, f32[128,128]{1,0:T(8,128)}, u32[]{:S(2)}) copy-start(f32[128,128]{1,0:T(8,128)} %constant.104.clone) | copy-start | bytes 196612
  58.4 13.1 %collective-permute-start.6 = (f32[5,64,128]{2,1,0:T(8,128)S(1)}, f32[5,64,128]{2,1,0:T(8,128)S(1)}, u32[]{:S(2)}, u32[]{:S(2)}) collective-permute-start(f32[5,64,128]{2,1,0:T(8,128)S(1)} %get-tuple-element.20), channel_id=1, source_target_pairs={{0,24},{8,0},{16,8},{24,16},{1,25},{9,1},{17,9},{25,17},{2,26},{10... | collective-permute-start | bytes 491528 | tf_op jit(solution)/shard_map/ppermute | solution.py:451
  65.3 5.2 %copy-start.18 = (f32[128,128]{1,0:T(8,128)S(1)}, f32[128,128]{1,0:T(8,128)}, u32[]{:S(2)}) copy-start(f32[128,128]{1,0:T(8,128)} %constant.103.clone) | copy-start | bytes 196612
  65.3 5.7 %copy-start.20 = (f32[7]{0:T(128)S(1)}, f32[7]{0:T(128)}, u32[]{:S(2)}) copy-start(f32[7]{0:T(128)} %constant.105.clone) | copy-start | bytes 88
  65.3 26.2 %copy-start.2 = (f32[256,256]{1,0:T(8,128)S(1)}, f32[256,256]{1,0:T(8,128)}, u32[]{:S(2)}) copy-start(f32[256,256]{1,0:T(8,128)} %constant.107.clone.cy_ref) | copy-start | bytes 786436
  65.3 26.2 %copy-start.3 = (f32[128,128]{1,0:T(8,128)S(1)}, f32[128,128]{1,0:T(8,128)}, u32[]{:S(2)}) copy-start(f32[128,128]{1,0:T(8,128)} %constant.108.clone.cx_ref) | copy-start | bytes 196612
  65.3 26.2 %copy-start.4 = (f32[128,128]{1,0:T(8,128)S(1)}, f32[128,128]{1,0:T(8,128)}, u32[]{:S(2)}) copy-start(f32[128,128]{1,0:T(8,128)} %constant.109.clone.cxt_ref) | copy-start | bytes 196612
  65.3 26.2 %copy-start.5 = (f32[8,128]{1,0:T(8,128)S(1)}, f32[8,128]{1,0:T(8,128)}, u32[]{:S(2)}) copy-start(f32[8,128]{1,0:T(8,128)} %constant.110.clone.ends_of_ref) | copy-start | bytes 12292
  65.3 26.2 %all-to-all-start.1 = ((f32[32,5,8,128]{3,2,1,0:T(8,128)}), f32[32,5,8,128]{3,2,1,0:T(8,128)S(1)}, u32[]{:S(2)}, u32[]{:S(2)}) async-start(f32[32,5,8,128]{3,2,1,0:T(8,128)} %bitcast.10), calls=%async_computation.1 | async-start | bytes 1310720 | tf_op jit(solution)/shard_map/all_to_all | solution.py:498
  70.5 21.0 %copy-start.9 = (f32[256,128]{0,1:T(8,128)}, f32[256,128]{0,1:T(8,128)S(1)}, u32[]{:S(2)}) copy-start(f32[256,128]{0,1:T(8,128)S(1)} %fusion.1) | copy-start | bytes 393220
  70.9 33.5 %copy-start.1 = (f32[256,256]{1,0:T(8,128)S(1)}, f32[256,256]{1,0:T(8,128)}, u32[]{:S(2)}) copy-start(f32[256,256]{1,0:T(8,128)} %constant.111.clone.cyt_ref) | copy-start | bytes 786436
  91.5 7.3 %copy-start.10 = (f32[256,128]{0,1:T(8,128)S(1)}, f32[256,128]{0,1:T(8,128)}, u32[]{:S(2)}) copy-start(f32[256,128]{0,1:T(8,128)} %copy-done.9) | copy-start | bytes 393220
  95.2 9.3 %all-to-all-start.2 = ((f32[8,16,256]{2,1,0:T(8,128)}), f32[8,16,256]{2,1,0:T(8,128)S(1)}, u32[]{:S(2)}, u32[]{:S(2)}) async-start(f32[8,16,256]{2,1,0:T(8,128)} %get-tuple-element.19), calls=%async_computation.2 | async-start | bytes 262144 | tf_op jit(solution)/shard_map/all_to_all | solution.py:520
  104.4 14.8 %copy-start.6 = (f32[20,64,128]{2,1,0:T(8,128)S(1)}, f32[20,64,128]{2,1,0:T(8,128)}, u32[]{:S(2)}) copy-start(f32[20,64,128]{2,1,0:T(8,128)} %param.19) | copy-start | bytes 1966084
  104.4 14.8 %copy-start.7 = (f32[20,64,128]{2,1,0:T(8,128)S(1)}, f32[20,64,128]{2,1,0:T(8,128)}, u32[]{:S(2)}) copy-start(f32[20,64,128]{2,1,0:T(8,128)} %param.20) | copy-start | bytes 1966084

commit v2 on v1

--- a/solution.py
+++ b/solution.py
@@ -49,6 +49,8 @@
 
 
 SLOT = 16
+PIECE = 384
+VMEM_GRANT = 30 << 20
 
 
 def tables_kernel(index_ref, mode_ref, weight_ref, basis_ref, w_ref, germ_ref, mass_ref, sum_ref):
@@ -191,101 +193,128 @@
     return jnp.exp2(jnp.dot(germ_ref[...], log, preferred_element_type=jnp.float32))
 
 
-def inner_kernel(rows, u_ref, log_ref, basis_ref, germ_ref, w_ref, mass_ref, g_ref, u_cat_ref, du_ref, r_ref, f_ref):
+def inner_kernel(
+    rows, x_rows, y_faces, extra, u_ref, log_ref, basis_ref, germ_ref, w_ref, mass_ref, *refs
+):
+    if extra:
+        g_ref, over_ref, u_cat_ref, du_ref, r_ref, f_ref = refs
+    else:
+        g_ref, u_cat_ref, du_ref, r_ref, f_ref = refs
     p = mass_ref.shape[0]
     cols = LANES
     lane = lax.broadcasted_iota(jnp.int32, (p, cols), 1)
+    n_x = len(x_rows)
+    start = min(x_rows[0], y_faces[0] - 1)
+    count = x_rows[-1] + 1 - start
     above = None
-    for y in range(rows):
+    for y in range(start, start + count):
         here = u_ref[pl.ds(y, p, stride=rows), :]
-        put_cat(u_cat_ref, pl.ds(y * cols, cols), here)
-        ahead = pltpu.roll(here, cols - 1, axis=1)
-        put_cat(du_ref, pl.ds(y * cols, cols), jnp.where(lane == cols - 1, 0.0, ahead - here))
-        if y > 0:
-            put_cat(du_ref, pl.ds((rows + y - 1) * cols, cols), here - above)
+        if y in x_rows:
+            at = pl.ds((y - x_rows[0]) * cols, cols)
+            put_cat(u_cat_ref, at, here)
+            ahead = pltpu.roll(here, cols - 1, axis=1)
+            put_cat(du_ref, at, jnp.where(lane == cols - 1, 0.0, ahead - here))
+        if y in y_faces and above is not None:
+            put_cat(du_ref, pl.ds((n_x + y - y_faces[0]) * cols, cols), here - above)
         above = here
 
-    chunks = [("x", y, 2) for y in range(0, rows, 2)]
-    chunks += [("y", y, min(2, rows - 1 - y)) for y in range(0, rows - 1, 2)]
+    chunks = [("x", y, min(2, x_rows[-1] + 1 - y)) for y in x_rows[::2]]
+    chunks += [("y", y, min(2, y_faces[-1] + 1 - y)) for y in y_faces[::2]]
 
     def lanes(chunk):
         kind, y, n = chunk
-        return pl.ds((y if kind == "x" else rows + y) * cols, n * cols)
+        at = y - x_rows[0] if kind == "x" else n_x + y - y_faces[0]
+        return pl.ds(at * cols, n * cols)
 
     def values(chunk):
         return jnp.dot(basis_ref[...], du_ref[:, lanes(chunk)], preferred_element_type=jnp.float32)
 
     def total(chunk):
         kind, y, n = chunk
+        y = y - start
         if kind == "y":
-            return r_ref[:, pl.ds(y * cols, n * cols)] + r_ref[:, pl.ds((y + 1) * cols, n * cols)]
+            return r_ref[:, pl.ds((y - 1) * cols, n * cols)] + r_ref[:, pl.ds(y * cols, n * cols)]
         sums = []
         for k in range(n):
             r = r_ref[:, pl.ds((y + k) * cols, cols)]
             sums.append(r + pltpu.roll(r, cols - 1, axis=1))
         return jnp.concatenate(sums, axis=1)
 
-    def fill(y):
-        span = pl.ds(y * cols, 2 * cols)
-        r_ref[:, span] = resistance(germ_ref, log_ref[:, span])
+    filled = []
+
+    def fill(top):
+        done = filled[-1] if filled else 0
+        if done < count:
+            n = min(2 if (count - done) % 2 == 0 else 3, count - done)
+            r_ref[:, pl.ds(done * cols, n * cols)] = resistance(
+                germ_ref, log_ref[:, pl.ds((start + done) * cols, n * cols)]
+            )
+            filled.append(done + n)
 
     fill(0)
     value = values(chunks[0])
     waiting = None
     for i, chunk in enumerate(chunks):
         later = values(chunks[i + 1]) if i + 1 < len(chunks) else None
-        if 2 * (i + 1) < rows:
-            fill(2 * (i + 1))
+        fill(i + 1)
         parts = split(value / total(chunk))
         if waiting is not None:
             f_ref[:, lanes(waiting[0])] = projected(w_ref, waiting[1])
         waiting = (chunk, parts)
         value = later
     stored = [
-        jnp.dot(mass_ref[...], u_cat_ref[:, pl.ds(y * cols, 2 * cols)], preferred_element_type=jnp.float32)
-        for y in range(0, rows, 2)
+        jnp.dot(mass_ref[...], u_cat_ref[:, pl.ds(k * cols, 2 * cols)], preferred_element_type=jnp.float32)
+        for k in range(0, n_x, 2)
     ]
     f_ref[:, lanes(waiting[0])] = projected(w_ref, waiting[1])
 
-    for y in range(rows):
-        out = stored[y // 2][:, (y % 2) * cols : (y % 2 + 1) * cols]
-        later = f_ref[:, pl.ds(y * cols, cols)]
+    for k, y in enumerate(x_rows):
+        out = stored[k // 2][:, (k % 2) * cols : (k % 2 + 1) * cols]
+        later = f_ref[:, pl.ds(k * cols, cols)]
         earlier = jnp.where(lane == 0, 0.0, pltpu.roll(later, 1, axis=1))
         later = jnp.where(lane == cols - 1, 0.0, later)
         out = out - (later - earlier)
-        if y < rows - 1:
-            out = out - f_ref[:, pl.ds((rows + y) * cols, cols)]
-        if y > 0:
-            out = out + f_ref[:, pl.ds((rows + y - 1) * cols, cols)]
-        g_ref[y] = out
-
-
-def inner_fluxes(rows, field, logs, basis_cat, weight_cat, germ_cat, mass_cat):
+        if y + 1 in y_faces:
+            out = out - f_ref[:, pl.ds((n_x + y + 1 - y_faces[0]) * cols, cols)]
+        if y in y_faces:
+            out = out + f_ref[:, pl.ds((n_x + y - y_faces[0]) * cols, cols)]
+        g_ref[k] = out
+    if extra:
+        over_ref[...] = f_ref[:, pl.ds(n_x * cols, cols)]
+
+
+def inner_fluxes(rows, x_rows, y_faces, extra, field, logs, basis_cat, weight_cat, germ_cat, mass_cat):
     p, cols = field.shape[0] // rows, field.shape[1]
     q = basis_cat.shape[0]
-    faces = (2 * rows - 1) * cols
+    n = len(x_rows)
+    faces = (n + len(y_faces)) * cols
+    count = x_rows[-1] + 1 - min(x_rows[0], y_faces[0] - 1)
+    shapes = [jax.ShapeDtypeStruct((n, p, cols), jnp.float32)]
+    if extra:
+        shapes.append(jax.ShapeDtypeStruct((p, cols), jnp.float32))
     return pl.pallas_call(
-        functools.partial(inner_kernel, rows),
-        out_shape=jax.ShapeDtypeStruct((rows, p, cols), jnp.float32),
+        functools.partial(inner_kernel, rows, x_rows, y_faces, extra),
+        out_shape=shapes,
         scratch_shapes=[
-            pltpu.VMEM((3 * p, rows * cols), jnp.bfloat16),
+            pltpu.VMEM((3 * p, n * cols), jnp.bfloat16),
             pltpu.VMEM((3 * p, faces), jnp.bfloat16),
-            pltpu.VMEM((q, rows * cols), jnp.float32),
+            pltpu.VMEM((q, count * cols), jnp.float32),
             pltpu.VMEM((p, faces), jnp.float32),
         ],
-        compiler_params=pltpu.CompilerParams(vmem_limit_bytes=50 << 20),
+        compiler_params=pltpu.CompilerParams(vmem_limit_bytes=VMEM_GRANT),
         cost_estimate=pl.CostEstimate(
-            flops=2 * q * faces * p * 6, bytes_accessed=8 << 20, transcendentals=q * rows * cols
+            flops=2 * q * faces * p * 6, bytes_accessed=4 << 20, transcendentals=q * n * cols
         ),
         name="inner_fluxes",
     )(field, logs, basis_cat, germ_cat, weight_cat, mass_cat)
 
 
 def outer_kernel(
-    rows, open_ref, g_ref, first_ref, last_ref, near_ref, up_ref, down_ref, left_ref, right_ref,
-    basis_ref, germ_ref, w_ref, out_ref, du_ref, le_ref, ll_ref,
+    rows, open_ref, ga_ref, gb_ref, over_ref, first_ref, last_ref, near_ref, up_ref, down_ref,
+    left_ref, right_ref, basis_ref, germ_ref, w_ref, out_ref, du_ref, le_ref, ll_ref,
 ):
     p = w_ref.shape[0] // 2
+    q = basis_ref.shape[0]
     cols = LANES
     near = near_ref[...]
     left = pltpu.roll(left_ref[...], cols - rows, axis=1)
@@ -307,52 +336,71 @@
         put_cat(le_ref, span, e[p : p + SLOT])
         put_cat(ll_ref, span, l[p : p + SLOT])
 
-    def values(span):
-        return jnp.dot(basis_ref[...], du_ref[:, span], preferred_element_type=jnp.float32)
-
-    def total(span):
-        return resistance(germ_ref, le_ref[:, span]) + resistance(germ_ref, ll_ref[:, span])
-
-    one, two = pl.ds(0, 2 * cols), pl.ds(2 * cols, cols)
-    v1 = values(one)
-    v2 = values(two)
-    t1 = total(one)
-    t2 = total(two)
-    p1 = split(v1 / t1)
-    p2 = split(v2 / t2)
-    f1 = projected(w_ref, p1)
-    side = projected(w_ref, p2)
+    def values(i):
+        return jnp.dot(
+            basis_ref[pl.ds(i * PIECE, PIECE), :], du_ref[...], preferred_element_type=jnp.float32
+        )
+
+    def total(i):
+        germ = germ_ref[pl.ds(i * PIECE, PIECE), :]
+        e = jnp.exp2(jnp.dot(germ, le_ref[...], preferred_element_type=jnp.float32))
+        return e + jnp.exp2(jnp.dot(germ, ll_ref[...], preferred_element_type=jnp.float32))
+
+    def project(i, parts):
+        top, low = parts
+        at = pl.ds(i * PIECE, PIECE)
+        both = jnp.dot(w_ref[:, at], top, preferred_element_type=jnp.float32)
+        rest = jnp.dot(w_ref[0:p, at], low, preferred_element_type=jnp.float32)
+        return both[0:p] + both[p : 2 * p] + rest
+
+    steps = q // PIECE
+    value, sums = values(0), total(0)
+    flux, waiting = None, None
+    for i in range(steps):
+        later = (values(i + 1), total(i + 1)) if i + 1 < steps else (None, None)
+        parts = split(value / sums)
+        if waiting is not None:
+            term = project(*waiting)
+            flux = term if flux is None else flux + term
+        waiting = (i, parts)
+        value, sums = later
+    flux = flux + project(*waiting)
+
     lane = lax.broadcasted_iota(jnp.int32, (p, cols), 1)
+    half = ga_ref.shape[0]
     for y in range(rows):
-        out = g_ref[y]
+        out = ga_ref[y] if y < half else gb_ref[y - half]
+        if y == half - 1:
+            out = out - over_ref[...]
         if y == 0:
-            out = out + f1[:, 0:cols]
+            out = out + flux[:, 0:cols]
         if y == rows - 1:
-            out = out - f1[:, cols : 2 * cols]
-        out = out + jnp.where(lane == 0, side[:, y : y + 1], 0.0)
-        out = out - jnp.where(lane == cols - 1, side[:, rows + y : rows + y + 1], 0.0)
+            out = out - flux[:, cols : 2 * cols]
+        out = out + jnp.where(lane == 0, flux[:, 2 * cols + y : 2 * cols + y + 1], 0.0)
+        at = 2 * cols + rows + y
+        out = out - jnp.where(lane == cols - 1, flux[:, at : at + 1], 0.0)
         out_ref[pl.ds(y, p, stride=rows), :] = out
 
 
 def outer_fluxes(rows, opened, inner, rims, halos, basis_cat, weight_cat, germ_cat):
-    p, cols = inner.shape[1:]
+    p, cols = inner[0].shape[1:]
     q = basis_cat.shape[0]
     vmem = pl.BlockSpec(memory_space=pltpu.VMEM)
     return pl.pallas_call(
         functools.partial(outer_kernel, rows),
-        in_specs=[pl.BlockSpec(memory_space=pltpu.SMEM)] + [vmem] * 11,
+        in_specs=[pl.BlockSpec(memory_space=pltpu.SMEM)] + [vmem] * 13,
         out_shape=jax.ShapeDtypeStruct((p * rows, cols), jnp.float32),
         scratch_shapes=[
             pltpu.VMEM((3 * p, 3 * cols), jnp.bfloat16),
             pltpu.VMEM((3 * SLOT, 3 * cols), jnp.bfloat16),
             pltpu.VMEM((3 * SLOT, 3 * cols), jnp.bfloat16),
         ],
-        compiler_params=pltpu.CompilerParams(vmem_limit_bytes=50 << 20),
+        compiler_params=pltpu.CompilerParams(vmem_limit_bytes=VMEM_GRANT),
         cost_estimate=pl.CostEstimate(
             flops=2 * q * 3 * cols * p * 6, bytes_accessed=8 << 20, transcendentals=q * 6 * cols
         ),
         name="outer_fluxes",
-    )(opened, inner, *rims, *halos, basis_cat, germ_cat, weight_cat)
+    )(opened, *inner, *rims, *halos, basis_cat, germ_cat, weight_cat)
 
 
 def local_kernel(
@@ -485,6 +533,11 @@
     top, low = halves(scaled_logs.reshape(SLOT, rows * cols))
     logs = jnp.concatenate([top, low, top], axis=0)
 
+    field, *pieces = lax.optimization_barrier((field, *pieces))
+    half = rows // 2
+    tables = (logs, basis_cat, weight_cat, germ_cat, mass_cat)
+    upper = inner_fluxes(rows, range(half), range(1, half), False, field, *tables)
+    field, upper = lax.optimization_barrier((field, upper))
     rims = rim_of(rows, field, scaled_logs.reshape(SLOT * rows, cols))
     first, last, near = rims
     halos = (
@@ -493,8 +546,8 @@
         rotated(near, "gx", 1),
         rotated(near, "gx", -1),
     )
-    inner = inner_fluxes(rows, field, logs, basis_cat, weight_cat, germ_cat, mass_cat)
-    galerkin = outer_fluxes(rows, opened, inner, rims, halos, basis_cat, weight_cat, germ_cat)
+    lower = inner_fluxes(rows, range(half, rows), range(half, rows), True, field, *tables)
+    galerkin = outer_fluxes(rows, opened, upper + lower, rims, halos, basis_cat, weight_cat, germ_cat)
     part = lax.all_to_all(
         galerkin.reshape(nsa * ngy, sub, rows, cols), ("sa", "gy"), 0, 0, tiled=True
     )

time: 122 us -> 127 us (1.041)
  waiting for transfers between devices: 36 us -> 27.2 us
  starting transfers between devices: 34.8 us -> 41.6 us
  local copies, waits for them, and re-layouts: 4.5 us -> 9.07 us
  other arithmetic: 1.26 us -> 3.37 us
    all_to_all x1, waiting for transfers between devices: 10.5 us -> 2.58 us  [on_device(): lax.all_to_all(outgoing, 'sa', 0, 0, tiled=True).reshape(p * rows, cols)]
    all_to_all x1, starting transfers between devices: 4.04 us -> 10.4 us  [on_device(): lax.all_to_all(galerkin.reshape(nsa * ngy, sub, rows, cols), ('sa', 'gy')...]
    unnamed x44 -> x56, local copies, waits for them, and re-layouts: 2.2 us -> 5.37 us
    concatenate x1, other arithmetic: 0.01 us -> 1.5 us  [on_device(): logs = jnp.concatenate([top, low, top], axis=0)]
    pallas_call x1 -> x2, Pallas kernels: 9.49 us -> 9.5 us  [inner_fluxes(): pl.pallas_call(functools.partial(inner_kernel, rows, x_rows, y_faces, ext...]
  transfers between devices with their start and end apart: 10 -> 10, of which waited for: 3 -> 3; matrix products, arithmetic and copies ran while one was open for 1% -> 4% of each run, Pallas kernels for 19% -> 10%
where the time goes in v2:
time: 127 us; the launch traced here: 126 us
  starting transfers between devices  41.6 us (33%)
  Pallas kernels  28.4 us (22%)
  waiting for transfers between devices  27.2 us (21%)
  blocking collectives  13.9 us (11%)
  local copies, waits for them, and re-layouts  9.07 us (7%)
  other arithmetic  3.37 us (3%)
  between operations  1.71 us (1%)
    all_to_all x1, waiting for transfers between devices, on_device(): lax.all_to_all(galerkin.reshape(nsa * ngy, sub, rows, cols), ('sa', 'gy')...  19.2 us
    ppermute x7, starting transfers between devices, rotated(): return lax.ppermute(x, axis, [(i, (i + by) % count) for i in range(count)])  17.6 us
    all_to_all x1, blocking collectives, on_device(): lax.all_to_all(columns, 'gy', 0, 0, tiled=True).reshape(modes, length, cols)  13.9 us
    all_to_all x1, starting transfers between devices, on_device(): lax.all_to_all(galerkin.reshape(nsa * ngy, sub, rows, cols), ('sa', 'gy')...  10.4 us
    all_to_all x1, starting transfers between devices, on_device(): lax.all_to_all(outgoing, 'sa', 0, 0, tiled=True).reshape(p * rows, cols)  10.3 us
    pallas_call x2, Pallas kernels, inner_fluxes(): pl.pallas_call(functools.partial(inner_kernel, rows, x_rows, y_faces, ext...  9.5 us
    pallas_call x1, Pallas kernels, node_tables(): pl.pallas_call(tables_kernel, grid=((q + pad) // QB,), in_specs=[pl.Block...  7.85 us
    all_to_all x1, waiting for transfers between devices, on_device(): jumps = lax.all_to_all(jumps, 'gx', 0, 0, tiled=True)  5.45 us
  transfers between devices with their start and end apart: 10, of which 3 were waited for; matrix products, arithmetic and copies ran while one was open for 4% of the time, Pallas kernels for 10%

profile of v2, /device:TPU:32, one launch (start us, length us, event | category | flops | bytes accessed | tf_op | source)
XLA Modules:
  0.0 126.4 jit_solution(5317352486713136287)
XLA Ops:
  0.6 2.0 %copy_bitcast_fusion = f32[8,20,8,128]{3,2,1,0:T(8,128)} fusion(f32[20,64,128]{2,1,0:T(8,128)} %param.19), kind=kLoop, calls=%fused_computation.2 | loop fusion | bytes 1310720 | tf_op jit(solution)/shard_map/transpose | solution.py:513
  2.7 10.3 %all-to-all-start = ((f32[8,20,8,128]{3,2,1,0:T(8,128)}), f32[8,20,8,128]{3,2,1,0:T(8,128)S(1)}, u32[]{:S(2)}, u32[]{:S(2)}) async-start(f32[8,20,8,128]{3,2,1,0:T(8,128)} %copy_bitcast_fusion), calls=%async_computation | async-start | bytes 1310720 | tf_op jit(solution)/shard_map/all_to_all | solution.py:514
  13.0 0.0 copy-done.16
  13.0 0.8 dynamic-slice_bitcast_fusion
  13.9 1.5 %collective-permute-start = (f32[5,64,128]{2,1,0:T(8,128)}, f32[5,64,128]{2,1,0:T(8,128)}, u32[]{:S(2)}, u32[]{:S(2)}) collective-permute-start(f32[5,64,128]{2,1,0:T(8,128)} %get-tuple-element.40), channel_id=1, source_target_pairs={{0,8},{8,16},{16,24},{24,0},{1,9},{9,17},{17,25},{25,1},{2,10},{10... | collective-permute-start | bytes 491528 | tf_op jit(solution)/shard_map/ppermute | solution.py:499
  15.4 2.7 %collective-permute-start.1 = (f32[5,64,128]{2,1,0:T(8,128)}, f32[5,64,128]{2,1,0:T(8,128)}, u32[]{:S(2)}, u32[]{:S(2)}) collective-permute-start(f32[5,64,128]{2,1,0:T(8,128)} %get-tuple-element.39), channel_id=1, source_target_pairs={{0,16},{8,24},{16,0},{24,8},{1,17},{9,25},{17,1},{25,9},{2,18},{10... | collective-permute-start | bytes 491528 | tf_op jit(solution)/shard_map/ppermute | solution.py:499
  18.1 1.4 %collective-permute-start.2 = (f32[5,64,128]{2,1,0:T(8,128)}, f32[5,64,128]{2,1,0:T(8,128)}, u32[]{:S(2)}, u32[]{:S(2)}) collective-permute-start(f32[5,64,128]{2,1,0:T(8,128)} %get-tuple-element.38), channel_id=1, source_target_pairs={{0,24},{8,0},{16,8},{24,16},{1,25},{9,1},{17,9},{25,17},{2,26},{10... | collective-permute-start | bytes 491528 | tf_op jit(solution)/shard_map/ppermute | solution.py:499
  19.5 0.0 copy-done.18
  19.6 0.6 fusion
  20.2 0.1 add_convert_fusion.open_ref
  20.3 0.6 pad.13.index_ref
  20.9 0.1 copy.26.mode_ref
  21.0 0.0 copy-done.19
  21.0 0.0 copy-start.5
  21.1 0.8 copy-done.5
  21.8 7.9 %node_tables.1 = (bf16[1536,480]{1,0:T(8,128)(2,1)S(1)}, bf16[320,1536]{1,0:T(8,128)(2,1)S(1)}, bf16[1536,48]{1,0:T(8,128)(2,1)S(1)}, bf16[160,480]{1,0:T(8,128)(2,1)S(1)}) custom-call(s32[8,1536]{1,0:T(8,128)S(1)} %copy-done.5, s32[160,8]{1,0:T(8,128)S(1)} %copy.26.mode_ref, f32[1,1536]{1,0:T(1,128)S(1)} %broadcast_in_dim.10.weight_ref), custom_call_target="tpu_custom_call" | custom-call | tf_op jit(solution)/shard_map/node_tables/pallas_call | solution.py:117
  29.7 0.0 copy-start
  29.7 0.7 copy-done
  30.5 1.5 %pad_maximum_fusion.log_ref = bf16[48,1024]{1,0:T(8,128)(2,1)} fusion(bf16[16,1024]{1,0:T(8,128)(2,1)} %get-tuple-element.45, bf16[16,1024]{1,0:T(8,128)(2,1)} %get-tuple-element.44), kind=kLoop, calls=%fused_computation.9 | loop fusion | flops 294912 | bytes 163840 | tf_op jit(solution)/shard_map/concatenate | solution.py:534
  32.0 0.0 collective-permute-done.s1_ref
  32.0 0.0 collective-permute-done.1.s2_ref
  32.0 0.0 collective-permute-done.2.s3_ref
  32.0 2.6 %all-to-all-done = f32[8,20,8,128]{3,2,1,0:T(8,128)S(1)} async-done(((f32[8,20,8,128]{3,2,1,0:T(8,128)}), f32[8,20,8,128]{3,2,1,0:T(8,128)S(1)}, u32[]{:S(2)}, u32[]{:S(2)}) %all-to-all-start) | async-done | bytes 655392 | tf_op jit(solution)/shard_map/all_to_all | solution.py:514
  34.6 1.0 copy-done.1
  35.6 0.9 copy-done.6
  36.5 0.9 copy-done.12
  37.4 4.7 %inner_fluxes.2.ga_ref = f32[4,160,128]{2,1,0:T(8,128)S(1)} custom-call(f32[1280,128]{1,0:T(8,128)S(1)} %bitcast.44, bf16[48,1024]{1,0:T(8,128)(2,1)S(1)} %copy-done.6, bf16[1536,480]{1,0:T(8,128)(2,1)S(1)} %get-tuple-element.21.basis_ref, bf16[1536,48]{1,0:T(8,128)(2,1)S(1)} %copy-done.1, bf16[320,1536]{1,0:T(8,128)(2,1)S(1)} %get-tuple-element.23.w_ref, ...), custom_call_target="tpu_custom_call" | custom-call | flops 2642411520 | bytes 4194304 | tf_op jit(solution)/shard_map/inner_fluxes/pallas_call | solution.py:295
  42.1 0.5 rim_of.1
  42.5 0.1 collective-permute-start.5
  42.6 1.7 %collective-permute-start.6 = (f32[176,128]{1,0:T(8,128)S(1)}, f32[176,128]{1,0:T(8,128)S(1)}, u32[]{:S(2)}, u32[]{:S(2)}) collective-permute-start(f32[176,128]{1,0:T(8,128)S(1)} %get-tuple-element.31.near_ref), channel_id=1, source_target_pairs={{0,224},{32,0},{64,32},{96,64},{128,96},{160,128},{192,160},{224,1... | collective-permute-start | bytes 270344 | tf_op jit(solution)/shard_map/ppermute | solution.py:499
  44.4 0.2 collective-permute-start.3
  44.6 9.9 %collective-permute-start.4 = (f32[176,128]{1,0:T(8,128)S(1)}, f32[176,128]{1,0:T(8,128)S(1)}, u32[]{:S(2)}, u32[]{:S(2)}) collective-permute-start(f32[176,128]{1,0:T(8,128)S(1)} %get-tuple-element.29.first_ref), channel_id=1, source_target_pairs={{0,31},{1,0},{2,1},{3,2},{4,3},{5,4},{6,5},{7,6},{8,7},{9,8},{10,9... | collective-permute-start | bytes 270344 | tf_op jit(solution)/shard_map/ppermute | solution.py:499
  54.5 0.0 copy-done.7
  54.5 4.8 %inner_fluxes.3 = (f32[4,160,128]{2,1,0:T(8,128)S(1)}, f32[160,128]{1,0:T(8,128)S(1)}) custom-call(f32[1280,128]{1,0:T(8,128)S(1)} %bitcast.46, bf16[48,1024]{1,0:T(8,128)(2,1)S(1)} %copy-done.7, bf16[1536,480]{1,0:T(8,128)(2,1)S(1)} %get-tuple-element.21.basis_ref, bf16[1536,48]{1,0:T(8,128)(2,1)S(1)} %copy-done.1, ...), custom_call_target="tpu_custom_call" | custom-call | flops 3019898880 | bytes 4194304 | tf_op jit(solution)/shard_map/inner_fluxes/pallas_call | solution.py:295
  59.3 0.0 collective-permute-done.3.up_ref
  59.4 0.0 collective-permute-done.4.down_ref
  59.4 0.0 collective-permute-done.5.left_ref
  59.4 0.0 collective-permute-done.6.right_ref
  59.4 0.0 copy-start.23
  59.4 0.0 copy-start.21
  59.4 0.0 copy-start.22
  59.4 0.0 copy-start.25
  59.5 4.6 %outer_fluxes.1 = f32[1280,128]{1,0:T(8,128)} custom-call(f32[4]{0:T(128)S(1)} %add_convert_fusion.open_ref, f32[4,160,128]{2,1,0:T(8,128)S(1)} %inner_fluxes.2.ga_ref, f32[4,160,128]{2,1,0:T(8,128)S(1)} %get-tuple-element.27.gb_ref, f32[160,128]{1,0:T(8,128)S(1)} %get-tuple-element.28.over_ref, f32[176,128]{1,0:T(8,128)S(1)} %get-tuple-element.29.first_ref, ...), custom_call_target="tpu_custom_call" | custom-call | flops 1132462080 | bytes 8388608 | tf_op jit(solution)/shard_map/outer_fluxes/pallas_call | solution.py:389
  64.0 0.0 copy-start.9
  64.1 0.0 copy-start.10
  64.1 10.4 %all-to-all-start.1 = ((f32[32,5,8,128]{3,2,1,0:T(8,128)}), f32[32,5,8,128]{3,2,1,0:T(8,128)S(1)}, u32[]{:S(2)}, u32[]{:S(2)}) async-start(f32[32,5,8,128]{3,2,1,0:T(8,128)} %bitcast.15), calls=%async_computation.1 | async-start | bytes 1310720 | tf_op jit(solution)/shard_map/all_to_all | solution.py:551
  75.2 0.4 fusion.1
  75.6 0.4 fusion.2
  76.0 0.0 copy-start.3
  76.0 0.2 convolution_bitcast_fusion
  76.2 0.2 convolution_bitcast_fusion.1
  76.4 0.1 add_divide_fusion.recip_ref
  76.6 19.2 %all-to-all-done.1.part_ref = f32[32,5,8,128]{3,2,1,0:T(8,128)S(1)} async-done(((f32[32,5,8,128]{3,2,1,0:T(8,128)}), f32[32,5,8,128]{3,2,1,0:T(8,128)S(1)}, u32[]{:S(2)}, u32[]{:S(2)}) %all-to-all-start.1) | async-done | bytes 655392 | tf_op jit(solution)/shard_map/all_to_all | solution.py:551
  95.8 0.0 copy-done.4
  95.8 0.0 copy-done.9
  95.8 4.7 %local_solve.1 = (f32[5,256,128]{2,1,0:T(8,128)S(1)}, f32[8,16,256]{2,1,0:T(8,128)}) custom-call(s32[1]{0:T(128)} %bitcast.place_ref, f32[32,5,8,128]{3,2,1,0:T(8,128)S(1)} %all-to-all-done.1.part_ref, f32[5,64,128]{2,1,0:T(8,128)S(1)} %get-tuple-element.32.s0_ref, f32[5,64,128]{2,1,0:T(8,128)} %collective-permute-done.s1_ref, ...), custom_call_target="tpu_custom_call" | custom-call | tf_op jit(solution)/shard_map/local_solve/pallas_call | solution.py:562
  100.5 3.3 %all-to-all-start.2 = ((f32[8,16,256]{2,1,0:T(8,128)}), f32[8,16,256]{2,1,0:T(8,128)S(1)}, u32[]{:S(2)}, u32[]{:S(2)}) async-start(f32[8,16,256]{2,1,0:T(8,128)} %get-tuple-element.37), calls=%async_computation.2 | async-start | bytes 262144 | tf_op jit(solution)/shard_map/all_to_all | solution.py:573
  103.8 0.1 copy.27.g_first_ref
  103.9 0.1 copy.28.g_last_ref
  104.0 5.4 %all-to-all-done.2.jump_ref = f32[8,16,256]{2,1,0:T(8,128)S(1)} async-done(((f32[8,16,256]{2,1,0:T(8,128)}), f32[8,16,256]{2,1,0:T(8,128)S(1)}, u32[]{:S(2)}, u32[]{:S(2)}) %all-to-all-start.2) | async-done | bytes 131104 | tf_op jit(solution)/shard_map/all_to_all | solution.py:573
  109.4 1.3 joined_solve.1
  110.7 13.9 %all_to_all.20 = f32[4,5,64,128]{3,2,1,0:T(8,128)S(1)} all-to-all(f32[4,5,64,128]{3,2,1,0:T(8,128)S(1)} %joined_solve.1), channel_id=1, replica_groups=mesh['gx'=8,'gy'=4,'sa'=8] {'gy'}, dimensions={0} | all-to-all | bytes 1310720 | tf_op jit(solution)/shard_map/all_to_all | solution.py:580
  124.6 1.0 multiply_add_fusion
  125.6 0.8 copy.35
  (41 shorter events, 0.1 us)
Async XLA Ops:
  0.6 12.4 %copy-start.16 = (f32[20,64,128]{2,1,0:T(8,128)S(1)}, f32[20,64,128]{2,1,0:T(8,128)}, u32[]{:S(2)}) copy-start(f32[20,64,128]{2,1,0:T(8,128)} %param.21) | copy-start | bytes 1966084
  2.7 16.8 %copy-start.18 = (f32[9,8,128]{2,1,0:T(8,128)S(1)}, f32[9,8,128]{2,1,0:T(8,128)}, u32[]{:S(2)}) copy-start(f32[9,8,128]{2,1,0:T(8,128)} %param.22) | copy-start | bytes 110596
  2.7 17.6 %copy-start.17 = (s32[1500,8]{0,1:T(8,128)S(1)}, s32[1500,8]{0,1:T(8,128)}, u32[]{:S(2)}) copy-start(s32[1500,8]{0,1:T(8,128)} %param.25) | copy-start | bytes 144004
  2.7 18.2 %copy-start.20 = (s32[160,8]{0,1:T(8,128)S(1)}, s32[160,8]{0,1:T(8,128)}, u32[]{:S(2)}) copy-start(s32[160,8]{0,1:T(8,128)} %param.26) | copy-start | bytes 15364
  2.7 18.3 %copy-start.19 = (f32[1500]{0:T(1024)S(1)}, f32[1500]{0:T(1024)}, u32[]{:S(2)}) copy-start(f32[1500]{0:T(1024)} %param.23) | copy-start | bytes 18004
  2.7 31.9 %all-to-all-start = ((f32[8,20,8,128]{3,2,1,0:T(8,128)}), f32[8,20,8,128]{3,2,1,0:T(8,128)S(1)}, u32[]{:S(2)}, u32[]{:S(2)}) async-start(f32[8,20,8,128]{3,2,1,0:T(8,128)} %copy_bitcast_fusion), calls=%async_computation | async-start | bytes 1310720 | tf_op jit(solution)/shard_map/all_to_all | solution.py:514
  13.9 18.1 %collective-permute-start = (f32[5,64,128]{2,1,0:T(8,128)}, f32[5,64,128]{2,1,0:T(8,128)}, u32[]{:S(2)}, u32[]{:S(2)}) collective-permute-start(f32[5,64,128]{2,1,0:T(8,128)} %get-tuple-element.40), channel_id=1, source_target_pairs={{0,8},{8,16},{16,24},{24,0},{1,9},{9,17},{17,25},{25,1},{2,10},{10... | collective-permute-start | bytes 491528 | tf_op jit(solution)/shard_map/ppermute | solution.py:499
  15.4 16.6 %collective-permute-start.1 = (f32[5,64,128]{2,1,0:T(8,128)}, f32[5,64,128]{2,1,0:T(8,128)}, u32[]{:S(2)}, u32[]{:S(2)}) collective-permute-start(f32[5,64,128]{2,1,0:T(8,128)} %get-tuple-element.39), channel_id=1, source_target_pairs={{0,16},{8,24},{16,0},{24,8},{1,17},{9,25},{17,1},{25,9},{2,18},{10... | collective-permute-start | bytes 491528 | tf_op jit(solution)/shard_map/ppermute | solution.py:499
  18.1 13.9 %collective-permute-start.2 = (f32[5,64,128]{2,1,0:T(8,128)}, f32[5,64,128]{2,1,0:T(8,128)}, u32[]{:S(2)}, u32[]{:S(2)}) collective-permute-start(f32[5,64,128]{2,1,0:T(8,128)} %get-tuple-element.38), channel_id=1, source_target_pairs={{0,24},{8,0},{16,8},{24,16},{1,25},{9,1},{17,9},{25,17},{2,26},{10... | collective-permute-start | bytes 491528 | tf_op jit(solution)/shard_map/ppermute | solution.py:499
  21.0 0.8 copy-start.5
  29.7 0.7 copy-start
  30.5 1.5 %copy-start.11 = (bf16[160,480]{1,0:T(8,128)(2,1)}, bf16[160,480]{1,0:T(8,128)(2,1)S(1)}, u32[]{:S(2)}) copy-start(bf16[160,480]{1,0:T(8,128)(2,1)S(1)} %get-tuple-element.24.mass_ref) | copy-start | bytes 460804
  34.6 1.0 copy-start.1
  35.6 0.9 copy-start.6
  36.5 0.9 copy-start.12
  37.4 17.1 %copy-start.7 = (bf16[48,1024]{1,0:T(8,128)(2,1)S(1)}, bf16[48,1024]{1,0:T(8,128)(2,1)}, u32[]{:S(2)}) copy-start(bf16[48,1024]{1,0:T(8,128)(2,1)} %pad_maximum_fusion.log_ref) | copy-start | bytes 294916
  37.4 17.1 %copy-start.13 = (bf16[160,480]{1,0:T(8,128)(2,1)S(1)}, bf16[160,480]{1,0:T(8,128)(2,1)}, u32[]{:S(2)}) copy-start(bf16[160,480]{1,0:T(8,128)(2,1)} %copy-done.11) | copy-start | bytes 460804
  42.5 16.8 %collective-permute-start.5 = (f32[176,128]{1,0:T(8,128)S(1)}, f32[176,128]{1,0:T(8,128)S(1)}, u32[]{:S(2)}, u32[]{:S(2)}) collective-permute-start(f32[176,128]{1,0:T(8,128)S(1)} %get-tuple-element.31.near_ref), channel_id=1, source_target_pairs={{0,32},{32,64},{64,96},{96,128},{128,160},{160,192},{192,224},{224... | collective-permute-start | bytes 270344 | tf_op jit(solution)/shard_map/ppermute | solution.py:499
  42.6 16.8 %collective-permute-start.6 = (f32[176,128]{1,0:T(8,128)S(1)}, f32[176,128]{1,0:T(8,128)S(1)}, u32[]{:S(2)}, u32[]{:S(2)}) collective-permute-start(f32[176,128]{1,0:T(8,128)S(1)} %get-tuple-element.31.near_ref), channel_id=1, source_target_pairs={{0,224},{32,0},{64,32},{96,64},{128,96},{160,128},{192,160},{224,1... | collective-permute-start | bytes 270344 | tf_op jit(solution)/shard_map/ppermute | solution.py:499
  44.4 15.0 %collective-permute-start.3 = (f32[176,128]{1,0:T(8,128)S(1)}, f32[176,128]{1,0:T(8,128)S(1)}, u32[]{:S(2)}, u32[]{:S(2)}) collective-permute-start(f32[176,128]{1,0:T(8,128)S(1)} %get-tuple-element.30.last_ref), channel_id=1, source_target_pairs={{0,1},{1,2},{2,3},{3,4},{4,5},{5,6},{6,7},{7,8},{8,9},{9,10},{10,1... | collective-permute-start | bytes 270344 | tf_op jit(solution)/shard_map/ppermute | solution.py:499
  44.6 14.8 %copy-start.2 = (bf16[1536,48]{1,0:T(8,128)(2,1)S(1)}, bf16[1536,48]{1,0:T(8,128)(2,1)}, u32[]{:S(2)}) copy-start(bf16[1536,48]{1,0:T(8,128)(2,1)} %copy-done) | copy-start | bytes 442372
  44.6 14.8 %collective-permute-start.4 = (f32[176,128]{1,0:T(8,128)S(1)}, f32[176,128]{1,0:T(8,128)S(1)}, u32[]{:S(2)}, u32[]{:S(2)}) collective-permute-start(f32[176,128]{1,0:T(8,128)S(1)} %get-tuple-element.29.first_ref), channel_id=1, source_target_pairs={{0,31},{1,0},{2,1},{3,2},{4,3},{5,4},{6,5},{7,6},{8,7},{9,8},{10,9... | collective-permute-start | bytes 270344 | tf_op jit(solution)/shard_map/ppermute | solution.py:499
  59.4 15.0 %copy-start.23 = (f32[9,7]{1,0:T(8,128)S(1)}, f32[9,7]{1,0:T(8,128)}, u32[]{:S(2)}) copy-start(f32[9,7]{1,0:T(8,128)} %constant.106.clone) | copy-start | bytes 760
  59.4 15.8 %copy-start.21 = (f32[256]{0:T(256)S(1)}, f32[256]{0:T(256)}, u32[]{:S(2)}) copy-start(f32[256]{0:T(256)} %constant.101.clone) | copy-start | bytes 3076
  59.4 15.7 %copy-start.22 = (f32[128]{0:T(128)S(1)}, f32[128]{0:T(128)}, u32[]{:S(2)}) copy-start(f32[128]{0:T(128)} %constant.102.clone) | copy-start | bytes 1540
  59.4 15.7 %copy-start.25 = (f32[128,128]{1,0:T(8,128)S(1)}, f32[128,128]{1,0:T(8,128)}, u32[]{:S(2)}) copy-start(f32[128,128]{1,0:T(8,128)} %constant.104.clone) | copy-start | bytes 196612
  64.0 11.5 %copy-start.24 = (f32[128,128]{1,0:T(8,128)S(1)}, f32[128,128]{1,0:T(8,128)}, u32[]{:S(2)}) copy-start(f32[128,128]{1,0:T(8,128)} %constant.103.clone) | copy-start | bytes 196612
  64.0 12.0 %copy-start.26 = (f32[7]{0:T(128)S(1)}, f32[7]{0:T(128)}, u32[]{:S(2)}) copy-start(f32[7]{0:T(128)} %constant.105.clone) | copy-start | bytes 88
  64.0 31.7 %copy-start.4 = (f32[256,256]{1,0:T(8,128)S(1)}, f32[256,256]{1,0:T(8,128)}, u32[]{:S(2)}) copy-start(f32[256,256]{1,0:T(8,128)} %constant.107.clone.cy_ref) | copy-start | bytes 786436
  64.0 31.7 %copy-start.8 = (f32[128,128]{1,0:T(8,128)S(1)}, f32[128,128]{1,0:T(8,128)}, u32[]{:S(2)}) copy-start(f32[128,128]{1,0:T(8,128)} %constant.108.clone.cx_ref) | copy-start | bytes 196612
  64.0 31.7 %copy-start.9 = (f32[128,128]{1,0:T(8,128)S(1)}, f32[128,128]{1,0:T(8,128)}, u32[]{:S(2)}) copy-start(f32[128,128]{1,0:T(8,128)} %constant.109.clone.cxt_ref) | copy-start | bytes 196612
  64.1 31.7 %copy-start.10 = (f32[8,128]{1,0:T(8,128)S(1)}, f32[8,128]{1,0:T(8,128)}, u32[]{:S(2)}) copy-start(f32[8,128]{1,0:T(8,128)} %constant.110.clone.ends_of_ref) | copy-start | bytes 12292
  64.1 31.7 %all-to-all-start.1 = ((f32[32,5,8,128]{3,2,1,0:T(8,128)}), f32[32,5,8,128]{3,2,1,0:T(8,128)S(1)}, u32[]{:S(2)}, u32[]{:S(2)}) async-start(f32[32,5,8,128]{3,2,1,0:T(8,128)} %bitcast.15), calls=%async_computation.1 | async-start | bytes 1310720 | tf_op jit(solution)/shard_map/all_to_all | solution.py:551
  76.0 33.5 %copy-start.3 = (f32[256,256]{1,0:T(8,128)S(1)}, f32[256,256]{1,0:T(8,128)}, u32[]{:S(2)}) copy-start(f32[256,256]{1,0:T(8,128)} %constant.111.clone.cyt_ref) | copy-start | bytes 786436
  100.5 9.0 %all-to-all-start.2 = ((f32[8,16,256]{2,1,0:T(8,128)}), f32[8,16,256]{2,1,0:T(8,128)S(1)}, u32[]{:S(2)}, u32[]{:S(2)}) async-start(f32[8,16,256]{2,1,0:T(8,128)} %get-tuple-element.37), calls=%async_computation.2 | async-start | bytes 262144 | tf_op jit(solution)/shard_map/all_to_all | solution.py:573
  109.4 15.1 %copy-start.14 = (f32[20,64,128]{2,1,0:T(8,128)S(1)}, f32[20,64,128]{2,1,0:T(8,128)}, u32[]{:S(2)}) copy-start(f32[20,64,128]{2,1,0:T(8,128)} %param.19) | copy-start | bytes 1966084
  109.4 15.1 %copy-start.15 = (f32[20,64,128]{2,1,0:T(8,128)S(1)}, f32[20,64,128]{2,1,0:T(8,128)}, u32[]{:S(2)}) copy-start(f32[20,64,128]{2,1,0:T(8,128)} %param.20) | copy-start | bytes 1966084

commit v3 on v1

--- a/solution.py
+++ b/solution.py
@@ -49,6 +49,8 @@
 
 
 SLOT = 16
+PIECE = 384
+VMEM_GRANT = 50 << 20
 
 
 def tables_kernel(index_ref, mode_ref, weight_ref, basis_ref, w_ref, germ_ref, mass_ref, sum_ref):
@@ -191,9 +193,16 @@
     return jnp.exp2(jnp.dot(germ_ref[...], log, preferred_element_type=jnp.float32))
 
 
-def inner_kernel(rows, u_ref, log_ref, basis_ref, germ_ref, w_ref, mass_ref, g_ref, u_cat_ref, du_ref, r_ref, f_ref):
+def inner_kernel(
+    rows, u_ref, log_ref, basis_hbm, germ_ref, w_hbm, mass_ref, g_ref, u_cat_ref, du_ref, r_ref, f_ref,
+    basis_ref, w_ref, sems,
+):
     p = mass_ref.shape[0]
     cols = LANES
+    basis_copy = pltpu.make_async_copy(basis_hbm, basis_ref, sems.at[0])
+    w_copy = pltpu.make_async_copy(w_hbm, w_ref, sems.at[1])
+    basis_copy.start()
+    w_copy.start()
     lane = lax.broadcasted_iota(jnp.int32, (p, cols), 1)
     above = None
     for y in range(rows):
@@ -230,6 +239,8 @@
         r_ref[:, span] = resistance(germ_ref, log_ref[:, span])
 
     fill(0)
+    basis_copy.wait()
+    w_copy.wait()
     value = values(chunks[0])
     waiting = None
     for i, chunk in enumerate(chunks):
@@ -257,23 +268,28 @@
             out = out - f_ref[:, pl.ds((rows + y) * cols, cols)]
         if y > 0:
             out = out + f_ref[:, pl.ds((rows + y - 1) * cols, cols)]
-        g_ref[y] = out
+        g_ref[pl.ds(y, p, stride=rows), :] = out
 
 
 def inner_fluxes(rows, field, logs, basis_cat, weight_cat, germ_cat, mass_cat):
     p, cols = field.shape[0] // rows, field.shape[1]
     q = basis_cat.shape[0]
     faces = (2 * rows - 1) * cols
+    vmem, hbm = (pl.BlockSpec(memory_space=space) for space in (pltpu.VMEM, pltpu.HBM))
     return pl.pallas_call(
         functools.partial(inner_kernel, rows),
-        out_shape=jax.ShapeDtypeStruct((rows, p, cols), jnp.float32),
+        in_specs=[vmem, vmem, hbm, vmem, hbm, vmem],
+        out_shape=jax.ShapeDtypeStruct((p * rows, cols), jnp.float32),
         scratch_shapes=[
             pltpu.VMEM((3 * p, rows * cols), jnp.bfloat16),
             pltpu.VMEM((3 * p, faces), jnp.bfloat16),
             pltpu.VMEM((q, rows * cols), jnp.float32),
             pltpu.VMEM((p, faces), jnp.float32),
+            pltpu.VMEM(basis_cat.shape, basis_cat.dtype),
+            pltpu.VMEM(weight_cat.shape, weight_cat.dtype),
+            pltpu.SemaphoreType.DMA((2,)),
         ],
-        compiler_params=pltpu.CompilerParams(vmem_limit_bytes=50 << 20),
+        compiler_params=pltpu.CompilerParams(vmem_limit_bytes=VMEM_GRANT),
         cost_estimate=pl.CostEstimate(
             flops=2 * q * faces * p * 6, bytes_accessed=8 << 20, transcendentals=q * rows * cols
         ),
@@ -282,10 +298,15 @@
 
 
 def outer_kernel(
-    rows, open_ref, g_ref, first_ref, last_ref, near_ref, up_ref, down_ref, left_ref, right_ref,
-    basis_ref, germ_ref, w_ref, out_ref, du_ref, le_ref, ll_ref,
+    rows, open_ref, first_ref, last_ref, near_ref, up_ref, down_ref,
+    left_ref, right_ref, basis_hbm, germ_ref, w_hbm, out_ref, du_ref, le_ref, ll_ref, basis_ref, w_ref, sems,
 ):
     p = w_ref.shape[0] // 2
+    basis_copy = pltpu.make_async_copy(basis_hbm, basis_ref, sems.at[0])
+    w_copy = pltpu.make_async_copy(w_hbm, w_ref, sems.at[1])
+    basis_copy.start()
+    w_copy.start()
+    q = basis_hbm.shape[0]
     cols = LANES
     near = near_ref[...]
     left = pltpu.roll(left_ref[...], cols - rows, axis=1)
@@ -307,70 +328,107 @@
         put_cat(le_ref, span, e[p : p + SLOT])
         put_cat(ll_ref, span, l[p : p + SLOT])
 
-    def values(span):
-        return jnp.dot(basis_ref[...], du_ref[:, span], preferred_element_type=jnp.float32)
-
-    def total(span):
-        return resistance(germ_ref, le_ref[:, span]) + resistance(germ_ref, ll_ref[:, span])
-
-    one, two = pl.ds(0, 2 * cols), pl.ds(2 * cols, cols)
-    v1 = values(one)
-    v2 = values(two)
-    t1 = total(one)
-    t2 = total(two)
-    p1 = split(v1 / t1)
-    p2 = split(v2 / t2)
-    f1 = projected(w_ref, p1)
-    side = projected(w_ref, p2)
-    lane = lax.broadcasted_iota(jnp.int32, (p, cols), 1)
-    for y in range(rows):
-        out = g_ref[y]
-        if y == 0:
-            out = out + f1[:, 0:cols]
-        if y == rows - 1:
-            out = out - f1[:, cols : 2 * cols]
-        out = out + jnp.where(lane == 0, side[:, y : y + 1], 0.0)
-        out = out - jnp.where(lane == cols - 1, side[:, rows + y : rows + y + 1], 0.0)
-        out_ref[pl.ds(y, p, stride=rows), :] = out
-
-
-def outer_fluxes(rows, opened, inner, rims, halos, basis_cat, weight_cat, germ_cat):
-    p, cols = inner.shape[1:]
-    q = basis_cat.shape[0]
-    vmem = pl.BlockSpec(memory_space=pltpu.VMEM)
+    def values(i):
+        return jnp.dot(
+            basis_ref[pl.ds(i * PIECE, PIECE), :], du_ref[...], preferred_element_type=jnp.float32
+        )
+
+    def total(i):
+        germ = germ_ref[pl.ds(i * PIECE, PIECE), :]
+        e = jnp.exp2(jnp.dot(germ, le_ref[...], preferred_element_type=jnp.float32))
+        return e + jnp.exp2(jnp.dot(germ, ll_ref[...], preferred_element_type=jnp.float32))
+
+    def project(i, parts):
+        top, low = parts
+        at = pl.ds(i * PIECE, PIECE)
+        both = jnp.dot(w_ref[:, at], top, preferred_element_type=jnp.float32)
+        rest = jnp.dot(w_ref[0:p, at], low, preferred_element_type=jnp.float32)
+        return both[0:p] + both[p : 2 * p] + rest
+
+    basis_copy.wait()
+    w_copy.wait()
+    steps = q // PIECE
+    value, sums = values(0), total(0)
+    flux, waiting = None, None
+    for i in range(steps):
+        later = (values(i + 1), total(i + 1)) if i + 1 < steps else (None, None)
+        parts = split(value / sums)
+        if waiting is not None:
+            term = project(*waiting)
+            flux = term if flux is None else flux + term
+        waiting = (i, parts)
+        value, sums = later
+    flux = flux + project(*waiting)
+
+    sub = p // out_ref.shape[0]
+    for d in range(out_ref.shape[0]):
+        span = slice(d * sub, (d + 1) * sub)
+        out_ref[d, 0:sub, :] = flux[span, 0:cols]
+        out_ref[d, sub : 2 * sub, :] = flux[span, cols : 2 * cols]
+        out_ref[d, 2 * sub : 3 * sub, :] = flux[span, 2 * cols : 3 * cols]
+        out_ref[d, 3 * sub : SLOT, :] = jnp.zeros((SLOT - 3 * sub, cols), jnp.float32)
+
+
+def outer_fluxes(rows, parts, opened, rims, halos, basis_cat, weight_cat, germ_cat):
+    q, cols = basis_cat.shape[0], LANES
+    p = weight_cat.shape[0] // 2
+    vmem, hbm = (pl.BlockSpec(memory_space=space) for space in (pltpu.VMEM, pltpu.HBM))
     return pl.pallas_call(
         functools.partial(outer_kernel, rows),
-        in_specs=[pl.BlockSpec(memory_space=pltpu.SMEM)] + [vmem] * 11,
-        out_shape=jax.ShapeDtypeStruct((p * rows, cols), jnp.float32),
+        in_specs=[pl.BlockSpec(memory_space=pltpu.SMEM)] + [vmem] * 7 + [hbm, vmem, hbm],
+        out_shape=jax.ShapeDtypeStruct((parts, SLOT, cols), jnp.float32),
         scratch_shapes=[
             pltpu.VMEM((3 * p, 3 * cols), jnp.bfloat16),
             pltpu.VMEM((3 * SLOT, 3 * cols), jnp.bfloat16),
             pltpu.VMEM((3 * SLOT, 3 * cols), jnp.bfloat16),
+            pltpu.VMEM(basis_cat.shape, basis_cat.dtype),
+            pltpu.VMEM(weight_cat.shape, weight_cat.dtype),
+            pltpu.SemaphoreType.DMA((2,)),
         ],
-        compiler_params=pltpu.CompilerParams(vmem_limit_bytes=50 << 20),
+        compiler_params=pltpu.CompilerParams(vmem_limit_bytes=VMEM_GRANT),
         cost_estimate=pl.CostEstimate(
-            flops=2 * q * 3 * cols * p * 6, bytes_accessed=8 << 20, transcendentals=q * 6 * cols
+            flops=2 * q * 3 * cols * p * 6, bytes_accessed=4 << 20, transcendentals=q * 6 * cols
         ),
         name="outer_fluxes",
-    )(opened, inner, *rims, *halos, basis_cat, germ_cat, weight_cat)
+    )(opened, *rims, *halos, basis_cat, germ_cat, weight_cat)
 
 
 def local_kernel(
-    nsa, place_ref, part_ref, s0_ref, s1_ref, s2_ref, s3_ref, cy_ref, cx_ref, cxt_ref, ends_of_ref,
-    recip_ref, coef_ref, z_ref, jump_ref, res_ref,
+    nsa, place_ref, part_ref, rim_ref, s0_ref, s1_ref, s2_ref, s3_ref, cy_ref, cxt_ref, side_of_ref,
+    ends_of_ref, recip_ref, coef_ref, scaled_ref, jump_ref, res_ref,
 ):
     modes, length, cols = s0_ref.shape
     rows = part_ref.shape[2]
     ngy = 4
     ny = ngy * length
+    row = lax.broadcasted_iota(jnp.int32, (rows, cols), 0)
+    lane = lax.broadcasted_iota(jnp.int32, (rows, cols), 1)
+    own = (lane == row) | (lane == rows + row)
+    first_row, last_row = row == 0, row == rows - 1
+    for g in range(ngy):
+        sides = jnp.concatenate(
+            [
+                jnp.where(own, rim_ref[s * ngy + g, 2 * modes + m : 2 * modes + m + 1, :], 0.0)
+                for s in range(nsa)
+                for m in range(modes)
+            ],
+            axis=0,
+        )
+        sides = jnp.dot(sides, side_of_ref[...], precision=HIGHEST, preferred_element_type=jnp.float32)
+        for s in range(nsa):
+            for m in range(modes):
+                block = s * ngy + g
+                at = (s * modes + m) * rows
+                gain = part_ref[block, m] + sides[at : at + rows]
+                gain = gain + jnp.where(first_row, rim_ref[block, m : m + 1, :], 0.0)
+                gain = gain - jnp.where(last_row, rim_ref[block, modes + m : modes + m + 1, :], 0.0)
+                res_ref[pl.ds(g * length + s * rows, rows), pl.ds(m * cols, cols)] = gain
     for d, src_ref in enumerate((s0_ref, s1_ref, s2_ref, s3_ref)):
         g = lax.rem(place_ref[0] + ngy - d, ngy)
-        for s in range(nsa):
-            span = pl.ds(pl.multiple_of(g * length + s * rows, 8), rows)
-            for m in range(modes):
-                res_ref[span, pl.ds(m * cols, cols)] = (
-                    src_ref[m, pl.ds(s * rows, rows), :] - part_ref[s * ngy + g, m]
-                )
+        span = pl.ds(pl.multiple_of(g * length, 8), length)
+        for m in range(modes):
+            at = pl.ds(m * cols, cols)
+            res_ref[span, at] = src_ref[m] - res_ref[span, at]
     spectral = jnp.dot(cy_ref[...], res_ref[...], precision=HIGHEST, preferred_element_type=jnp.float32)
     spectral = jnp.concatenate([spectral[:, m * cols : (m + 1) * cols] for m in range(modes)], axis=0)
     spectral = jnp.dot(spectral, cxt_ref[...], precision=HIGHEST, preferred_element_type=jnp.float32)
@@ -392,15 +450,19 @@
             jump_ref[i, 0:8, :] = term
         if i > 0:
             jump_ref[i - 1, 8:16, :] = term
-    z = jnp.dot(scaled, cx_ref[...], precision=HIGHEST, preferred_element_type=jnp.float32)
-    for m in range(modes):
-        z_ref[m] = z[m * ny : (m + 1) * ny]
+    scaled_ref[...] = scaled
+
+
+def back_kernel(scaled_ref, cx_ref, z_ref):
+    z_ref[...] = jnp.dot(
+        scaled_ref[...], cx_ref[...], precision=HIGHEST, preferred_element_type=jnp.float32
+    )
 
 
 def joined_kernel(z_ref, jump_ref, g_first_ref, g_last_ref, cyt_ref, out_ref):
-    modes, ny, cols = z_ref.shape
     blocks = jump_ref.shape[0]
-    ngy = out_ref.shape[0]
+    ngy, modes = out_ref.shape[:2]
+    ny, cols = g_first_ref.shape
     length = ny // ngy
     total = jump_ref[0]
     for i in range(1, blocks):
@@ -408,7 +470,7 @@
     both = jnp.concatenate([total, jnp.zeros((LANES - 16, ny), jnp.float32)], axis=0).T
     x = jnp.concatenate(
         [
-            z_ref[m]
+            z_ref[m * ny : (m + 1) * ny]
             + g_first_ref[...] * both[:, m : m + 1]
             - g_last_ref[...] * both[:, 8 + m : 9 + m]
             for m in range(modes)
@@ -451,6 +513,52 @@
     return lax.ppermute(x, axis, [(i, (i + by) % count) for i in range(count)])
 
 
+def row_blocks_kernel(x_ref, out_ref, sems):
+    blocks, _, rows, _ = out_ref.shape
+    copies = [
+        pltpu.make_async_copy(x_ref.at[:, pl.ds(k * rows, rows), :], out_ref.at[k], sems.at[k])
+        for k in range(blocks)
+    ]
+    for copy in copies:
+        copy.start()
+    for copy in copies:
+        copy.wait()
+
+
+def row_blocks(x, blocks):
+    modes, length, cols = x.shape
+    anywhere = pl.BlockSpec(memory_space=pl.ANY)
+    return pl.pallas_call(
+        row_blocks_kernel,
+        in_specs=[anywhere],
+        out_specs=anywhere,
+        out_shape=jax.ShapeDtypeStruct((blocks, modes, length // blocks, cols), x.dtype),
+        scratch_shapes=[pltpu.SemaphoreType.DMA((blocks,))],
+        name="row_blocks",
+    )(x)
+
+
+def relaxed_kernel(now_ref, before_ref, update_ref, fresh_ref, out_ref):
+    update = update_ref[...]
+    before = before_ref[...]
+    fresh_ref[...] = before + relax_weight * (now_ref[...] - before + step_length * update)
+    out_ref[...] = update
+
+
+def relaxed(now, before, update):
+    modes, length, cols = now.shape
+    block = pl.BlockSpec((modes // 4, length, cols), lambda i: (i, 0, 0))
+    shape = jax.ShapeDtypeStruct(now.shape, now.dtype)
+    return pl.pallas_call(
+        relaxed_kernel,
+        grid=(4,),
+        in_specs=[block] * 3,
+        out_specs=[block] * 2,
+        out_shape=[shape] * 2,
+        name="relaxed",
+    )(now, before, update)
+
+
 def on_device(
     field_now, field_before, source, log_fields, weights, mean_perm, node_index, mode_index
 ):
@@ -462,7 +570,7 @@
     sub = modes // ngy
     fields = log_fields.shape[0]
 
-    outgoing = field_now.reshape(modes, nsa, rows, cols).transpose(1, 0, 2, 3)
+    outgoing = row_blocks(field_now, nsa)
     field = lax.all_to_all(outgoing, "sa", 0, 0, tiled=True).reshape(p * rows, cols)
 
     place = lax.axis_index("gy")
@@ -485,6 +593,10 @@
     top, low = halves(scaled_logs.reshape(SLOT, rows * cols))
     logs = jnp.concatenate([top, low, top], axis=0)
 
+    field, *pieces = lax.optimization_barrier((field, *pieces))
+    inner = inner_fluxes(rows, field, logs, basis_cat, weight_cat, germ_cat, mass_cat)
+    field, inner = lax.optimization_barrier((field, inner))
+    part = lax.all_to_all(inner.reshape(nsa * ngy, sub, rows, cols), ("sa", "gy"), 0, 0, tiled=True)
     rims = rim_of(rows, field, scaled_logs.reshape(SLOT * rows, cols))
     first, last, near = rims
     halos = (
@@ -493,31 +605,41 @@
         rotated(near, "gx", 1),
         rotated(near, "gx", -1),
     )
-    inner = inner_fluxes(rows, field, logs, basis_cat, weight_cat, germ_cat, mass_cat)
-    galerkin = outer_fluxes(rows, opened, inner, rims, halos, basis_cat, weight_cat, germ_cat)
-    part = lax.all_to_all(
-        galerkin.reshape(nsa * ngy, sub, rows, cols), ("sa", "gy"), 0, 0, tiled=True
-    )
+    outer = outer_fluxes(rows, nsa * ngy, opened, rims, halos, basis_cat, weight_cat, germ_cat)
+    outer, part = lax.optimization_barrier((outer, part))
+    rim_part = lax.all_to_all(outer, ("sa", "gy"), 0, 0, tiled=True)
 
     cy = cosine_matrix(ny)
     cx = cosine_matrix(cols)
     ends_of = np.zeros((8, cols))
     ends_of[0], ends_of[1] = cx[:, 0], cx[:, -1]
+    side_of = np.zeros((cols, cols))
+    side_of[:rows, 0] = 1.0
+    side_of[rows : 2 * rows, -1] = -1.0
     f32 = functools.partial(jnp.asarray, dtype=jnp.float32)
-    params = pltpu.CompilerParams(vmem_limit_bytes=40 << 20)
+    params = pltpu.CompilerParams(vmem_limit_bytes=VMEM_GRANT)
     vmem = pl.BlockSpec(memory_space=pltpu.VMEM)
-    z, jumps = pl.pallas_call(
+    scaled, jumps = pl.pallas_call(
         functools.partial(local_kernel, nsa),
-        in_specs=[pl.BlockSpec(memory_space=pltpu.SMEM)] + [vmem] * 11,
+        in_specs=[pl.BlockSpec(memory_space=pltpu.SMEM)] + [vmem] * 12,
         out_shape=(
-            jax.ShapeDtypeStruct((sub, ny, cols), jnp.float32),
+            jax.ShapeDtypeStruct((sub * ny, cols), jnp.float32),
             jax.ShapeDtypeStruct((ngx, 16, ny), jnp.float32),
         ),
         scratch_shapes=[pltpu.VMEM((ny, sub * cols), jnp.float32)],
         compiler_params=params,
         name="local_solve",
-    )(place[None], part, *pieces, f32(cy), f32(cx), f32(cx.T), f32(ends_of), recip, coef)
+    )(place[None], part, rim_part, *pieces, f32(cy), f32(cx.T), f32(side_of), f32(ends_of), recip, coef)
     jumps = lax.all_to_all(jumps, "gx", 0, 0, tiled=True)
+    z = pl.pallas_call(
+        back_kernel,
+        out_shape=jax.ShapeDtypeStruct((sub * ny, cols), jnp.float32),
+        compiler_params=params,
+        cost_estimate=pl.CostEstimate(
+            flops=12 * sub * ny * cols * cols, bytes_accessed=2 << 20, transcendentals=0
+        ),
+        name="back",
+    )(scaled, f32(cx))
     columns = pl.pallas_call(
         joined_kernel,
         out_shape=jax.ShapeDtypeStruct((ngy, sub, length, cols), jnp.float32),
@@ -525,7 +647,7 @@
         name="joined_solve",
     )(z, jumps, g_first, g_last, f32(cy.T))
     update = lax.all_to_all(columns, "gy", 0, 0, tiled=True).reshape(modes, length, cols)
-    fresh = field_before + relax_weight * (field_now - field_before + step_length * update)
+    fresh, update = relaxed(field_now, field_before, update)
     return (fresh, update)
 
 

time: 122 us -> 159 us (1.30)
  Pallas kernels: 28.1 us -> 53.8 us
  starting transfers between devices: 34.8 us -> 44.7 us
    pallas_call x1 -> x4, Pallas kernels: 9.49 us -> 35.5 us  [the longest x1 21 us: row_blocks(): pl.pallas_call(row_blocks_kernel, in_specs=[anywhere], out_specs=anywhere...]
    ppermute x7, waiting for transfers between devices: 0.02 us -> 14.1 us  [rotated(): return lax.ppermute(x, axis, [(i, (i + by) % count) for i in range(count)])]
    all_to_all x1 -> x2, waiting for transfers between devices: 20 us -> 12.5 us  [the longest x1 12.5 us: on_device(): rim_part = lax.all_to_all(outer, ('sa', 'gy'), 0, 0, tiled=True)]
    all_to_all x1 -> x2, starting transfers between devices: 4.04 us -> 10.1 us  [the longest x1 6.22 us: on_device(): lax.all_to_all(inner.reshape(nsa * ngy, sub, rows, cols), ('sa', 'gy'), 0...]
    all_to_all x1, waiting for transfers between devices: 10.5 us -> 5.46 us  [on_device(): lax.all_to_all(outgoing, 'sa', 0, 0, tiled=True).reshape(p * rows, cols)]
    all_to_all x1, starting transfers between devices: 3.59 us -> 6.58 us  [on_device(): jumps = lax.all_to_all(jumps, 'gx', 0, 0, tiled=True)]
    unnamed x44 -> x45, local copies, waits for them, and re-layouts: 2.2 us -> 4.7 us
    transpose x1 -> x0, local copies, waits for them, and re-layouts: 2.04 us -> none  [on_device(): outgoing = field_now.reshape(modes, nsa, rows, cols).transpose(1, 0, 2, 3)]
  transfers between devices with their start and end apart: 10 -> 11, of which waited for: 3 -> 4; matrix products, arithmetic and copies ran while one was open for 1% -> 1% of each run, Pallas kernels for 19% -> 8%
where the time goes in v3:
time: 159 us; the launch traced here: 158 us
  Pallas kernels  53.8 us (34%)
  starting transfers between devices  44.7 us (28%)
  waiting for transfers between devices  36.8 us (23%)
  blocking collectives  14.1 us (9%)
  local copies, waits for them, and re-layouts  4.96 us (3%)
  between operations  1.78 us (1%)
    pallas_call x1, Pallas kernels, row_blocks(): pl.pallas_call(row_blocks_kernel, in_specs=[anywhere], out_specs=anywhere...  21 us
    ppermute x7, starting transfers between devices, rotated(): return lax.ppermute(x, axis, [(i, (i + by) % count) for i in range(count)])  17.7 us
    all_to_all x1, blocking collectives, on_device(): lax.all_to_all(columns, 'gy', 0, 0, tiled=True).reshape(modes, length, cols)  14.1 us
    ppermute x7, waiting for transfers between devices, rotated(): return lax.ppermute(x, axis, [(i, (i + by) % count) for i in range(count)])  14.1 us
    all_to_all x1, waiting for transfers between devices, on_device(): rim_part = lax.all_to_all(outer, ('sa', 'gy'), 0, 0, tiled=True)  12.5 us
    all_to_all x1, starting transfers between devices, on_device(): lax.all_to_all(outgoing, 'sa', 0, 0, tiled=True).reshape(p * rows, cols)  10.3 us
    pallas_call x1, Pallas kernels, inner_fluxes(): pl.pallas_call(functools.partial(inner_kernel, rows), in_specs=[vmem, vme...  10.1 us
    pallas_call x1, Pallas kernels, node_tables(): pl.pallas_call(tables_kernel, grid=((q + pad) // QB,), in_specs=[pl.Block...  7.87 us
  transfers between devices with their start and end apart: 11, of which 4 were waited for; matrix products, arithmetic and copies ran while one was open for 1% of the time, Pallas kernels for 8%

profile of v3, /device:TPU:32, one launch (start us, length us, event | category | flops | bytes accessed | tf_op | source)
XLA Modules:
  0.0 157.6 jit_solution(12082919856177008888)
XLA Ops:
  0.6 0.0 copy-start.11
  0.6 21.0 %row_blocks.1 = f32[8,20,8,128]{3,2,1,0:T(8,128)} custom-call(f32[20,64,128]{2,1,0:T(8,128)} %now_ref.1), custom_call_target="tpu_custom_call" | custom-call | tf_op jit(solution)/shard_map/row_blocks/pallas_call | solution.py:531
  21.7 0.0 copy-start.13
  21.7 0.0 copy-start.15
  21.7 0.0 copy-start.12
  21.7 0.0 copy-start.14
  21.7 10.3 %all-to-all-start = ((f32[8,20,8,128]{3,2,1,0:T(8,128)}), f32[8,20,8,128]{3,2,1,0:T(8,128)S(1)}, u32[]{:S(2)}, u32[]{:S(2)}) async-start(f32[8,20,8,128]{3,2,1,0:T(8,128)} %row_blocks.1), calls=%async_computation | async-start | bytes 1310720 | tf_op jit(solution)/shard_map/all_to_all | solution.py:574
  32.1 0.0 copy-done.11
  32.1 0.1 dynamic-slice_bitcast_fusion
  32.1 1.6 collective-permute-start
  33.7 2.7 %collective-permute-start.1 = (f32[5,64,128]{2,1,0:T(8,128)S(1)}, f32[5,64,128]{2,1,0:T(8,128)S(1)}, u32[]{:S(2)}, u32[]{:S(2)}) collective-permute-start(f32[5,64,128]{2,1,0:T(8,128)S(1)} %get-tuple-element.39), channel_id=1, source_target_pairs={{0,16},{8,24},{16,0},{24,8},{1,17},{9,25},{17,1},{25,9},{2,18},{10... | collective-permute-start | bytes 491528 | tf_op jit(solution)/shard_map/ppermute | solution.py:513
  36.4 1.4 collective-permute-start.2
  37.9 0.0 copy-done.13
  37.9 0.0 copy-done.15
  37.9 0.1 copy.25.mode_ref
  38.0 0.0 copy-done.12
  38.1 0.0 copy-done.14
  38.1 7.9 %node_tables.1 = (bf16[1536,480]{1,0:T(8,128)(2,1)S(1)}, bf16[320,1536]{1,0:T(8,128)(2,1)S(1)}, bf16[1536,48]{1,0:T(8,128)(2,1)S(1)}, bf16[160,480]{1,0:T(8,128)(2,1)S(1)}) custom-call(s32[8,1536]{1,0:T(8,128)S(1)} %pad.13.index_ref, s32[160,8]{1,0:T(8,128)S(1)} %copy.25.mode_ref, f32[1,1536]{1,0:T(1,128)S(1)} %broadcast_in_dim.10.weight_ref), custom_call_target="tpu_custom_call" | custom-call | tf_op jit(solution)/shard_map/node_tables/pallas_call | solution.py:117
  46.0 0.0 copy-start.6
  46.0 1.2 copy-done.6
  47.2 1.0 copy-done.8
  48.1 0.0 collective-permute-done.s1_ref
  48.1 0.0 collective-permute-done.1.s2_ref
  48.1 0.0 collective-permute-done.2.s3_ref
  48.1 5.5 %all-to-all-done = f32[8,20,8,128]{3,2,1,0:T(8,128)S(1)} async-done(((f32[8,20,8,128]{3,2,1,0:T(8,128)}), f32[8,20,8,128]{3,2,1,0:T(8,128)S(1)}, u32[]{:S(2)}, u32[]{:S(2)}) %all-to-all-start) | async-done | bytes 655392 | tf_op jit(solution)/shard_map/all_to_all | solution.py:574
  53.6 1.2 copy-done.9
  54.8 10.1 %inner_fluxes.1 = f32[1280,128]{1,0:T(8,128)} custom-call(f32[1280,128]{1,0:T(8,128)S(1)} %bitcast.38, bf16[48,1024]{1,0:T(8,128)(2,1)S(1)} %pad_maximum_fusion.log_ref, bf16[1536,480]{1,0:T(8,128)(2,1)} %copy-done.6, bf16[1536,48]{1,0:T(8,128)(2,1)S(1)} %get-tuple-element.22.germ_ref, bf16[320,1536]{1,0:T(8,128)(2,1)S(1)} %copy-done.9, ...), custom_call_target="tpu_custom_call" | custom-call | flops 5662310400 | bytes 8388608 | tf_op jit(solution)/shard_map/inner_fluxes/pallas_call | solution.py:279
  64.9 0.0 copy-start.20
  64.9 6.2 %all-to-all-start.1 = ((f32[32,5,8,128]{3,2,1,0:T(8,128)}), f32[32,5,8,128]{3,2,1,0:T(8,128)S(1)}, u32[]{:S(2)}, u32[]{:S(2)}) async-start(f32[32,5,8,128]{3,2,1,0:T(8,128)} %bitcast.13), calls=%async_computation.1 | async-start | bytes 1310720 | tf_op jit(solution)/shard_map/all_to_all | solution.py:599
  71.9 0.4 fusion.1
  72.3 0.4 fusion.2
  72.7 0.5 rim_of.1
  73.2 0.1 collective-permute-start.5
  73.3 1.7 %collective-permute-start.6 = (f32[176,128]{1,0:T(8,128)S(1)}, f32[176,128]{1,0:T(8,128)S(1)}, u32[]{:S(2)}, u32[]{:S(2)}) collective-permute-start(f32[176,128]{1,0:T(8,128)S(1)} %get-tuple-element.28.near_ref), channel_id=1, source_target_pairs={{0,224},{32,0},{64,32},{96,64},{128,96},{160,128},{192,160},{224,1... | collective-permute-start | bytes 270344 | tf_op jit(solution)/shard_map/ppermute | solution.py:513
  75.0 1.8 %collective-permute-start.3 = (f32[176,128]{1,0:T(8,128)S(1)}, f32[176,128]{1,0:T(8,128)S(1)}, u32[]{:S(2)}, u32[]{:S(2)}) collective-permute-start(f32[176,128]{1,0:T(8,128)S(1)} %get-tuple-element.27.last_ref), channel_id=1, source_target_pairs={{0,1},{1,2},{2,3},{3,4},{4,5},{5,6},{6,7},{7,8},{8,9},{9,10},{10,1... | collective-permute-start | bytes 270344 | tf_op jit(solution)/shard_map/ppermute | solution.py:513
  76.8 8.4 %collective-permute-start.4 = (f32[176,128]{1,0:T(8,128)S(1)}, f32[176,128]{1,0:T(8,128)S(1)}, u32[]{:S(2)}, u32[]{:S(2)}) collective-permute-start(f32[176,128]{1,0:T(8,128)S(1)} %get-tuple-element.26.first_ref), channel_id=1, source_target_pairs={{0,31},{1,0},{2,1},{3,2},{4,3},{5,4},{6,5},{7,6},{8,7},{9,8},{10,9... | collective-permute-start | bytes 270344 | tf_op jit(solution)/shard_map/ppermute | solution.py:513
  85.2 0.1 add_convert_fusion.open_ref
  85.3 0.0 copy-start.5
  85.3 14.1 %collective-permute-done.3.up_ref = f32[176,128]{1,0:T(8,128)S(1)} collective-permute-done((f32[176,128]{1,0:T(8,128)S(1)}, f32[176,128]{1,0:T(8,128)S(1)}, u32[]{:S(2)}, u32[]{:S(2)}) %collective-permute-start.3) | collective-permute-done | bytes 90144 | tf_op jit(solution)/shard_map/ppermute | solution.py:513
  99.3 0.0 collective-permute-done.4.down_ref
  99.4 0.0 collective-permute-done.5.left_ref
  99.4 0.0 collective-permute-done.6.right_ref
  99.4 0.0 copy-done.7
  99.4 0.0 copy-start.10
  99.4 1.2 copy-done.10
  100.6 4.4 %outer_fluxes.1 = f32[32,16,128]{2,1,0:T(8,128)} custom-call(f32[4]{0:T(128)S(1)} %add_convert_fusion.open_ref, f32[176,128]{1,0:T(8,128)S(1)} %get-tuple-element.26.first_ref, f32[176,128]{1,0:T(8,128)S(1)} %get-tuple-element.27.last_ref, f32[176,128]{1,0:T(8,128)S(1)} %get-tuple-element.28.near_ref, f32[176,128]{1,0:T(8,128)S(1)} %collective-permute-done.3.up_ref, ...), custom_call_target="tpu_custom_call" | custom-call | flops 1132462080 | bytes 4194304 | tf_op jit(solution)/shard_map/outer_fluxes/pallas_call | solution.py:376
  105.0 0.0 all-to-all-done.1.part_ref
  105.0 3.9 %all-to-all-start.2 = ((f32[32,16,128]{2,1,0:T(8,128)}), f32[32,16,128]{2,1,0:T(8,128)S(1)}, u32[]{:S(2)}, u32[]{:S(2)}) async-start(f32[32,16,128]{2,1,0:T(8,128)} %outer_fluxes.1), calls=%async_computation.2 | async-start | bytes 524288 | tf_op jit(solution)/shard_map/all_to_all | solution.py:610
  108.9 0.0 copy-done.21
  108.9 0.2 convolution_bitcast_fusion
  109.1 0.2 convolution_bitcast_fusion.1
  109.3 0.0 copy-start.4
  109.3 0.1 add_divide_fusion.recip_ref
  109.4 12.5 %all-to-all-done.2.rim_ref = f32[32,16,128]{2,1,0:T(8,128)S(1)} async-done(((f32[32,16,128]{2,1,0:T(8,128)}), f32[32,16,128]{2,1,0:T(8,128)S(1)}, u32[]{:S(2)}, u32[]{:S(2)}) %all-to-all-start.2) | async-done | bytes 262176 | tf_op jit(solution)/shard_map/all_to_all | solution.py:610
  121.9 4.4 %local_solve.1 = (f32[1280,128]{1,0:T(8,128)S(1)}, f32[8,16,256]{2,1,0:T(8,128)}) custom-call(s32[1]{0:T(128)} %bitcast.place_ref, f32[32,5,8,128]{3,2,1,0:T(8,128)S(1)} %all-to-all-done.1.part_ref, f32[32,16,128]{2,1,0:T(8,128)S(1)} %all-to-all-done.2.rim_ref, f32[5,64,128]{2,1,0:T(8,128)S(1)} %get-tuple-element.32.s0_ref, ...), custom_call_target="tpu_custom_call" | custom-call | tf_op jit(solution)/shard_map/local_solve/pallas_call | solution.py:622
  126.3 6.6 %all-to-all-start.3 = ((f32[8,16,256]{2,1,0:T(8,128)}), f32[8,16,256]{2,1,0:T(8,128)S(1)}, u32[]{:S(2)}, u32[]{:S(2)}) async-start(f32[8,16,256]{2,1,0:T(8,128)} %get-tuple-element.37), calls=%async_computation.3 | async-start | bytes 262144 | tf_op jit(solution)/shard_map/all_to_all | solution.py:633
  132.9 0.1 copy.26.g_first_ref
  133.0 0.1 copy.27.g_last_ref
  133.1 0.0 copy-done.4
  133.1 0.7 back.1.z_ref
  133.8 4.8 %all-to-all-done.3.jump_ref = f32[8,16,256]{2,1,0:T(8,128)S(1)} async-done(((f32[8,16,256]{2,1,0:T(8,128)}), f32[8,16,256]{2,1,0:T(8,128)S(1)}, u32[]{:S(2)}, u32[]{:S(2)}) %all-to-all-start.3) | async-done | bytes 131104 | tf_op jit(solution)/shard_map/all_to_all | solution.py:633
  138.6 1.3 joined_solve.1
  139.9 14.1 %all_to_all.25 = f32[4,5,64,128]{3,2,1,0:T(8,128)} all-to-all(f32[4,5,64,128]{3,2,1,0:T(8,128)S(1)} %joined_solve.1), channel_id=1, replica_groups=mesh['gx'=8,'gy'=4,'sa'=8] {'gy'}, dimensions={0} | all-to-all | bytes 1310720 | tf_op jit(solution)/shard_map/all_to_all | solution.py:649
  153.9 3.7 %relaxed.1 = (f32[20,64,128]{2,1,0:T(8,128)}, f32[20,64,128]{2,1,0:T(8,128)}) custom-call(f32[20,64,128]{2,1,0:T(8,128)} %now_ref.1, f32[20,64,128]{2,1,0:T(8,128)} %before_ref.1, f32[20,64,128]{2,1,0:T(8,128)} %bitcast.40), custom_call_target="tpu_custom_call" | custom-call | tf_op jit(solution)/shard_map/relaxed/pallas_call | solution.py:552
  (32 shorter events, 0.1 us)
Async XLA Ops:
  0.6 31.4 %copy-start.11 = (f32[20,64,128]{2,1,0:T(8,128)S(1)}, f32[20,64,128]{2,1,0:T(8,128)}, u32[]{:S(2)}) copy-start(f32[20,64,128]{2,1,0:T(8,128)} %param.22) | copy-start | bytes 1966084
  21.7 16.2 %copy-start.13 = (f32[9,8,128]{2,1,0:T(8,128)S(1)}, f32[9,8,128]{2,1,0:T(8,128)}, u32[]{:S(2)}) copy-start(f32[9,8,128]{2,1,0:T(8,128)} %param.23) | copy-start | bytes 110596
  21.7 16.2 %copy-start.15 = (s32[160,8]{0,1:T(8,128)S(1)}, s32[160,8]{0,1:T(8,128)}, u32[]{:S(2)}) copy-start(s32[160,8]{0,1:T(8,128)} %param.27) | copy-start | bytes 15364
  21.7 16.3 %copy-start.12 = (s32[1500,8]{0,1:T(8,128)S(1)}, s32[1500,8]{0,1:T(8,128)}, u32[]{:S(2)}) copy-start(s32[1500,8]{0,1:T(8,128)} %param.26) | copy-start | bytes 144004
  21.7 16.3 %copy-start.14 = (f32[1500]{0:T(1024)S(1)}, f32[1500]{0:T(1024)}, u32[]{:S(2)}) copy-start(f32[1500]{0:T(1024)} %param.24) | copy-start | bytes 18004
  21.7 31.9 %all-to-all-start = ((f32[8,20,8,128]{3,2,1,0:T(8,128)}), f32[8,20,8,128]{3,2,1,0:T(8,128)S(1)}, u32[]{:S(2)}, u32[]{:S(2)}) async-start(f32[8,20,8,128]{3,2,1,0:T(8,128)} %row_blocks.1), calls=%async_computation | async-start | bytes 1310720 | tf_op jit(solution)/shard_map/all_to_all | solution.py:574
  32.1 16.0 %collective-permute-start = (f32[5,64,128]{2,1,0:T(8,128)S(1)}, f32[5,64,128]{2,1,0:T(8,128)S(1)}, u32[]{:S(2)}, u32[]{:S(2)}) collective-permute-start(f32[5,64,128]{2,1,0:T(8,128)S(1)} %get-tuple-element.40), channel_id=1, source_target_pairs={{0,8},{8,16},{16,24},{24,0},{1,9},{9,17},{17,25},{25,1},{2,10},{10... | collective-permute-start | bytes 491528 | tf_op jit(solution)/shard_map/ppermute | solution.py:513
  33.7 14.4 %collective-permute-start.1 = (f32[5,64,128]{2,1,0:T(8,128)S(1)}, f32[5,64,128]{2,1,0:T(8,128)S(1)}, u32[]{:S(2)}, u32[]{:S(2)}) collective-permute-start(f32[5,64,128]{2,1,0:T(8,128)S(1)} %get-tuple-element.39), channel_id=1, source_target_pairs={{0,16},{8,24},{16,0},{24,8},{1,17},{9,25},{17,1},{25,9},{2,18},{10... | collective-permute-start | bytes 491528 | tf_op jit(solution)/shard_map/ppermute | solution.py:513
  36.4 11.7 %collective-permute-start.2 = (f32[5,64,128]{2,1,0:T(8,128)S(1)}, f32[5,64,128]{2,1,0:T(8,128)S(1)}, u32[]{:S(2)}, u32[]{:S(2)}) collective-permute-start(f32[5,64,128]{2,1,0:T(8,128)S(1)} %get-tuple-element.38), channel_id=1, source_target_pairs={{0,24},{8,0},{16,8},{24,16},{1,25},{9,1},{17,9},{25,17},{2,26},{10... | collective-permute-start | bytes 491528 | tf_op jit(solution)/shard_map/ppermute | solution.py:513
  46.0 1.2 copy-start.6
  47.2 1.0 copy-start.8
  53.6 1.2 copy-start.9
  54.8 17.1 %copy-start.18 = (f32[9,7]{1,0:T(8,128)S(1)}, f32[9,7]{1,0:T(8,128)}, u32[]{:S(2)}) copy-start(f32[9,7]{1,0:T(8,128)} %constant.104.clone) | copy-start | bytes 760
  54.8 17.1 %copy-start.16 = (f32[256]{0:T(256)S(1)}, f32[256]{0:T(256)}, u32[]{:S(2)}) copy-start(f32[256]{0:T(256)} %constant.99.clone) | copy-start | bytes 3076
  54.8 17.1 %copy-start.17 = (f32[128]{0:T(128)S(1)}, f32[128]{0:T(128)}, u32[]{:S(2)}) copy-start(f32[128]{0:T(128)} %constant.100.clone) | copy-start | bytes 1540
  54.8 17.1 %copy-start.19 = (f32[128,128]{1,0:T(8,128)S(1)}, f32[128,128]{1,0:T(8,128)}, u32[]{:S(2)}) copy-start(f32[128,128]{1,0:T(8,128)} %constant.102.clone) | copy-start | bytes 196612
  64.9 7.4 %copy-start.20 = (f32[128,128]{1,0:T(8,128)S(1)}, f32[128,128]{1,0:T(8,128)}, u32[]{:S(2)}) copy-start(f32[128,128]{1,0:T(8,128)} %constant.101.clone) | copy-start | bytes 196612
  64.9 40.0 %all-to-all-start.1 = ((f32[32,5,8,128]{3,2,1,0:T(8,128)}), f32[32,5,8,128]{3,2,1,0:T(8,128)S(1)}, u32[]{:S(2)}, u32[]{:S(2)}) async-start(f32[32,5,8,128]{3,2,1,0:T(8,128)} %bitcast.13), calls=%async_computation.1 | async-start | bytes 1310720 | tf_op jit(solution)/shard_map/all_to_all | solution.py:599
  71.9 27.5 %copy-start.7 = (bf16[1536,480]{1,0:T(8,128)(2,1)S(1)}, bf16[1536,480]{1,0:T(8,128)(2,1)}, u32[]{:S(2)}) copy-start(bf16[1536,480]{1,0:T(8,128)(2,1)} %copy-done.6) | copy-start | bytes 4423684
  73.2 26.1 %collective-permute-start.5 = (f32[176,128]{1,0:T(8,128)S(1)}, f32[176,128]{1,0:T(8,128)S(1)}, u32[]{:S(2)}, u32[]{:S(2)}) collective-permute-start(f32[176,128]{1,0:T(8,128)S(1)} %get-tuple-element.28.near_ref), channel_id=1, source_target_pairs={{0,32},{32,64},{64,96},{96,128},{128,160},{160,192},{192,224},{224... | collective-permute-start | bytes 270344 | tf_op jit(solution)/shard_map/ppermute | solution.py:513
  73.3 26.1 %collective-permute-start.6 = (f32[176,128]{1,0:T(8,128)S(1)}, f32[176,128]{1,0:T(8,128)S(1)}, u32[]{:S(2)}, u32[]{:S(2)}) collective-permute-start(f32[176,128]{1,0:T(8,128)S(1)} %get-tuple-element.28.near_ref), channel_id=1, source_target_pairs={{0,224},{32,0},{64,32},{96,64},{128,96},{160,128},{192,160},{224,1... | collective-permute-start | bytes 270344 | tf_op jit(solution)/shard_map/ppermute | solution.py:513
  75.0 24.3 %collective-permute-start.3 = (f32[176,128]{1,0:T(8,128)S(1)}, f32[176,128]{1,0:T(8,128)S(1)}, u32[]{:S(2)}, u32[]{:S(2)}) collective-permute-start(f32[176,128]{1,0:T(8,128)S(1)} %get-tuple-element.27.last_ref), channel_id=1, source_target_pairs={{0,1},{1,2},{2,3},{3,4},{4,5},{5,6},{6,7},{7,8},{8,9},{9,10},{10,1... | collective-permute-start | bytes 270344 | tf_op jit(solution)/shard_map/ppermute | solution.py:513
  76.8 22.5 %collective-permute-start.4 = (f32[176,128]{1,0:T(8,128)S(1)}, f32[176,128]{1,0:T(8,128)S(1)}, u32[]{:S(2)}, u32[]{:S(2)}) collective-permute-start(f32[176,128]{1,0:T(8,128)S(1)} %get-tuple-element.26.first_ref), channel_id=1, source_target_pairs={{0,31},{1,0},{2,1},{3,2},{4,3},{5,4},{6,5},{7,6},{8,7},{9,8},{10,9... | collective-permute-start | bytes 270344 | tf_op jit(solution)/shard_map/ppermute | solution.py:513
  85.2 23.7 %copy-start.21 = (f32[7]{0:T(128)S(1)}, f32[7]{0:T(128)}, u32[]{:S(2)}) copy-start(f32[7]{0:T(128)} %constant.103.clone) | copy-start | bytes 88
  85.3 36.7 %copy-start.1 = (f32[256,256]{1,0:T(8,128)S(1)}, f32[256,256]{1,0:T(8,128)}, u32[]{:S(2)}) copy-start(f32[256,256]{1,0:T(8,128)} %constant.105.clone.cy_ref) | copy-start | bytes 786436
  85.3 36.7 %copy-start.2 = (f32[128,128]{1,0:T(8,128)S(1)}, f32[128,128]{1,0:T(8,128)}, u32[]{:S(2)}) copy-start(f32[128,128]{1,0:T(8,128)} %constant.106.clone.cxt_ref) | copy-start | bytes 196612
  85.3 36.7 %copy-start.3 = (f32[128,128]{1,0:T(8,128)S(1)}, f32[128,128]{1,0:T(8,128)}, u32[]{:S(2)}) copy-start(f32[128,128]{1,0:T(8,128)} %constant.107.clone.side_of_ref) | copy-start | bytes 196612
  85.3 36.7 %copy-start.5 = (f32[8,128]{1,0:T(8,128)S(1)}, f32[8,128]{1,0:T(8,128)}, u32[]{:S(2)}) copy-start(f32[8,128]{1,0:T(8,128)} %constant.108.clone.ends_of_ref) | copy-start | bytes 12292
  99.4 1.2 copy-start.10
  105.0 17.0 %all-to-all-start.2 = ((f32[32,16,128]{2,1,0:T(8,128)}), f32[32,16,128]{2,1,0:T(8,128)S(1)}, u32[]{:S(2)}, u32[]{:S(2)}) async-start(f32[32,16,128]{2,1,0:T(8,128)} %outer_fluxes.1), calls=%async_computation.2 | async-start | bytes 524288 | tf_op jit(solution)/shard_map/all_to_all | solution.py:610
  109.3 23.8 %copy-start.4 = (f32[128,128]{1,0:T(8,128)S(1)}, f32[128,128]{1,0:T(8,128)}, u32[]{:S(2)}) copy-start(f32[128,128]{1,0:T(8,128)} %constant.109.clone.cx_ref) | copy-start | bytes 196612
  126.3 12.3 %copy-start = (f32[256,256]{1,0:T(8,128)S(1)}, f32[256,256]{1,0:T(8,128)}, u32[]{:S(2)}) copy-start(f32[256,256]{1,0:T(8,128)} %constant.110.clone.cyt_ref) | copy-start | bytes 786436
  126.3 12.3 %all-to-all-start.3 = ((f32[8,16,256]{2,1,0:T(8,128)}), f32[8,16,256]{2,1,0:T(8,128)S(1)}, u32[]{:S(2)}, u32[]{:S(2)}) async-start(f32[8,16,256]{2,1,0:T(8,128)} %get-tuple-element.37), calls=%async_computation.3 | async-start | bytes 262144 | tf_op jit(solution)/shard_map/all_to_all | solution.py:633

commit v4 on v1

--- a/solution.py
+++ b/solution.py
@@ -49,6 +49,7 @@
 
 
 SLOT = 16
+PIECE = 384
 
 
 def tables_kernel(index_ref, mode_ref, weight_ref, basis_ref, w_ref, germ_ref, mass_ref, sum_ref):
@@ -282,10 +283,11 @@
 
 
 def outer_kernel(
-    rows, open_ref, g_ref, first_ref, last_ref, near_ref, up_ref, down_ref, left_ref, right_ref,
-    basis_ref, germ_ref, w_ref, out_ref, du_ref, le_ref, ll_ref,
+    rows, open_ref, g_ref, first_ref, last_ref, near_ref, up_ref, down_ref,
+    left_ref, right_ref, basis_ref, germ_ref, w_ref, out_ref, du_ref, le_ref, ll_ref,
 ):
     p = w_ref.shape[0] // 2
+    q = basis_ref.shape[0]
     cols = LANES
     near = near_ref[...]
     left = pltpu.roll(left_ref[...], cols - rows, axis=1)
@@ -307,30 +309,46 @@
         put_cat(le_ref, span, e[p : p + SLOT])
         put_cat(ll_ref, span, l[p : p + SLOT])
 
-    def values(span):
-        return jnp.dot(basis_ref[...], du_ref[:, span], preferred_element_type=jnp.float32)
-
-    def total(span):
-        return resistance(germ_ref, le_ref[:, span]) + resistance(germ_ref, ll_ref[:, span])
-
-    one, two = pl.ds(0, 2 * cols), pl.ds(2 * cols, cols)
-    v1 = values(one)
-    v2 = values(two)
-    t1 = total(one)
-    t2 = total(two)
-    p1 = split(v1 / t1)
-    p2 = split(v2 / t2)
-    f1 = projected(w_ref, p1)
-    side = projected(w_ref, p2)
+    def values(i):
+        return jnp.dot(
+            basis_ref[pl.ds(i * PIECE, PIECE), :], du_ref[...], preferred_element_type=jnp.float32
+        )
+
+    def total(i):
+        germ = germ_ref[pl.ds(i * PIECE, PIECE), :]
+        e = jnp.exp2(jnp.dot(germ, le_ref[...], preferred_element_type=jnp.float32))
+        return e + jnp.exp2(jnp.dot(germ, ll_ref[...], preferred_element_type=jnp.float32))
+
+    def project(i, parts):
+        top, low = parts
+        at = pl.ds(i * PIECE, PIECE)
+        both = jnp.dot(w_ref[:, at], top, preferred_element_type=jnp.float32)
+        rest = jnp.dot(w_ref[0:p, at], low, preferred_element_type=jnp.float32)
+        return both[0:p] + both[p : 2 * p] + rest
+
+    steps = q // PIECE
+    value, sums = values(0), total(0)
+    flux, waiting = None, None
+    for i in range(steps):
+        later = (values(i + 1), total(i + 1)) if i + 1 < steps else (None, None)
+        parts = split(value / sums)
+        if waiting is not None:
+            term = project(*waiting)
+            flux = term if flux is None else flux + term
+        waiting = (i, parts)
+        value, sums = later
+    flux = flux + project(*waiting)
+
     lane = lax.broadcasted_iota(jnp.int32, (p, cols), 1)
     for y in range(rows):
         out = g_ref[y]
         if y == 0:
-            out = out + f1[:, 0:cols]
+            out = out + flux[:, 0:cols]
         if y == rows - 1:
-            out = out - f1[:, cols : 2 * cols]
-        out = out + jnp.where(lane == 0, side[:, y : y + 1], 0.0)
-        out = out - jnp.where(lane == cols - 1, side[:, rows + y : rows + y + 1], 0.0)
+            out = out - flux[:, cols : 2 * cols]
+        out = out + jnp.where(lane == 0, flux[:, 2 * cols + y : 2 * cols + y + 1], 0.0)
+        at = 2 * cols + rows + y
+        out = out - jnp.where(lane == cols - 1, flux[:, at : at + 1], 0.0)
         out_ref[pl.ds(y, p, stride=rows), :] = out
 
 
@@ -356,8 +374,8 @@
 
 
 def local_kernel(
-    nsa, place_ref, part_ref, s0_ref, s1_ref, s2_ref, s3_ref, cy_ref, cx_ref, cxt_ref, ends_of_ref,
-    recip_ref, coef_ref, z_ref, jump_ref, res_ref,
+    nsa, place_ref, part_ref, s0_ref, s1_ref, s2_ref, s3_ref, cy_ref, cxt_ref, ends_of_ref,
+    recip_ref, coef_ref, scaled_ref, jump_ref, res_ref,
 ):
     modes, length, cols = s0_ref.shape
     rows = part_ref.shape[2]
@@ -392,15 +410,19 @@
             jump_ref[i, 0:8, :] = term
         if i > 0:
             jump_ref[i - 1, 8:16, :] = term
-    z = jnp.dot(scaled, cx_ref[...], precision=HIGHEST, preferred_element_type=jnp.float32)
-    for m in range(modes):
-        z_ref[m] = z[m * ny : (m + 1) * ny]
+    scaled_ref[...] = scaled
+
+
+def back_kernel(scaled_ref, cx_ref, z_ref):
+    z_ref[...] = jnp.dot(
+        scaled_ref[...], cx_ref[...], precision=HIGHEST, preferred_element_type=jnp.float32
+    )
 
 
 def joined_kernel(z_ref, jump_ref, g_first_ref, g_last_ref, cyt_ref, out_ref):
-    modes, ny, cols = z_ref.shape
     blocks = jump_ref.shape[0]
-    ngy = out_ref.shape[0]
+    ngy, modes = out_ref.shape[:2]
+    ny, cols = g_first_ref.shape
     length = ny // ngy
     total = jump_ref[0]
     for i in range(1, blocks):
@@ -408,7 +430,7 @@
     both = jnp.concatenate([total, jnp.zeros((LANES - 16, ny), jnp.float32)], axis=0).T
     x = jnp.concatenate(
         [
-            z_ref[m]
+            z_ref[m * ny : (m + 1) * ny]
             + g_first_ref[...] * both[:, m : m + 1]
             - g_last_ref[...] * both[:, 8 + m : 9 + m]
             for m in range(modes)
@@ -485,6 +507,7 @@
     top, low = halves(scaled_logs.reshape(SLOT, rows * cols))
     logs = jnp.concatenate([top, low, top], axis=0)
 
+    field, *pieces = lax.optimization_barrier((field, *pieces))
     rims = rim_of(rows, field, scaled_logs.reshape(SLOT * rows, cols))
     first, last, near = rims
     halos = (
@@ -506,18 +529,27 @@
     f32 = functools.partial(jnp.asarray, dtype=jnp.float32)
     params = pltpu.CompilerParams(vmem_limit_bytes=40 << 20)
     vmem = pl.BlockSpec(memory_space=pltpu.VMEM)
-    z, jumps = pl.pallas_call(
+    scaled, jumps = pl.pallas_call(
         functools.partial(local_kernel, nsa),
-        in_specs=[pl.BlockSpec(memory_space=pltpu.SMEM)] + [vmem] * 11,
+        in_specs=[pl.BlockSpec(memory_space=pltpu.SMEM)] + [vmem] * 10,
         out_shape=(
-            jax.ShapeDtypeStruct((sub, ny, cols), jnp.float32),
+            jax.ShapeDtypeStruct((sub * ny, cols), jnp.float32),
             jax.ShapeDtypeStruct((ngx, 16, ny), jnp.float32),
         ),
         scratch_shapes=[pltpu.VMEM((ny, sub * cols), jnp.float32)],
         compiler_params=params,
         name="local_solve",
-    )(place[None], part, *pieces, f32(cy), f32(cx), f32(cx.T), f32(ends_of), recip, coef)
+    )(place[None], part, *pieces, f32(cy), f32(cx.T), f32(ends_of), recip, coef)
     jumps = lax.all_to_all(jumps, "gx", 0, 0, tiled=True)
+    z = pl.pallas_call(
+        back_kernel,
+        out_shape=jax.ShapeDtypeStruct((sub * ny, cols), jnp.float32),
+        compiler_params=params,
+        cost_estimate=pl.CostEstimate(
+            flops=12 * sub * ny * cols * cols, bytes_accessed=2 << 20, transcendentals=0
+        ),
+        name="back",
+    )(scaled, f32(cx))
     columns = pl.pallas_call(
         joined_kernel,
         out_shape=jax.ShapeDtypeStruct((ngy, sub, length, cols), jnp.float32),

time: 122 us -> 120 us (0.984)
  waiting for transfers between devices: 36 us -> 30.4 us
  starting transfers between devices: 34.8 us -> 37.6 us
    all_to_all x1, waiting for transfers between devices: 10.5 us -> 5.73 us  [on_device(): lax.all_to_all(outgoing, 'sa', 0, 0, tiled=True).reshape(p * rows, cols)]
    all_to_all x1, starting transfers between devices: 4.04 us -> 6.31 us  [on_device(): lax.all_to_all(galerkin.reshape(nsa * ngy, sub, rows, cols), ('sa', 'gy')...]
  transfers between devices with their start and end apart: 10 -> 10, of which waited for: 3 -> 3; matrix products, arithmetic and copies ran while one was open for 1% -> 2% of each run, Pallas kernels for 19% -> 15%
where the time goes in v4:
time: 120 us
  starting transfers between devices  37.6 us (31%)
  waiting for transfers between devices  30.4 us (25%)
  Pallas kernels  28.7 us (24%)
  blocking collectives  13.9 us (12%)
  local copies, waits for them, and re-layouts  5.19 us (4%)
  between operations  1.74 us (1%)
  other arithmetic  1.25 us (1%)
    all_to_all x1, waiting for transfers between devices, on_device(): lax.all_to_all(galerkin.reshape(nsa * ngy, sub, rows, cols), ('sa', 'gy')...  20 us
    ppermute x7, starting transfers between devices, rotated(): return lax.ppermute(x, axis, [(i, (i + by) % count) for i in range(count)])  17.6 us
    all_to_all x1, blocking collectives, on_device(): lax.all_to_all(columns, 'gy', 0, 0, tiled=True).reshape(modes, length, cols)  13.9 us
    all_to_all x1, starting transfers between devices, on_device(): lax.all_to_all(outgoing, 'sa', 0, 0, tiled=True).reshape(p * rows, cols)  10.3 us
    pallas_call x1, Pallas kernels, inner_fluxes(): pl.pallas_call(functools.partial(inner_kernel, rows), out_shape=jax.Shape...  9.52 us
    pallas_call x1, Pallas kernels, node_tables(): pl.pallas_call(tables_kernel, grid=((q + pad) // QB,), in_specs=[pl.Block...  7.87 us
    all_to_all x1, starting transfers between devices, on_device(): lax.all_to_all(galerkin.reshape(nsa * ngy, sub, rows, cols), ('sa', 'gy')...  6.31 us
    all_to_all x1, waiting for transfers between devices, on_device(): lax.all_to_all(outgoing, 'sa', 0, 0, tiled=True).reshape(p * rows, cols)  5.73 us
  transfers between devices with their start and end apart: 10, of which 3 were waited for; matrix products, arithmetic and copies ran while one was open for 2% of the time, Pallas kernels for 15%

profile of v4, /device:TPU:32, one launch (start us, length us, event | category | flops | bytes accessed | tf_op | source)
XLA Modules:
  0.0 120.0 jit_solution(2697493927661130554)
XLA Ops:
  0.6 0.0 copy-start.8
  0.6 2.0 %copy_bitcast_fusion = f32[8,20,8,128]{3,2,1,0:T(8,128)} fusion(f32[20,64,128]{2,1,0:T(8,128)} %param.19), kind=kLoop, calls=%fused_computation.2 | loop fusion | bytes 1310720 | tf_op jit(solution)/shard_map/transpose | solution.py:487
  2.7 10.3 %all-to-all-start = ((f32[8,20,8,128]{3,2,1,0:T(8,128)}), f32[8,20,8,128]{3,2,1,0:T(8,128)S(1)}, u32[]{:S(2)}, u32[]{:S(2)}) async-start(f32[8,20,8,128]{3,2,1,0:T(8,128)} %copy_bitcast_fusion), calls=%async_computation | async-start | bytes 1310720 | tf_op jit(solution)/shard_map/all_to_all | solution.py:488
  13.0 0.0 copy-done.8
  13.0 0.7 dynamic-slice_bitcast_fusion
  13.8 1.5 %collective-permute-start = (f32[5,64,128]{2,1,0:T(8,128)}, f32[5,64,128]{2,1,0:T(8,128)S(1)}, u32[]{:S(2)}, u32[]{:S(2)}) collective-permute-start(f32[5,64,128]{2,1,0:T(8,128)} %get-tuple-element.32), channel_id=1, source_target_pairs={{0,8},{8,16},{16,24},{24,0},{1,9},{9,17},{17,25},{25,1},{2,10},{10... | collective-permute-start | bytes 491528 | tf_op jit(solution)/shard_map/ppermute | solution.py:473
  15.3 2.7 %collective-permute-start.1 = (f32[5,64,128]{2,1,0:T(8,128)S(1)}, f32[5,64,128]{2,1,0:T(8,128)S(1)}, u32[]{:S(2)}, u32[]{:S(2)}) collective-permute-start(f32[5,64,128]{2,1,0:T(8,128)S(1)} %get-tuple-element.31), channel_id=1, source_target_pairs={{0,16},{8,24},{16,0},{24,8},{1,17},{9,25},{17,1},{25,9},{2,18},{10... | collective-permute-start | bytes 491528 | tf_op jit(solution)/shard_map/ppermute | solution.py:473
  18.0 1.4 %collective-permute-start.2 = (f32[5,64,128]{2,1,0:T(8,128)S(1)}, f32[5,64,128]{2,1,0:T(8,128)S(1)}, u32[]{:S(2)}, u32[]{:S(2)}) collective-permute-start(f32[5,64,128]{2,1,0:T(8,128)S(1)} %get-tuple-element.30), channel_id=1, source_target_pairs={{0,24},{8,0},{16,8},{24,16},{1,25},{9,1},{17,9},{25,17},{2,26},{10... | collective-permute-start | bytes 491528 | tf_op jit(solution)/shard_map/ppermute | solution.py:473
  19.4 0.0 copy-done.10
  19.5 0.1 add_convert_fusion.open_ref
  19.6 0.0 copy-done.12
  19.6 0.1 copy.26.mode_ref
  19.7 0.0 copy-done.9
  19.7 0.0 copy-done.11
  19.7 7.9 %node_tables.1 = (bf16[1536,480]{1,0:T(8,128)(2,1)S(1)}, bf16[320,1536]{1,0:T(8,128)(2,1)S(1)}, bf16[1536,48]{1,0:T(8,128)(2,1)S(1)}, bf16[160,480]{1,0:T(8,128)(2,1)S(1)}) custom-call(s32[8,1536]{1,0:T(8,128)S(1)} %pad.13.index_ref, s32[160,8]{1,0:T(8,128)S(1)} %copy.26.mode_ref, f32[1,1536]{1,0:T(1,128)S(1)} %broadcast_in_dim.10.weight_ref), custom_call_target="tpu_custom_call" | custom-call | tf_op jit(solution)/shard_map/node_tables/pallas_call | solution.py:116
  27.6 0.0 copy-start
  27.6 1.2 copy-done
  28.8 0.0 collective-permute-done.s1_ref
  28.8 0.0 collective-permute-done.1.s2_ref
  28.8 0.0 collective-permute-done.2.s3_ref
  28.8 5.7 %all-to-all-done = f32[8,20,8,128]{3,2,1,0:T(8,128)S(1)} async-done(((f32[8,20,8,128]{3,2,1,0:T(8,128)}), f32[8,20,8,128]{3,2,1,0:T(8,128)S(1)}, u32[]{:S(2)}, u32[]{:S(2)}) %all-to-all-start) | async-done | bytes 655392 | tf_op jit(solution)/shard_map/all_to_all | solution.py:488
  34.6 0.5 rim_of.1
  35.0 0.1 collective-permute-start.5
  35.1 1.7 %collective-permute-start.6 = (f32[176,128]{1,0:T(8,128)S(1)}, f32[176,128]{1,0:T(8,128)S(1)}, u32[]{:S(2)}, u32[]{:S(2)}) collective-permute-start(f32[176,128]{1,0:T(8,128)S(1)} %get-tuple-element.23.near_ref), channel_id=1, source_target_pairs={{0,224},{32,0},{64,32},{96,64},{128,96},{160,128},{192,160},{224,1... | collective-permute-start | bytes 270344 | tf_op jit(solution)/shard_map/ppermute | solution.py:473
  36.9 0.2 collective-permute-start.3
  37.1 9.9 %collective-permute-start.4 = (f32[176,128]{1,0:T(8,128)S(1)}, f32[176,128]{1,0:T(8,128)S(1)}, u32[]{:S(2)}, u32[]{:S(2)}) collective-permute-start(f32[176,128]{1,0:T(8,128)S(1)} %get-tuple-element.21.first_ref), channel_id=1, source_target_pairs={{0,31},{1,0},{2,1},{3,2},{4,3},{5,4},{6,5},{7,6},{8,7},{9,8},{10,9... | collective-permute-start | bytes 270344 | tf_op jit(solution)/shard_map/ppermute | solution.py:473
  47.0 9.5 %inner_fluxes.1.g_ref = f32[8,160,128]{2,1,0:T(8,128)S(1)} custom-call(f32[1280,128]{1,0:T(8,128)S(1)} %bitcast.45, bf16[48,1024]{1,0:T(8,128)(2,1)S(1)} %pad_maximum_fusion.log_ref, bf16[1536,480]{1,0:T(8,128)(2,1)} %copy-done, bf16[1536,48]{1,0:T(8,128)(2,1)S(1)} %get-tuple-element.18.germ_ref, bf16[320,1536]{1,0:T(8,128)(2,1)S(1)} %get-tuple-element.19.w_ref, ...), custom_call_target="tpu_custom_call" | custom-call | flops 5662310400 | bytes 8388608 | tf_op jit(solution)/shard_map/inner_fluxes/pallas_call | solution.py:268
  56.5 0.0 copy-start.15
  56.6 0.0 copy-start.13
  56.6 0.0 copy-start.14
  56.6 0.0 copy-start.17
  56.6 0.0 collective-permute-done.3.up_ref
  56.6 0.0 collective-permute-done.4.down_ref
  56.6 0.0 collective-permute-done.5.left_ref
  56.6 0.0 collective-permute-done.6.right_ref
  56.6 5.3 %outer_fluxes.1 = f32[1280,128]{1,0:T(8,128)} custom-call(f32[4]{0:T(128)S(1)} %add_convert_fusion.open_ref, f32[8,160,128]{2,1,0:T(8,128)S(1)} %inner_fluxes.1.g_ref, f32[176,128]{1,0:T(8,128)S(1)} %get-tuple-element.21.first_ref, f32[176,128]{1,0:T(8,128)S(1)} %get-tuple-element.22.last_ref, f32[176,128]{1,0:T(8,128)S(1)} %get-tuple-element.23.near_ref, ...), custom_call_target="tpu_custom_call" | custom-call | flops 1132462080 | bytes 8388608 | tf_op jit(solution)/shard_map/outer_fluxes/pallas_call | solution.py:359
  62.0 0.0 copy-start.5
  62.0 6.3 %all-to-all-start.1 = ((f32[32,5,8,128]{3,2,1,0:T(8,128)}), f32[32,5,8,128]{3,2,1,0:T(8,128)S(1)}, u32[]{:S(2)}, u32[]{:S(2)}) async-start(f32[32,5,8,128]{3,2,1,0:T(8,128)} %bitcast.15), calls=%async_computation.1 | async-start | bytes 1310720 | tf_op jit(solution)/shard_map/all_to_all | solution.py:521
  68.3 0.0 copy-done.15
  69.0 0.0 copy-done.13
  69.0 0.0 copy-done.14
  69.1 0.4 fusion.1
  69.4 0.0 copy-done.16
  69.5 0.4 fusion.2
  69.8 0.0 copy-start.4
  69.9 0.2 convolution_bitcast_fusion
  70.1 0.2 convolution_bitcast_fusion.1
  70.3 0.1 add_divide_fusion.recip_ref
  70.4 20.0 %all-to-all-done.1.part_ref = f32[32,5,8,128]{3,2,1,0:T(8,128)S(1)} async-done(((f32[32,5,8,128]{3,2,1,0:T(8,128)}), f32[32,5,8,128]{3,2,1,0:T(8,128)S(1)}, u32[]{:S(2)}, u32[]{:S(2)}) %all-to-all-start.1) | async-done | bytes 655392 | tf_op jit(solution)/shard_map/all_to_all | solution.py:521
  90.4 0.0 copy-start.1
  90.4 3.6 %local_solve.1 = (f32[1280,128]{1,0:T(8,128)S(1)}, f32[8,16,256]{2,1,0:T(8,128)}) custom-call(s32[1]{0:T(128)} %bitcast.place_ref, f32[32,5,8,128]{3,2,1,0:T(8,128)S(1)} %all-to-all-done.1.part_ref, f32[5,64,128]{2,1,0:T(8,128)S(1)} %get-tuple-element.24.s0_ref, f32[5,64,128]{2,1,0:T(8,128)S(1)} %collective-permute-done.s1_ref, ...), custom_call_target="tpu_custom_call" | custom-call | tf_op jit(solution)/shard_map/local_solve/pallas_call | solution.py:532
  94.0 3.3 %all-to-all-start.2 = ((f32[8,16,256]{2,1,0:T(8,128)}), f32[8,16,256]{2,1,0:T(8,128)S(1)}, u32[]{:S(2)}, u32[]{:S(2)}) async-start(f32[8,16,256]{2,1,0:T(8,128)} %get-tuple-element.29), calls=%async_computation.2 | async-start | bytes 262144 | tf_op jit(solution)/shard_map/all_to_all | solution.py:543
  97.3 0.1 copy.27.g_first_ref
  97.4 0.1 copy.28.g_last_ref
  97.5 0.0 copy-done.4
  97.5 0.7 back.1.z_ref
  98.2 0.0 copy-start.6
  98.2 0.0 copy-start.7
  98.2 4.7 %all-to-all-done.2.jump_ref = f32[8,16,256]{2,1,0:T(8,128)S(1)} async-done(((f32[8,16,256]{2,1,0:T(8,128)}), f32[8,16,256]{2,1,0:T(8,128)S(1)}, u32[]{:S(2)}, u32[]{:S(2)}) %all-to-all-start.2) | async-done | bytes 131104 | tf_op jit(solution)/shard_map/all_to_all | solution.py:543
  103.0 1.3 %joined_solve.1 = f32[4,5,64,128]{3,2,1,0:T(8,128)S(1)} custom-call(f32[1280,128]{1,0:T(8,128)S(1)} %back.1.z_ref, f32[8,16,256]{2,1,0:T(8,128)S(1)} %all-to-all-done.2.jump_ref, f32[256,128]{1,0:T(8,128)S(1)} %copy.27.g_first_ref, f32[256,128]{1,0:T(8,128)S(1)} %copy.28.g_last_ref, f32[256,256]{1,0:T(8,128)S(1)} %copy-done.1), custom_call_target="tpu_custom_call" | custom-call | tf_op jit(solution)/shard_map/joined_solve/pallas_call | solution.py:553
  104.2 13.9 %all_to_all.20 = f32[4,5,64,128]{3,2,1,0:T(8,128)S(1)} all-to-all(f32[4,5,64,128]{3,2,1,0:T(8,128)S(1)} %joined_solve.1), channel_id=1, replica_groups=mesh['gx'=8,'gy'=4,'sa'=8] {'gy'}, dimensions={0} | all-to-all | bytes 1310720 | tf_op jit(solution)/shard_map/all_to_all | solution.py:559
  118.1 0.0 copy-done.6
  118.1 1.0 multiply_add_fusion
  119.1 0.8 copy.35
  (25 shorter events, 0.1 us)
Async XLA Ops:
  0.6 12.4 %copy-start.8 = (f32[20,64,128]{2,1,0:T(8,128)S(1)}, f32[20,64,128]{2,1,0:T(8,128)}, u32[]{:S(2)}) copy-start(f32[20,64,128]{2,1,0:T(8,128)} %param.21) | copy-start | bytes 1966084
  2.7 16.8 %copy-start.10 = (f32[9,8,128]{2,1,0:T(8,128)S(1)}, f32[9,8,128]{2,1,0:T(8,128)}, u32[]{:S(2)}) copy-start(f32[9,8,128]{2,1,0:T(8,128)} %param.22) | copy-start | bytes 110596
  2.7 16.9 %copy-start.12 = (s32[160,8]{0,1:T(8,128)S(1)}, s32[160,8]{0,1:T(8,128)}, u32[]{:S(2)}) copy-start(s32[160,8]{0,1:T(8,128)} %param.26) | copy-start | bytes 15364
  2.7 17.0 %copy-start.9 = (s32[1500,8]{0,1:T(8,128)S(1)}, s32[1500,8]{0,1:T(8,128)}, u32[]{:S(2)}) copy-start(s32[1500,8]{0,1:T(8,128)} %param.25) | copy-start | bytes 144004
  2.7 17.0 %copy-start.11 = (f32[1500]{0:T(1024)S(1)}, f32[1500]{0:T(1024)}, u32[]{:S(2)}) copy-start(f32[1500]{0:T(1024)} %param.23) | copy-start | bytes 18004
  2.7 31.9 %all-to-all-start = ((f32[8,20,8,128]{3,2,1,0:T(8,128)}), f32[8,20,8,128]{3,2,1,0:T(8,128)S(1)}, u32[]{:S(2)}, u32[]{:S(2)}) async-start(f32[8,20,8,128]{3,2,1,0:T(8,128)} %copy_bitcast_fusion), calls=%async_computation | async-start | bytes 1310720 | tf_op jit(solution)/shard_map/all_to_all | solution.py:488
  13.8 15.0 %collective-permute-start = (f32[5,64,128]{2,1,0:T(8,128)}, f32[5,64,128]{2,1,0:T(8,128)S(1)}, u32[]{:S(2)}, u32[]{:S(2)}) collective-permute-start(f32[5,64,128]{2,1,0:T(8,128)} %get-tuple-element.32), channel_id=1, source_target_pairs={{0,8},{8,16},{16,24},{24,0},{1,9},{9,17},{17,25},{25,1},{2,10},{10... | collective-permute-start | bytes 491528 | tf_op jit(solution)/shard_map/ppermute | solution.py:473
  15.3 13.6 %collective-permute-start.1 = (f32[5,64,128]{2,1,0:T(8,128)S(1)}, f32[5,64,128]{2,1,0:T(8,128)S(1)}, u32[]{:S(2)}, u32[]{:S(2)}) collective-permute-start(f32[5,64,128]{2,1,0:T(8,128)S(1)} %get-tuple-element.31), channel_id=1, source_target_pairs={{0,16},{8,24},{16,0},{24,8},{1,17},{9,25},{17,1},{25,9},{2,18},{10... | collective-permute-start | bytes 491528 | tf_op jit(solution)/shard_map/ppermute | solution.py:473
  18.0 10.8 %collective-permute-start.2 = (f32[5,64,128]{2,1,0:T(8,128)S(1)}, f32[5,64,128]{2,1,0:T(8,128)S(1)}, u32[]{:S(2)}, u32[]{:S(2)}) collective-permute-start(f32[5,64,128]{2,1,0:T(8,128)S(1)} %get-tuple-element.30), channel_id=1, source_target_pairs={{0,24},{8,0},{16,8},{24,16},{1,25},{9,1},{17,9},{25,17},{2,26},{10... | collective-permute-start | bytes 491528 | tf_op jit(solution)/shard_map/ppermute | solution.py:473
  27.6 1.2 copy-start
  35.0 21.6 %collective-permute-start.5 = (f32[176,128]{1,0:T(8,128)S(1)}, f32[176,128]{1,0:T(8,128)S(1)}, u32[]{:S(2)}, u32[]{:S(2)}) collective-permute-start(f32[176,128]{1,0:T(8,128)S(1)} %get-tuple-element.23.near_ref), channel_id=1, source_target_pairs={{0,32},{32,64},{64,96},{96,128},{128,160},{160,192},{192,224},{224... | collective-permute-start | bytes 270344 | tf_op jit(solution)/shard_map/ppermute | solution.py:473
  35.1 21.5 %collective-permute-start.6 = (f32[176,128]{1,0:T(8,128)S(1)}, f32[176,128]{1,0:T(8,128)S(1)}, u32[]{:S(2)}, u32[]{:S(2)}) collective-permute-start(f32[176,128]{1,0:T(8,128)S(1)} %get-tuple-element.23.near_ref), channel_id=1, source_target_pairs={{0,224},{32,0},{64,32},{96,64},{128,96},{160,128},{192,160},{224,1... | collective-permute-start | bytes 270344 | tf_op jit(solution)/shard_map/ppermute | solution.py:473
  36.9 19.7 %collective-permute-start.3 = (f32[176,128]{1,0:T(8,128)S(1)}, f32[176,128]{1,0:T(8,128)S(1)}, u32[]{:S(2)}, u32[]{:S(2)}) collective-permute-start(f32[176,128]{1,0:T(8,128)S(1)} %get-tuple-element.22.last_ref), channel_id=1, source_target_pairs={{0,1},{1,2},{2,3},{3,4},{4,5},{5,6},{6,7},{7,8},{8,9},{9,10},{10,1... | collective-permute-start | bytes 270344 | tf_op jit(solution)/shard_map/ppermute | solution.py:473
  37.1 19.5 %collective-permute-start.4 = (f32[176,128]{1,0:T(8,128)S(1)}, f32[176,128]{1,0:T(8,128)S(1)}, u32[]{:S(2)}, u32[]{:S(2)}) collective-permute-start(f32[176,128]{1,0:T(8,128)S(1)} %get-tuple-element.21.first_ref), channel_id=1, source_target_pairs={{0,31},{1,0},{2,1},{3,2},{4,3},{5,4},{6,5},{7,6},{8,7},{9,8},{10,9... | collective-permute-start | bytes 270344 | tf_op jit(solution)/shard_map/ppermute | solution.py:473
  56.5 11.8 %copy-start.15 = (f32[9,7]{1,0:T(8,128)S(1)}, f32[9,7]{1,0:T(8,128)}, u32[]{:S(2)}) copy-start(f32[9,7]{1,0:T(8,128)} %constant.106.clone) | copy-start | bytes 760
  56.6 12.5 %copy-start.13 = (f32[256]{0:T(256)S(1)}, f32[256]{0:T(256)}, u32[]{:S(2)}) copy-start(f32[256]{0:T(256)} %constant.101.clone) | copy-start | bytes 3076
  56.6 12.5 %copy-start.14 = (f32[128]{0:T(128)S(1)}, f32[128]{0:T(128)}, u32[]{:S(2)}) copy-start(f32[128]{0:T(128)} %constant.102.clone) | copy-start | bytes 1540
  56.6 12.5 %copy-start.17 = (f32[128,128]{1,0:T(8,128)S(1)}, f32[128,128]{1,0:T(8,128)}, u32[]{:S(2)}) copy-start(f32[128,128]{1,0:T(8,128)} %constant.104.clone) | copy-start | bytes 196612
  62.0 7.5 %copy-start.16 = (f32[128,128]{1,0:T(8,128)S(1)}, f32[128,128]{1,0:T(8,128)}, u32[]{:S(2)}) copy-start(f32[128,128]{1,0:T(8,128)} %constant.103.clone) | copy-start | bytes 196612
  62.0 7.9 %copy-start.18 = (f32[7]{0:T(128)S(1)}, f32[7]{0:T(128)}, u32[]{:S(2)}) copy-start(f32[7]{0:T(128)} %constant.105.clone) | copy-start | bytes 88
  62.0 28.4 %copy-start.2 = (f32[256,256]{1,0:T(8,128)S(1)}, f32[256,256]{1,0:T(8,128)}, u32[]{:S(2)}) copy-start(f32[256,256]{1,0:T(8,128)} %constant.107.clone.cy_ref) | copy-start | bytes 786436
  62.0 28.4 %copy-start.3 = (f32[128,128]{1,0:T(8,128)S(1)}, f32[128,128]{1,0:T(8,128)}, u32[]{:S(2)}) copy-start(f32[128,128]{1,0:T(8,128)} %constant.108.clone.cxt_ref) | copy-start | bytes 196612
  62.0 28.4 %copy-start.5 = (f32[8,128]{1,0:T(8,128)S(1)}, f32[8,128]{1,0:T(8,128)}, u32[]{:S(2)}) copy-start(f32[8,128]{1,0:T(8,128)} %constant.109.clone.ends_of_ref) | copy-start | bytes 12292
  62.0 28.4 %all-to-all-start.1 = ((f32[32,5,8,128]{3,2,1,0:T(8,128)}), f32[32,5,8,128]{3,2,1,0:T(8,128)S(1)}, u32[]{:S(2)}, u32[]{:S(2)}) async-start(f32[32,5,8,128]{3,2,1,0:T(8,128)} %bitcast.15), calls=%async_computation.1 | async-start | bytes 1310720 | tf_op jit(solution)/shard_map/all_to_all | solution.py:521
  69.8 27.7 %copy-start.4 = (f32[128,128]{1,0:T(8,128)S(1)}, f32[128,128]{1,0:T(8,128)}, u32[]{:S(2)}) copy-start(f32[128,128]{1,0:T(8,128)} %constant.110.clone.cx_ref) | copy-start | bytes 196612
  90.4 12.6 %copy-start.1 = (f32[256,256]{1,0:T(8,128)S(1)}, f32[256,256]{1,0:T(8,128)}, u32[]{:S(2)}) copy-start(f32[256,256]{1,0:T(8,128)} %constant.111.clone.cyt_ref) | copy-start | bytes 786436
  94.0 9.0 %all-to-all-start.2 = ((f32[8,16,256]{2,1,0:T(8,128)}), f32[8,16,256]{2,1,0:T(8,128)S(1)}, u32[]{:S(2)}, u32[]{:S(2)}) async-start(f32[8,16,256]{2,1,0:T(8,128)} %get-tuple-element.29), calls=%async_computation.2 | async-start | bytes 262144 | tf_op jit(solution)/shard_map/all_to_all | solution.py:543
  98.2 19.9 %copy-start.6 = (f32[20,64,128]{2,1,0:T(8,128)S(1)}, f32[20,64,128]{2,1,0:T(8,128)}, u32[]{:S(2)}) copy-start(f32[20,64,128]{2,1,0:T(8,128)} %param.19) | copy-start | bytes 1966084
  98.2 19.9 %copy-start.7 = (f32[20,64,128]{2,1,0:T(8,128)S(1)}, f32[20,64,128]{2,1,0:T(8,128)}, u32[]{:S(2)}) copy-start(f32[20,64,128]{2,1,0:T(8,128)} %param.20) | copy-start | bytes 1966084

commit v5 on v4

--- a/solution.py
+++ b/solution.py
@@ -383,11 +383,11 @@
     ny = ngy * length
     for d, src_ref in enumerate((s0_ref, s1_ref, s2_ref, s3_ref)):
         g = lax.rem(place_ref[0] + ngy - d, ngy)
-        for s in range(nsa):
-            span = pl.ds(pl.multiple_of(g * length + s * rows, 8), rows)
+        for s, block in enumerate(row_order(nsa)):
+            span = pl.ds(pl.multiple_of(g * length + block * rows, 8), rows)
             for m in range(modes):
                 res_ref[span, pl.ds(m * cols, cols)] = (
-                    src_ref[m, pl.ds(s * rows, rows), :] - part_ref[s * ngy + g, m]
+                    src_ref[m, pl.ds(block * rows, rows), :] - part_ref[s * ngy + g, m]
                 )
     spectral = jnp.dot(cy_ref[...], res_ref[...], precision=HIGHEST, preferred_element_type=jnp.float32)
     spectral = jnp.concatenate([spectral[:, m * cols : (m + 1) * cols] for m in range(modes)], axis=0)
@@ -468,6 +468,11 @@
     return recip, g_first, g_last, jnp.stack(coef)
 
 
+def row_order(count):
+    half = count // 2
+    return list(range(half)) + list(range(count - 1, half - 1, -1))
+
+
 def rotated(x, axis, by):
     count = lax.axis_size(axis)
     return lax.ppermute(x, axis, [(i, (i + by) % count) for i in range(count)])
@@ -484,7 +489,9 @@
     sub = modes // ngy
     fields = log_fields.shape[0]
 
-    outgoing = field_now.reshape(modes, nsa, rows, cols).transpose(1, 0, 2, 3)
+    order = row_order(nsa)
+    parts = field_now.reshape(modes, nsa, rows, cols)
+    outgoing = jnp.stack([parts[:, block] for block in order])
     field = lax.all_to_all(outgoing, "sa", 0, 0, tiled=True).reshape(p * rows, cols)
 
     place = lax.axis_index("gy")
@@ -496,7 +503,13 @@
     recip, g_first, g_last, coef = solve_tables(mean_perm, ny, cols, ngx, lax.axis_index("gx"))
 
     row_axis = ("gy", "sa")
-    row_index = lax.axis_index(row_axis)
+    member = lax.axis_index("sa")
+    row_index = place * nsa + jnp.where(member < nsa // 2, member, nsa - 1 - (member - nsa // 2))
+    log_fields = lax.ppermute(
+        log_fields, row_axis, [(g * nsa + order[i], g * nsa + i) for g in range(ngy) for i in range(nsa)]
+    )
+    chain = [g * nsa + order.index(k) for g in range(ngy) for k in range(nsa)]
+    ring = [(a, b) for a, b in zip(chain, chain[1:] + chain[:1])]
     col_index = lax.axis_index("gx")
     opened = jnp.stack(
         [row_index > 0, row_index < ngy * nsa - 1, col_index > 0, col_index < ngx - 1]
@@ -511,8 +524,8 @@
     rims = rim_of(rows, field, scaled_logs.reshape(SLOT * rows, cols))
     first, last, near = rims
     halos = (
-        rotated(last, row_axis, 1),
-        rotated(first, row_axis, -1),
+        lax.ppermute(last, row_axis, ring),
+        lax.ppermute(first, row_axis, [(b, a) for a, b in ring]),
         rotated(near, "gx", 1),
         rotated(near, "gx", -1),
     )

time: 120 us -> 128 us (1.067)
  local copies, waits for them, and re-layouts: 5.19 us -> 15.5 us
  starting transfers between devices: 37.6 us -> 34.9 us
    unnamed x40 -> x47, local copies, waits for them, and re-layouts: 2.21 us -> 13 us
    ppermute x7 -> x5, starting transfers between devices: 17.6 us -> 7.47 us  [rotated(): return lax.ppermute(x, axis, [(i, (i + by) % count) for i in range(count)])]
    ppermute x0 -> x3, starting transfers between devices: none -> 8.7 us  [the longest x1 7.81 us: on_device(): lax.ppermute(first, row_axis, [(b, a) for a, b in ring])]
    transpose x1 -> x0, local copies, waits for them, and re-layouts: 2.04 us -> none  [on_device(): outgoing = field_now.reshape(modes, nsa, rows, cols).transpose(1, 0, 2, 3)]
    all_to_all x1, starting transfers between devices: 6.31 us -> 4.76 us  [on_device(): lax.all_to_all(galerkin.reshape(nsa * ngy, sub, rows, cols), ('sa', 'gy')...]
    another operation x0 -> x1, local copies, waits for them, and re-layouts: none -> 1.54 us  [on_device(): outgoing = jnp.stack([parts[:, block] for block in order])]
  transfers between devices with their start and end apart: 10 -> 11, of which waited for: 3 -> 3; matrix products, arithmetic and copies ran while one was open for 2% -> 2% of each run, Pallas kernels for 15% -> 14%
where the time goes in v5:
time: 128 us; the launch traced here: 127 us
  starting transfers between devices  34.9 us (27%)
  waiting for transfers between devices  30.2 us (24%)
  Pallas kernels  28.7 us (22%)
  local copies, waits for them, and re-layouts  15.5 us (12%)
  blocking collectives  13.5 us (11%)
  between operations  1.77 us (1%)
    all_to_all x1, waiting for transfers between devices, on_device(): lax.all_to_all(galerkin.reshape(nsa * ngy, sub, rows, cols), ('sa', 'gy')...  20.4 us
    all_to_all x1, blocking collectives, on_device(): lax.all_to_all(columns, 'gy', 0, 0, tiled=True).reshape(modes, length, cols)  13.5 us
    unnamed x47, local copies, waits for them, and re-layouts  13 us
    all_to_all x1, starting transfers between devices, on_device(): lax.all_to_all(outgoing, 'sa', 0, 0, tiled=True).reshape(p * rows, cols)  10.2 us
    pallas_call x1, Pallas kernels, inner_fluxes(): pl.pallas_call(functools.partial(inner_kernel, rows), out_shape=jax.Shape...  9.52 us
    pallas_call x1, Pallas kernels, node_tables(): pl.pallas_call(tables_kernel, grid=((q + pad) // QB,), in_specs=[pl.Block...  7.87 us
    ppermute x1, starting transfers between devices, on_device(): lax.ppermute(first, row_axis, [(b, a) for a, b in ring])  7.81 us
    ppermute x5, starting transfers between devices, rotated(): return lax.ppermute(x, axis, [(i, (i + by) % count) for i in range(count)])  7.47 us
  transfers between devices with their start and end apart: 11, of which 3 were waited for; matrix products, arithmetic and copies ran while one was open for 2% of the time, Pallas kernels for 14%

profile of v5, /device:TPU:32, one launch (start us, length us, event | category | flops | bytes accessed | tf_op | source)
XLA Modules:
  0.0 127.0 jit_solution(5325927745343309265)
XLA Ops:
  0.6 0.0 copy-start.8
  0.6 1.6 %fusion.7 = f32[8,20,8,128]{3,2,1,0:T(8,128)} fusion(f32[20,8,8,128]{3,2,1,0:T(8,128)} %bitcast.91), kind=kLoop, calls=%fused_computation.26 | loop fusion | bytes 163840
  2.2 1.5 %fusion.6 = f32[8,20,8,128]{3,2,1,0:T(8,128)} fusion(f32[8,20,8,128]{3,2,1,0:T(8,128)} %fusion.7, f32[20,8,8,128]{3,2,1,0:T(8,128)} %bitcast.92), kind=kLoop, calls=%fused_computation.24 | loop fusion | bytes 163840
  3.8 1.5 %fusion.5 = f32[8,20,8,128]{3,2,1,0:T(8,128)} fusion(f32[8,20,8,128]{3,2,1,0:T(8,128)} %fusion.6, f32[20,8,8,128]{3,2,1,0:T(8,128)} %bitcast.93), kind=kLoop, calls=%fused_computation.22 | loop fusion | bytes 163840
  5.3 1.5 %fusion.4 = f32[8,20,8,128]{3,2,1,0:T(8,128)} fusion(f32[8,20,8,128]{3,2,1,0:T(8,128)} %fusion.5, f32[20,8,8,128]{3,2,1,0:T(8,128)} %bitcast.94), kind=kLoop, calls=%fused_computation.20 | loop fusion | bytes 163840
  6.8 1.5 %fusion.3 = f32[8,20,8,128]{3,2,1,0:T(8,128)} fusion(f32[8,20,8,128]{3,2,1,0:T(8,128)} %fusion.4, f32[20,8,8,128]{3,2,1,0:T(8,128)} %bitcast.95), kind=kLoop, calls=%fused_computation.18 | loop fusion | bytes 163840
  8.3 1.5 %fusion.2 = f32[8,20,8,128]{3,2,1,0:T(8,128)} fusion(f32[8,20,8,128]{3,2,1,0:T(8,128)} %fusion.3, f32[20,8,8,128]{3,2,1,0:T(8,128)} %bitcast.96), kind=kLoop, calls=%fused_computation.16 | loop fusion | bytes 163840
  9.9 1.5 %fusion.1 = f32[8,20,8,128]{3,2,1,0:T(8,128)} fusion(f32[8,20,8,128]{3,2,1,0:T(8,128)} %fusion.2, f32[20,8,8,128]{3,2,1,0:T(8,128)} %bitcast.97), kind=kLoop, calls=%fused_computation.14 | loop fusion | bytes 163840
  11.4 1.5 %fusion = f32[8,20,8,128]{3,2,1,0:T(8,128)} fusion(f32[8,20,8,128]{3,2,1,0:T(8,128)} %fusion.1, f32[20,8,8,128]{3,2,1,0:T(8,128)} %bitcast.98), kind=kLoop, calls=%fused_computation.12 | loop fusion | bytes 163840 | tf_op jit(solution)/shard_map/stack | solution.py:494
  13.0 10.2 %all-to-all-start = ((f32[8,20,8,128]{3,2,1,0:T(8,128)}), f32[8,20,8,128]{3,2,1,0:T(8,128)S(1)}, u32[]{:S(2)}, u32[]{:S(2)}) async-start(f32[8,20,8,128]{3,2,1,0:T(8,128)} %fusion), calls=%async_computation | async-start | bytes 1310720 | tf_op jit(solution)/shard_map/all_to_all | solution.py:495
  23.1 0.0 copy-done.8
  23.2 0.7 dynamic-slice_bitcast_fusion
  23.9 1.5 %collective-permute-start = (f32[5,64,128]{2,1,0:T(8,128)}, f32[5,64,128]{2,1,0:T(8,128)S(1)}, u32[]{:S(2)}, u32[]{:S(2)}) collective-permute-start(f32[5,64,128]{2,1,0:T(8,128)} %get-tuple-element.32), channel_id=1, source_target_pairs={{0,8},{8,16},{16,24},{24,0},{1,9},{9,17},{17,25},{25,1},{2,10},{10... | collective-permute-start | bytes 491528 | tf_op jit(solution)/shard_map/ppermute | solution.py:478
  25.4 2.7 %collective-permute-start.1 = (f32[5,64,128]{2,1,0:T(8,128)S(1)}, f32[5,64,128]{2,1,0:T(8,128)S(1)}, u32[]{:S(2)}, u32[]{:S(2)}) collective-permute-start(f32[5,64,128]{2,1,0:T(8,128)S(1)} %get-tuple-element.31), channel_id=1, source_target_pairs={{0,16},{8,24},{16,0},{24,8},{1,17},{9,25},{17,1},{25,9},{2,18},{10... | collective-permute-start | bytes 491528 | tf_op jit(solution)/shard_map/ppermute | solution.py:478
  28.1 1.4 %collective-permute-start.2 = (f32[5,64,128]{2,1,0:T(8,128)S(1)}, f32[5,64,128]{2,1,0:T(8,128)S(1)}, u32[]{:S(2)}, u32[]{:S(2)}) collective-permute-start(f32[5,64,128]{2,1,0:T(8,128)S(1)} %get-tuple-element.30), channel_id=1, source_target_pairs={{0,24},{8,0},{16,8},{24,16},{1,25},{9,1},{17,9},{25,17},{2,26},{10... | collective-permute-start | bytes 491528 | tf_op jit(solution)/shard_map/ppermute | solution.py:478
  29.5 0.0 copy-done.15
  29.5 0.7 collective-permute-start.3
  30.2 0.1 add_convert_fusion.open_ref
  30.3 0.0 copy-done.11
  30.3 0.1 copy.40.mode_ref
  30.5 7.9 %node_tables.1 = (bf16[1536,480]{1,0:T(8,128)(2,1)S(1)}, bf16[320,1536]{1,0:T(8,128)(2,1)S(1)}, bf16[1536,48]{1,0:T(8,128)(2,1)S(1)}, bf16[160,480]{1,0:T(8,128)(2,1)S(1)}) custom-call(s32[8,1536]{1,0:T(8,128)S(1)} %pad.13.index_ref, s32[160,8]{1,0:T(8,128)S(1)} %copy.40.mode_ref, f32[1,1536]{1,0:T(1,128)S(1)} %broadcast_in_dim.10.weight_ref), custom_call_target="tpu_custom_call" | custom-call | tf_op jit(solution)/shard_map/node_tables/pallas_call | solution.py:116
  38.4 1.2 copy-done
  39.5 0.0 collective-permute-done.3
  39.6 0.0 collective-permute-done.s1_ref
  39.6 0.0 collective-permute-done.1.s2_ref
  39.6 0.0 collective-permute-done.2.s3_ref
  39.6 5.0 %all-to-all-done = f32[8,20,8,128]{3,2,1,0:T(8,128)S(1)} async-done(((f32[8,20,8,128]{3,2,1,0:T(8,128)}), f32[8,20,8,128]{3,2,1,0:T(8,128)S(1)}, u32[]{:S(2)}, u32[]{:S(2)}) %all-to-all-start) | async-done | bytes 655392 | tf_op jit(solution)/shard_map/all_to_all | solution.py:495
  44.7 0.5 rim_of.1
  45.2 0.1 collective-permute-start.6
  45.3 1.7 %collective-permute-start.7 = (f32[176,128]{1,0:T(8,128)S(1)}, f32[176,128]{1,0:T(8,128)S(1)}, u32[]{:S(2)}, u32[]{:S(2)}) collective-permute-start(f32[176,128]{1,0:T(8,128)S(1)} %get-tuple-element.23.near_ref), channel_id=1, source_target_pairs={{0,224},{32,0},{64,32},{96,64},{128,96},{160,128},{192,160},{224,1... | collective-permute-start | bytes 270344 | tf_op jit(solution)/shard_map/ppermute | solution.py:478
  47.0 0.2 collective-permute-start.4
  47.2 7.8 %collective-permute-start.5 = (f32[176,128]{1,0:T(8,128)S(1)}, f32[176,128]{1,0:T(8,128)S(1)}, u32[]{:S(2)}, u32[]{:S(2)}) collective-permute-start(f32[176,128]{1,0:T(8,128)S(1)} %get-tuple-element.21.first_ref), channel_id=1, source_target_pairs={{1,0},{2,1},{3,2},{7,3},{6,7},{5,6},{4,5},{8,4},{9,8},{10,9},{11,1... | collective-permute-start | bytes 270344 | tf_op jit(solution)/shard_map/ppermute | solution.py:528
  55.0 9.5 %inner_fluxes.1.g_ref = f32[8,160,128]{2,1,0:T(8,128)S(1)} custom-call(f32[1280,128]{1,0:T(8,128)S(1)} %bitcast.89, bf16[48,1024]{1,0:T(8,128)(2,1)S(1)} %pad_maximum_fusion.log_ref, bf16[1536,480]{1,0:T(8,128)(2,1)} %copy-done, bf16[1536,48]{1,0:T(8,128)(2,1)S(1)} %get-tuple-element.18.germ_ref, bf16[320,1536]{1,0:T(8,128)(2,1)S(1)} %get-tuple-element.19.w_ref, ...), custom_call_target="tpu_custom_call" | custom-call | flops 5662310400 | bytes 8388608 | tf_op jit(solution)/shard_map/inner_fluxes/pallas_call | solution.py:268
  64.6 0.0 copy-start.14
  64.6 0.0 copy-start.12
  64.6 0.0 copy-start.13
  64.6 0.0 copy-start.17
  64.6 0.0 collective-permute-done.4.up_ref
  64.6 0.0 collective-permute-done.5.down_ref
  64.6 0.0 collective-permute-done.6.left_ref
  64.6 0.0 collective-permute-done.7.right_ref
  64.6 5.3 %outer_fluxes.1 = f32[1280,128]{1,0:T(8,128)} custom-call(f32[4]{0:T(128)S(1)} %add_convert_fusion.open_ref, f32[8,160,128]{2,1,0:T(8,128)S(1)} %inner_fluxes.1.g_ref, f32[176,128]{1,0:T(8,128)S(1)} %get-tuple-element.21.first_ref, f32[176,128]{1,0:T(8,128)S(1)} %get-tuple-element.22.last_ref, f32[176,128]{1,0:T(8,128)S(1)} %get-tuple-element.23.near_ref, ...), custom_call_target="tpu_custom_call" | custom-call | flops 1132462080 | bytes 8388608 | tf_op jit(solution)/shard_map/outer_fluxes/pallas_call | solution.py:359
  70.0 0.0 copy-start.5
  70.0 4.8 %all-to-all-start.1 = ((f32[32,5,8,128]{3,2,1,0:T(8,128)}), f32[32,5,8,128]{3,2,1,0:T(8,128)S(1)}, u32[]{:S(2)}, u32[]{:S(2)}) async-start(f32[32,5,8,128]{3,2,1,0:T(8,128)} %bitcast.22), calls=%async_computation.1 | async-start | bytes 1310720 | tf_op jit(solution)/shard_map/all_to_all | solution.py:534
  75.5 0.4 fusion.10
  75.9 0.4 fusion.9
  76.3 0.0 copy-start.4
  76.3 0.2 convolution_bitcast_fusion
  76.5 0.2 convolution_bitcast_fusion.1
  76.8 0.1 add_divide_fusion.recip_ref
  76.9 20.4 %all-to-all-done.1.part_ref = f32[32,5,8,128]{3,2,1,0:T(8,128)S(1)} async-done(((f32[32,5,8,128]{3,2,1,0:T(8,128)}), f32[32,5,8,128]{3,2,1,0:T(8,128)S(1)}, u32[]{:S(2)}, u32[]{:S(2)}) %all-to-all-start.1) | async-done | bytes 655392 | tf_op jit(solution)/shard_map/all_to_all | solution.py:534
  97.3 0.0 copy-start.1
  97.3 3.6 %local_solve.1 = (f32[1280,128]{1,0:T(8,128)S(1)}, f32[8,16,256]{2,1,0:T(8,128)}) custom-call(s32[1]{0:T(128)} %bitcast.place_ref, f32[32,5,8,128]{3,2,1,0:T(8,128)S(1)} %all-to-all-done.1.part_ref, f32[5,64,128]{2,1,0:T(8,128)S(1)} %get-tuple-element.24.s0_ref, f32[5,64,128]{2,1,0:T(8,128)S(1)} %collective-permute-done.s1_ref, ...), custom_call_target="tpu_custom_call" | custom-call | tf_op jit(solution)/shard_map/local_solve/pallas_call | solution.py:545
  100.8 3.8 %all-to-all-start.2 = ((f32[8,16,256]{2,1,0:T(8,128)}), f32[8,16,256]{2,1,0:T(8,128)S(1)}, u32[]{:S(2)}, u32[]{:S(2)}) async-start(f32[8,16,256]{2,1,0:T(8,128)} %get-tuple-element.29), calls=%async_computation.2 | async-start | bytes 262144 | tf_op jit(solution)/shard_map/all_to_all | solution.py:556
  104.7 0.1 copy.41.g_first_ref
  104.8 0.1 copy.42.g_last_ref
  104.9 0.7 back.1.z_ref
  105.6 0.0 copy-start.6
  105.6 0.0 copy-start.7
  105.6 4.8 %all-to-all-done.2.jump_ref = f32[8,16,256]{2,1,0:T(8,128)S(1)} async-done(((f32[8,16,256]{2,1,0:T(8,128)}), f32[8,16,256]{2,1,0:T(8,128)S(1)}, u32[]{:S(2)}, u32[]{:S(2)}) %all-to-all-start.2) | async-done | bytes 131104 | tf_op jit(solution)/shard_map/all_to_all | solution.py:556
  110.4 1.3 joined_solve.1
  111.6 13.5 %all_to_all.20 = f32[4,5,64,128]{3,2,1,0:T(8,128)S(1)} all-to-all(f32[4,5,64,128]{3,2,1,0:T(8,128)S(1)} %joined_solve.1), channel_id=1, replica_groups=mesh['gx'=8,'gy'=4,'sa'=8] {'gy'}, dimensions={0} | all-to-all | bytes 1310720 | tf_op jit(solution)/shard_map/all_to_all | solution.py:572
  125.1 1.0 multiply_add_fusion
  126.1 0.8 copy.63
  (34 shorter events, 0.1 us)
Async XLA Ops:
  0.6 22.5 %copy-start.8 = (f32[20,64,128]{2,1,0:T(8,128)S(1)}, f32[20,64,128]{2,1,0:T(8,128)}, u32[]{:S(2)}) copy-start(f32[20,64,128]{2,1,0:T(8,128)} %param.21) | copy-start | bytes 1966084
  9.9 19.7 %copy-start.15 = (f32[9,8,128]{2,1,0:T(8,128)S(1)}, f32[9,8,128]{2,1,0:T(8,128)}, u32[]{:S(2)}) copy-start(f32[9,8,128]{2,1,0:T(8,128)} %param.22) | copy-start | bytes 110596
  9.9 20.4 %copy-start.11 = (s32[160,8]{0,1:T(8,128)S(1)}, s32[160,8]{0,1:T(8,128)}, u32[]{:S(2)}) copy-start(s32[160,8]{0,1:T(8,128)} %param.26) | copy-start | bytes 15364
  9.9 20.5 %copy-start.9 = (s32[1500,8]{0,1:T(8,128)S(1)}, s32[1500,8]{0,1:T(8,128)}, u32[]{:S(2)}) copy-start(s32[1500,8]{0,1:T(8,128)} %param.25) | copy-start | bytes 144004
  11.4 19.0 %copy-start.10 = (f32[1500]{0:T(1024)S(1)}, f32[1500]{0:T(1024)}, u32[]{:S(2)}) copy-start(f32[1500]{0:T(1024)} %param.23) | copy-start | bytes 18004
  13.0 31.7 %all-to-all-start = ((f32[8,20,8,128]{3,2,1,0:T(8,128)}), f32[8,20,8,128]{3,2,1,0:T(8,128)S(1)}, u32[]{:S(2)}, u32[]{:S(2)}) async-start(f32[8,20,8,128]{3,2,1,0:T(8,128)} %fusion), calls=%async_computation | async-start | bytes 1310720 | tf_op jit(solution)/shard_map/all_to_all | solution.py:495
  23.9 15.7 %collective-permute-start = (f32[5,64,128]{2,1,0:T(8,128)}, f32[5,64,128]{2,1,0:T(8,128)S(1)}, u32[]{:S(2)}, u32[]{:S(2)}) collective-permute-start(f32[5,64,128]{2,1,0:T(8,128)} %get-tuple-element.32), channel_id=1, source_target_pairs={{0,8},{8,16},{16,24},{24,0},{1,9},{9,17},{17,25},{25,1},{2,10},{10... | collective-permute-start | bytes 491528 | tf_op jit(solution)/shard_map/ppermute | solution.py:478
  25.4 14.2 %collective-permute-start.1 = (f32[5,64,128]{2,1,0:T(8,128)S(1)}, f32[5,64,128]{2,1,0:T(8,128)S(1)}, u32[]{:S(2)}, u32[]{:S(2)}) collective-permute-start(f32[5,64,128]{2,1,0:T(8,128)S(1)} %get-tuple-element.31), channel_id=1, source_target_pairs={{0,16},{8,24},{16,0},{24,8},{1,17},{9,25},{17,1},{25,9},{2,18},{10... | collective-permute-start | bytes 491528 | tf_op jit(solution)/shard_map/ppermute | solution.py:478
  28.1 11.5 %collective-permute-start.2 = (f32[5,64,128]{2,1,0:T(8,128)S(1)}, f32[5,64,128]{2,1,0:T(8,128)S(1)}, u32[]{:S(2)}, u32[]{:S(2)}) collective-permute-start(f32[5,64,128]{2,1,0:T(8,128)S(1)} %get-tuple-element.30), channel_id=1, source_target_pairs={{0,24},{8,0},{16,8},{24,16},{1,25},{9,1},{17,9},{25,17},{2,26},{10... | collective-permute-start | bytes 491528 | tf_op jit(solution)/shard_map/ppermute | solution.py:478
  29.5 10.0 %collective-permute-start.3 = (f32[9,8,128]{2,1,0:T(8,128)S(1)}, f32[9,8,128]{2,1,0:T(8,128)S(1)}, u32[]{:S(2)}, u32[]{:S(2)}) collective-permute-start(f32[9,8,128]{2,1,0:T(8,128)S(1)} %copy-done.15), channel_id=1, source_target_pairs={{0,0},{1,1},{2,2},{3,3},{7,4},{6,5},{5,6},{4,7},{8,8},{9,9},{10,10... | collective-permute-start | bytes 110600 | tf_op jit(solution)/shard_map/ppermute | solution.py:508
  38.4 1.2 copy-start
  45.2 19.5 %collective-permute-start.6 = (f32[176,128]{1,0:T(8,128)S(1)}, f32[176,128]{1,0:T(8,128)S(1)}, u32[]{:S(2)}, u32[]{:S(2)}) collective-permute-start(f32[176,128]{1,0:T(8,128)S(1)} %get-tuple-element.23.near_ref), channel_id=1, source_target_pairs={{0,32},{32,64},{64,96},{96,128},{128,160},{160,192},{192,224},{224... | collective-permute-start | bytes 270344 | tf_op jit(solution)/shard_map/ppermute | solution.py:478
  45.3 19.4 %collective-permute-start.7 = (f32[176,128]{1,0:T(8,128)S(1)}, f32[176,128]{1,0:T(8,128)S(1)}, u32[]{:S(2)}, u32[]{:S(2)}) collective-permute-start(f32[176,128]{1,0:T(8,128)S(1)} %get-tuple-element.23.near_ref), channel_id=1, source_target_pairs={{0,224},{32,0},{64,32},{96,64},{128,96},{160,128},{192,160},{224,1... | collective-permute-start | bytes 270344 | tf_op jit(solution)/shard_map/ppermute | solution.py:478
  47.0 17.6 %collective-permute-start.4 = (f32[176,128]{1,0:T(8,128)S(1)}, f32[176,128]{1,0:T(8,128)S(1)}, u32[]{:S(2)}, u32[]{:S(2)}) collective-permute-start(f32[176,128]{1,0:T(8,128)S(1)} %get-tuple-element.22.last_ref), channel_id=1, source_target_pairs={{0,1},{1,2},{2,3},{3,7},{7,6},{6,5},{5,4},{4,8},{8,9},{9,10},{10,1... | collective-permute-start | bytes 270344 | tf_op jit(solution)/shard_map/ppermute | solution.py:527
  47.2 17.4 %collective-permute-start.5 = (f32[176,128]{1,0:T(8,128)S(1)}, f32[176,128]{1,0:T(8,128)S(1)}, u32[]{:S(2)}, u32[]{:S(2)}) collective-permute-start(f32[176,128]{1,0:T(8,128)S(1)} %get-tuple-element.21.first_ref), channel_id=1, source_target_pairs={{1,0},{2,1},{3,2},{7,3},{6,7},{5,6},{4,5},{8,4},{9,8},{10,9},{11,1... | collective-permute-start | bytes 270344 | tf_op jit(solution)/shard_map/ppermute | solution.py:528
  64.6 10.2 %copy-start.14 = (f32[9,7]{1,0:T(8,128)S(1)}, f32[9,7]{1,0:T(8,128)}, u32[]{:S(2)}) copy-start(f32[9,7]{1,0:T(8,128)} %constant.108.clone) | copy-start | bytes 760
  64.6 10.9 %copy-start.12 = (f32[256]{0:T(256)S(1)}, f32[256]{0:T(256)}, u32[]{:S(2)}) copy-start(f32[256]{0:T(256)} %constant.103.clone) | copy-start | bytes 3076
  64.6 10.9 %copy-start.13 = (f32[128]{0:T(128)S(1)}, f32[128]{0:T(128)}, u32[]{:S(2)}) copy-start(f32[128]{0:T(128)} %constant.104.clone) | copy-start | bytes 1540
  64.6 10.9 %copy-start.17 = (f32[128,128]{1,0:T(8,128)S(1)}, f32[128,128]{1,0:T(8,128)}, u32[]{:S(2)}) copy-start(f32[128,128]{1,0:T(8,128)} %constant.105.clone) | copy-start | bytes 196612
  70.0 5.9 %copy-start.16 = (f32[128,128]{1,0:T(8,128)S(1)}, f32[128,128]{1,0:T(8,128)}, u32[]{:S(2)}) copy-start(f32[128,128]{1,0:T(8,128)} %constant.106.clone) | copy-start | bytes 196612
  70.0 6.3 %copy-start.18 = (f32[7]{0:T(128)S(1)}, f32[7]{0:T(128)}, u32[]{:S(2)}) copy-start(f32[7]{0:T(128)} %constant.107.clone) | copy-start | bytes 88
  70.0 27.3 %copy-start.2 = (f32[256,256]{1,0:T(8,128)S(1)}, f32[256,256]{1,0:T(8,128)}, u32[]{:S(2)}) copy-start(f32[256,256]{1,0:T(8,128)} %constant.109.clone.cy_ref) | copy-start | bytes 786436
  70.0 27.3 %copy-start.3 = (f32[128,128]{1,0:T(8,128)S(1)}, f32[128,128]{1,0:T(8,128)}, u32[]{:S(2)}) copy-start(f32[128,128]{1,0:T(8,128)} %constant.110.clone.cxt_ref) | copy-start | bytes 196612
  70.0 27.2 %copy-start.5 = (f32[8,128]{1,0:T(8,128)S(1)}, f32[8,128]{1,0:T(8,128)}, u32[]{:S(2)}) copy-start(f32[8,128]{1,0:T(8,128)} %constant.111.clone.ends_of_ref) | copy-start | bytes 12292
  70.0 27.2 %all-to-all-start.1 = ((f32[32,5,8,128]{3,2,1,0:T(8,128)}), f32[32,5,8,128]{3,2,1,0:T(8,128)S(1)}, u32[]{:S(2)}, u32[]{:S(2)}) async-start(f32[32,5,8,128]{3,2,1,0:T(8,128)} %bitcast.22), calls=%async_computation.1 | async-start | bytes 1310720 | tf_op jit(solution)/shard_map/all_to_all | solution.py:534
  76.3 28.6 %copy-start.4 = (f32[128,128]{1,0:T(8,128)S(1)}, f32[128,128]{1,0:T(8,128)}, u32[]{:S(2)}) copy-start(f32[128,128]{1,0:T(8,128)} %constant.112.clone.cx_ref) | copy-start | bytes 196612
  97.3 13.1 %copy-start.1 = (f32[256,256]{1,0:T(8,128)S(1)}, f32[256,256]{1,0:T(8,128)}, u32[]{:S(2)}) copy-start(f32[256,256]{1,0:T(8,128)} %constant.113.clone.cyt_ref) | copy-start | bytes 786436
  100.8 9.5 %all-to-all-start.2 = ((f32[8,16,256]{2,1,0:T(8,128)}), f32[8,16,256]{2,1,0:T(8,128)S(1)}, u32[]{:S(2)}, u32[]{:S(2)}) async-start(f32[8,16,256]{2,1,0:T(8,128)} %get-tuple-element.29), calls=%async_computation.2 | async-start | bytes 262144 | tf_op jit(solution)/shard_map/all_to_all | solution.py:556
  105.6 19.6 %copy-start.6 = (f32[20,64,128]{2,1,0:T(8,128)S(1)}, f32[20,64,128]{2,1,0:T(8,128)}, u32[]{:S(2)}) copy-start(f32[20,64,128]{2,1,0:T(8,128)} %param.19) | copy-start | bytes 1966084
  105.6 19.6 %copy-start.7 = (f32[20,64,128]{2,1,0:T(8,128)S(1)}, f32[20,64,128]{2,1,0:T(8,128)}, u32[]{:S(2)}) copy-start(f32[20,64,128]{2,1,0:T(8,128)} %param.20) | copy-start | bytes 1966084

commit v6 on v5

--- a/solution.py
+++ b/solution.py
@@ -478,6 +478,21 @@
     return lax.ppermute(x, axis, [(i, (i + by) % count) for i in range(count)])
 
 
+def dealt_kernel(order, x_ref, out_ref):
+    rows = out_ref.shape[2]
+    for k, block in enumerate(order):
+        out_ref[k] = x_ref[:, block * rows : (block + 1) * rows, :]
+
+
+def dealt(x, order):
+    modes, length, cols = x.shape
+    return pl.pallas_call(
+        functools.partial(dealt_kernel, order),
+        out_shape=jax.ShapeDtypeStruct((len(order), modes, length // len(order), cols), x.dtype),
+        name="dealt",
+    )(x)
+
+
 def on_device(
     field_now, field_before, source, log_fields, weights, mean_perm, node_index, mode_index
 ):
@@ -490,8 +505,7 @@
     fields = log_fields.shape[0]
 
     order = row_order(nsa)
-    parts = field_now.reshape(modes, nsa, rows, cols)
-    outgoing = jnp.stack([parts[:, block] for block in order])
+    outgoing = dealt(field_now, order)
     field = lax.all_to_all(outgoing, "sa", 0, 0, tiled=True).reshape(p * rows, cols)
 
     place = lax.axis_index("gy")

time: 128 us -> 118 us (0.922)
  local copies, waits for them, and re-layouts: 15.5 us -> 2.48 us
  Pallas kernels: 28.7 us -> 31.5 us
    unnamed x47 -> x38, local copies, waits for them, and re-layouts: 13 us -> 2.21 us
    pallas_call x0 -> x1, Pallas kernels: none -> 2.04 us  [dealt(): pl.pallas_call(functools.partial(dealt_kernel, order), out_shape=jax.Shap...]
    another operation x1 -> x0, local copies, waits for them, and re-layouts: 1.54 us -> none  [on_device(): outgoing = jnp.stack([parts[:, block] for block in order])]
  transfers between devices with their start and end apart: 11 -> 11, of which waited for: 3 -> 3; matrix products, arithmetic and copies ran while one was open for 2% -> 2% of each run, Pallas kernels for 14% -> 16%
where the time goes in v6:
time: 118 us; the launch traced here: 117 us
  starting transfers between devices  35 us (30%)
  Pallas kernels  31.5 us (27%)
  waiting for transfers between devices  30.4 us (26%)
  blocking collectives  13.5 us (11%)
  local copies, waits for them, and re-layouts  2.48 us (2%)
  between operations  1.75 us (1%)
  other arithmetic  1.25 us (1%)
    all_to_all x1, waiting for transfers between devices, on_device(): lax.all_to_all(galerkin.reshape(nsa * ngy, sub, rows, cols), ('sa', 'gy')...  20.7 us
    all_to_all x1, blocking collectives, on_device(): lax.all_to_all(columns, 'gy', 0, 0, tiled=True).reshape(modes, length, cols)  13.5 us
    all_to_all x1, starting transfers between devices, on_device(): lax.all_to_all(outgoing, 'sa', 0, 0, tiled=True).reshape(p * rows, cols)  10.3 us
    pallas_call x1, Pallas kernels, inner_fluxes(): pl.pallas_call(functools.partial(inner_kernel, rows), out_shape=jax.Shape...  10.2 us
    pallas_call x1, Pallas kernels, node_tables(): pl.pallas_call(tables_kernel, grid=((q + pad) // QB,), in_specs=[pl.Block...  7.87 us
    ppermute x1, starting transfers between devices, on_device(): lax.ppermute(first, row_axis, [(b, a) for a, b in ring])  7.81 us
    ppermute x5, starting transfers between devices, rotated(): return lax.ppermute(x, axis, [(i, (i + by) % count) for i in range(count)])  7.55 us
    pallas_call x1, Pallas kernels, outer_fluxes(): pl.pallas_call(functools.partial(outer_kernel, rows), in_specs=[pl.BlockS...  5.43 us
  transfers between devices with their start and end apart: 11, of which 3 were waited for; matrix products, arithmetic and copies ran while one was open for 2% of the time, Pallas kernels for 16%

profile of v6, /device:TPU:32, one launch (start us, length us, event | category | flops | bytes accessed | tf_op | source)
XLA Modules:
  0.0 117.0 jit_solution(3269069698739699264)
XLA Ops:
  0.6 0.0 copy-start.8
  0.6 2.0 %dealt.1 = f32[8,20,8,128]{3,2,1,0:T(8,128)} custom-call(f32[20,64,128]{2,1,0:T(8,128)} %x_ref.1), custom_call_target="tpu_custom_call" | custom-call | tf_op jit(solution)/shard_map/dealt/pallas_call | solution.py:489
  2.7 10.3 %all-to-all-start = ((f32[8,20,8,128]{3,2,1,0:T(8,128)}), f32[8,20,8,128]{3,2,1,0:T(8,128)S(1)}, u32[]{:S(2)}, u32[]{:S(2)}) async-start(f32[8,20,8,128]{3,2,1,0:T(8,128)} %dealt.1), calls=%async_computation | async-start | bytes 1310720 | tf_op jit(solution)/shard_map/all_to_all | solution.py:509
  13.0 0.0 copy-done.8
  13.0 0.1 dynamic-slice_bitcast_fusion
  13.1 1.6 %collective-permute-start = (f32[5,64,128]{2,1,0:T(8,128)S(1)}, f32[5,64,128]{2,1,0:T(8,128)S(1)}, u32[]{:S(2)}, u32[]{:S(2)}) collective-permute-start(f32[5,64,128]{2,1,0:T(8,128)S(1)} %get-tuple-element.32), channel_id=1, source_target_pairs={{0,8},{8,16},{16,24},{24,0},{1,9},{9,17},{17,25},{25,1},{2,10},{10... | collective-permute-start | bytes 491528 | tf_op jit(solution)/shard_map/ppermute | solution.py:478
  14.7 2.7 %collective-permute-start.1 = (f32[5,64,128]{2,1,0:T(8,128)S(1)}, f32[5,64,128]{2,1,0:T(8,128)S(1)}, u32[]{:S(2)}, u32[]{:S(2)}) collective-permute-start(f32[5,64,128]{2,1,0:T(8,128)S(1)} %get-tuple-element.31), channel_id=1, source_target_pairs={{0,16},{8,24},{16,0},{24,8},{1,17},{9,25},{17,1},{25,9},{2,18},{10... | collective-permute-start | bytes 491528 | tf_op jit(solution)/shard_map/ppermute | solution.py:478
  17.4 1.4 %collective-permute-start.2 = (f32[5,64,128]{2,1,0:T(8,128)S(1)}, f32[5,64,128]{2,1,0:T(8,128)S(1)}, u32[]{:S(2)}, u32[]{:S(2)}) collective-permute-start(f32[5,64,128]{2,1,0:T(8,128)S(1)} %get-tuple-element.30), channel_id=1, source_target_pairs={{0,24},{8,0},{16,8},{24,16},{1,25},{9,1},{17,9},{25,17},{2,26},{10... | collective-permute-start | bytes 491528 | tf_op jit(solution)/shard_map/ppermute | solution.py:478
  18.8 1.4 %collective-permute-start.3 = (f32[9,8,128]{2,1,0:T(8,128)}, f32[9,8,128]{2,1,0:T(8,128)S(1)}, u32[]{:S(2)}, u32[]{:S(2)}) collective-permute-start(f32[9,8,128]{2,1,0:T(8,128)} %param.22), channel_id=1, source_target_pairs={{0,0},{1,1},{2,2},{3,3},{7,4},{6,5},{5,6},{4,7},{8,8},{9,9},{10,10... | collective-permute-start | bytes 110600 | tf_op jit(solution)/shard_map/ppermute | solution.py:522
  20.2 0.1 add_convert_fusion.open_ref
  20.3 0.0 copy-done.11
  20.3 0.1 copy.24.mode_ref
  20.4 0.0 copy-done.9
  20.4 0.0 copy-done.10
  20.5 7.9 %node_tables.1 = (bf16[1536,480]{1,0:T(8,128)(2,1)S(1)}, bf16[320,1536]{1,0:T(8,128)(2,1)S(1)}, bf16[1536,48]{1,0:T(8,128)(2,1)S(1)}, bf16[160,480]{1,0:T(8,128)(2,1)S(1)}) custom-call(s32[8,1536]{1,0:T(8,128)S(1)} %pad.13.index_ref, s32[160,8]{1,0:T(8,128)S(1)} %copy.24.mode_ref, f32[1,1536]{1,0:T(1,128)S(1)} %broadcast_in_dim.10.weight_ref), custom_call_target="tpu_custom_call" | custom-call | tf_op jit(solution)/shard_map/node_tables/pallas_call | solution.py:116
  28.4 0.0 copy-start
  28.4 1.2 %copy-done = bf16[1536,480]{1,0:T(8,128)(2,1)} copy-done((bf16[1536,480]{1,0:T(8,128)(2,1)}, bf16[1536,480]{1,0:T(8,128)(2,1)S(1)}, u32[]{:S(2)}) %copy-start) | copy-done | bytes 1474584
  29.6 0.0 collective-permute-done.3
  29.6 0.0 collective-permute-done.s1_ref
  29.6 0.0 collective-permute-done.1.s2_ref
  29.7 0.0 collective-permute-done.2.s3_ref
  29.7 4.9 %all-to-all-done = f32[8,20,8,128]{3,2,1,0:T(8,128)S(1)} async-done(((f32[8,20,8,128]{3,2,1,0:T(8,128)}), f32[8,20,8,128]{3,2,1,0:T(8,128)S(1)}, u32[]{:S(2)}, u32[]{:S(2)}) %all-to-all-start) | async-done | bytes 655392 | tf_op jit(solution)/shard_map/all_to_all | solution.py:509
  34.5 0.5 rim_of.1
  35.0 0.1 collective-permute-start.6
  35.1 1.7 %collective-permute-start.7 = (f32[176,128]{1,0:T(8,128)S(1)}, f32[176,128]{1,0:T(8,128)S(1)}, u32[]{:S(2)}, u32[]{:S(2)}) collective-permute-start(f32[176,128]{1,0:T(8,128)S(1)} %get-tuple-element.23.near_ref), channel_id=1, source_target_pairs={{0,224},{32,0},{64,32},{96,64},{128,96},{160,128},{192,160},{224,1... | collective-permute-start | bytes 270344 | tf_op jit(solution)/shard_map/ppermute | solution.py:478
  36.8 0.2 collective-permute-start.4
  37.1 7.8 %collective-permute-start.5 = (f32[176,128]{1,0:T(8,128)S(1)}, f32[176,128]{1,0:T(8,128)S(1)}, u32[]{:S(2)}, u32[]{:S(2)}) collective-permute-start(f32[176,128]{1,0:T(8,128)S(1)} %get-tuple-element.21.first_ref), channel_id=1, source_target_pairs={{1,0},{2,1},{3,2},{7,3},{6,7},{5,6},{4,5},{8,4},{9,8},{10,9},{11,1... | collective-permute-start | bytes 270344 | tf_op jit(solution)/shard_map/ppermute | solution.py:542
  44.9 10.2 %inner_fluxes.1.g_ref = f32[8,160,128]{2,1,0:T(8,128)S(1)} custom-call(f32[1280,128]{1,0:T(8,128)S(1)} %bitcast.40, bf16[48,1024]{1,0:T(8,128)(2,1)S(1)} %pad_maximum_fusion.log_ref, bf16[1536,480]{1,0:T(8,128)(2,1)} %copy-done, bf16[1536,48]{1,0:T(8,128)(2,1)S(1)} %get-tuple-element.18.germ_ref, bf16[320,1536]{1,0:T(8,128)(2,1)S(1)} %get-tuple-element.19.w_ref, ...), custom_call_target="tpu_custom_call" | custom-call | flops 5662310400 | bytes 8388608 | tf_op jit(solution)/shard_map/inner_fluxes/pallas_call | solution.py:268
  55.1 0.0 copy-start.14
  55.1 0.0 copy-start.12
  55.1 0.0 copy-start.13
  55.1 0.0 copy-start.16
  55.1 0.0 collective-permute-done.4.up_ref
  55.1 0.0 collective-permute-done.5.down_ref
  55.1 0.0 collective-permute-done.6.left_ref
  55.1 0.0 collective-permute-done.7.right_ref
  55.1 5.4 %outer_fluxes.1 = f32[1280,128]{1,0:T(8,128)} custom-call(f32[4]{0:T(128)S(1)} %add_convert_fusion.open_ref, f32[8,160,128]{2,1,0:T(8,128)S(1)} %inner_fluxes.1.g_ref, f32[176,128]{1,0:T(8,128)S(1)} %get-tuple-element.21.first_ref, f32[176,128]{1,0:T(8,128)S(1)} %get-tuple-element.22.last_ref, f32[176,128]{1,0:T(8,128)S(1)} %get-tuple-element.23.near_ref, ...), custom_call_target="tpu_custom_call" | custom-call | flops 1132462080 | bytes 8388608 | tf_op jit(solution)/shard_map/outer_fluxes/pallas_call | solution.py:359
  60.6 0.0 copy-start.5
  60.6 4.3 %all-to-all-start.1 = ((f32[32,5,8,128]{3,2,1,0:T(8,128)}), f32[32,5,8,128]{3,2,1,0:T(8,128)S(1)}, u32[]{:S(2)}, u32[]{:S(2)}) async-start(f32[32,5,8,128]{3,2,1,0:T(8,128)} %bitcast.13), calls=%async_computation.1 | async-start | bytes 1310720 | tf_op jit(solution)/shard_map/all_to_all | solution.py:548
  64.9 0.0 copy-done.14
  65.6 0.0 copy-done.12
  65.6 0.0 copy-done.13
  65.6 0.0 copy-done.16
  65.6 0.4 fusion.1
  66.0 0.4 fusion.2
  66.4 0.0 copy-start.4
  66.4 0.2 convolution_bitcast_fusion
  66.7 0.2 convolution_bitcast_fusion.1
  66.9 0.1 add_divide_fusion.recip_ref
  67.0 20.7 %all-to-all-done.1.part_ref = f32[32,5,8,128]{3,2,1,0:T(8,128)S(1)} async-done(((f32[32,5,8,128]{3,2,1,0:T(8,128)}), f32[32,5,8,128]{3,2,1,0:T(8,128)S(1)}, u32[]{:S(2)}, u32[]{:S(2)}) %all-to-all-start.1) | async-done | bytes 655392 | tf_op jit(solution)/shard_map/all_to_all | solution.py:548
  87.7 0.0 copy-done.2
  87.8 0.0 copy-start.1
  87.8 3.6 %local_solve.1 = (f32[1280,128]{1,0:T(8,128)S(1)}, f32[8,16,256]{2,1,0:T(8,128)}) custom-call(s32[1]{0:T(128)} %bitcast.place_ref, f32[32,5,8,128]{3,2,1,0:T(8,128)S(1)} %all-to-all-done.1.part_ref, f32[5,64,128]{2,1,0:T(8,128)S(1)} %get-tuple-element.24.s0_ref, f32[5,64,128]{2,1,0:T(8,128)S(1)} %collective-permute-done.s1_ref, ...), custom_call_target="tpu_custom_call" | custom-call | tf_op jit(solution)/shard_map/local_solve/pallas_call | solution.py:559
  91.4 3.4 %all-to-all-start.2 = ((f32[8,16,256]{2,1,0:T(8,128)}), f32[8,16,256]{2,1,0:T(8,128)S(1)}, u32[]{:S(2)}, u32[]{:S(2)}) async-start(f32[8,16,256]{2,1,0:T(8,128)} %get-tuple-element.29), calls=%async_computation.2 | async-start | bytes 262144 | tf_op jit(solution)/shard_map/all_to_all | solution.py:570
  94.7 0.1 copy.25.g_first_ref
  94.8 0.1 copy.26.g_last_ref
  94.9 0.7 back.1.z_ref
  95.6 0.0 copy-start.6
  95.6 0.0 copy-start.7
  95.6 4.8 %all-to-all-done.2.jump_ref = f32[8,16,256]{2,1,0:T(8,128)S(1)} async-done(((f32[8,16,256]{2,1,0:T(8,128)}), f32[8,16,256]{2,1,0:T(8,128)S(1)}, u32[]{:S(2)}, u32[]{:S(2)}) %all-to-all-start.2) | async-done | bytes 131104 | tf_op jit(solution)/shard_map/all_to_all | solution.py:570
  100.4 1.3 %joined_solve.1 = f32[4,5,64,128]{3,2,1,0:T(8,128)S(1)} custom-call(f32[1280,128]{1,0:T(8,128)S(1)} %back.1.z_ref, f32[8,16,256]{2,1,0:T(8,128)S(1)} %all-to-all-done.2.jump_ref, f32[256,128]{1,0:T(8,128)S(1)} %copy.25.g_first_ref, f32[256,128]{1,0:T(8,128)S(1)} %copy.26.g_last_ref, f32[256,256]{1,0:T(8,128)S(1)} %copy-done.1), custom_call_target="tpu_custom_call" | custom-call | tf_op jit(solution)/shard_map/joined_solve/pallas_call | solution.py:580
  101.7 13.5 %all_to_all.20 = f32[4,5,64,128]{3,2,1,0:T(8,128)S(1)} all-to-all(f32[4,5,64,128]{3,2,1,0:T(8,128)S(1)} %joined_solve.1), channel_id=1, replica_groups=mesh['gx'=8,'gy'=4,'sa'=8] {'gy'}, dimensions={0} | all-to-all | bytes 1310720 | tf_op jit(solution)/shard_map/all_to_all | solution.py:586
  115.2 1.0 multiply_add_fusion
  116.2 0.8 copy.32
  (25 shorter events, 0.1 us)
Async XLA Ops:
  0.6 12.4 %copy-start.8 = (f32[20,64,128]{2,1,0:T(8,128)S(1)}, f32[20,64,128]{2,1,0:T(8,128)}, u32[]{:S(2)}) copy-start(f32[20,64,128]{2,1,0:T(8,128)} %param.21) | copy-start | bytes 1966084
  2.7 17.6 %copy-start.11 = (s32[160,8]{0,1:T(8,128)S(1)}, s32[160,8]{0,1:T(8,128)}, u32[]{:S(2)}) copy-start(s32[160,8]{0,1:T(8,128)} %param.26) | copy-start | bytes 15364
  2.7 17.7 %copy-start.9 = (s32[1500,8]{0,1:T(8,128)S(1)}, s32[1500,8]{0,1:T(8,128)}, u32[]{:S(2)}) copy-start(s32[1500,8]{0,1:T(8,128)} %param.25) | copy-start | bytes 144004
  2.7 17.8 %copy-start.10 = (f32[1500]{0:T(1024)S(1)}, f32[1500]{0:T(1024)}, u32[]{:S(2)}) copy-start(f32[1500]{0:T(1024)} %param.23) | copy-start | bytes 18004
  2.7 31.9 %all-to-all-start = ((f32[8,20,8,128]{3,2,1,0:T(8,128)}), f32[8,20,8,128]{3,2,1,0:T(8,128)S(1)}, u32[]{:S(2)}, u32[]{:S(2)}) async-start(f32[8,20,8,128]{3,2,1,0:T(8,128)} %dealt.1), calls=%async_computation | async-start | bytes 1310720 | tf_op jit(solution)/shard_map/all_to_all | solution.py:509
  13.1 16.5 %collective-permute-start = (f32[5,64,128]{2,1,0:T(8,128)S(1)}, f32[5,64,128]{2,1,0:T(8,128)S(1)}, u32[]{:S(2)}, u32[]{:S(2)}) collective-permute-start(f32[5,64,128]{2,1,0:T(8,128)S(1)} %get-tuple-element.32), channel_id=1, source_target_pairs={{0,8},{8,16},{16,24},{24,0},{1,9},{9,17},{17,25},{25,1},{2,10},{10... | collective-permute-start | bytes 491528 | tf_op jit(solution)/shard_map/ppermute | solution.py:478
  14.7 15.0 %collective-permute-start.1 = (f32[5,64,128]{2,1,0:T(8,128)S(1)}, f32[5,64,128]{2,1,0:T(8,128)S(1)}, u32[]{:S(2)}, u32[]{:S(2)}) collective-permute-start(f32[5,64,128]{2,1,0:T(8,128)S(1)} %get-tuple-element.31), channel_id=1, source_target_pairs={{0,16},{8,24},{16,0},{24,8},{1,17},{9,25},{17,1},{25,9},{2,18},{10... | collective-permute-start | bytes 491528 | tf_op jit(solution)/shard_map/ppermute | solution.py:478
  17.4 12.3 %collective-permute-start.2 = (f32[5,64,128]{2,1,0:T(8,128)S(1)}, f32[5,64,128]{2,1,0:T(8,128)S(1)}, u32[]{:S(2)}, u32[]{:S(2)}) collective-permute-start(f32[5,64,128]{2,1,0:T(8,128)S(1)} %get-tuple-element.30), channel_id=1, source_target_pairs={{0,24},{8,0},{16,8},{24,16},{1,25},{9,1},{17,9},{25,17},{2,26},{10... | collective-permute-start | bytes 491528 | tf_op jit(solution)/shard_map/ppermute | solution.py:478
  18.8 10.7 %collective-permute-start.3 = (f32[9,8,128]{2,1,0:T(8,128)}, f32[9,8,128]{2,1,0:T(8,128)S(1)}, u32[]{:S(2)}, u32[]{:S(2)}) collective-permute-start(f32[9,8,128]{2,1,0:T(8,128)} %param.22), channel_id=1, source_target_pairs={{0,0},{1,1},{2,2},{3,3},{7,4},{6,5},{5,6},{4,7},{8,8},{9,9},{10,10... | collective-permute-start | bytes 110600 | tf_op jit(solution)/shard_map/ppermute | solution.py:522
  28.4 1.2 %copy-start = (bf16[1536,480]{1,0:T(8,128)(2,1)}, bf16[1536,480]{1,0:T(8,128)(2,1)S(1)}, u32[]{:S(2)}) copy-start(bf16[1536,480]{1,0:T(8,128)(2,1)S(1)} %get-tuple-element.17.basis_ref) | copy-start | bytes 4423684
  35.0 20.1 %collective-permute-start.6 = (f32[176,128]{1,0:T(8,128)S(1)}, f32[176,128]{1,0:T(8,128)S(1)}, u32[]{:S(2)}, u32[]{:S(2)}) collective-permute-start(f32[176,128]{1,0:T(8,128)S(1)} %get-tuple-element.23.near_ref), channel_id=1, source_target_pairs={{0,32},{32,64},{64,96},{96,128},{128,160},{160,192},{192,224},{224... | collective-permute-start | bytes 270344 | tf_op jit(solution)/shard_map/ppermute | solution.py:478
  35.1 20.0 %collective-permute-start.7 = (f32[176,128]{1,0:T(8,128)S(1)}, f32[176,128]{1,0:T(8,128)S(1)}, u32[]{:S(2)}, u32[]{:S(2)}) collective-permute-start(f32[176,128]{1,0:T(8,128)S(1)} %get-tuple-element.23.near_ref), channel_id=1, source_target_pairs={{0,224},{32,0},{64,32},{96,64},{128,96},{160,128},{192,160},{224,1... | collective-permute-start | bytes 270344 | tf_op jit(solution)/shard_map/ppermute | solution.py:478
  36.8 18.3 %collective-permute-start.4 = (f32[176,128]{1,0:T(8,128)S(1)}, f32[176,128]{1,0:T(8,128)S(1)}, u32[]{:S(2)}, u32[]{:S(2)}) collective-permute-start(f32[176,128]{1,0:T(8,128)S(1)} %get-tuple-element.22.last_ref), channel_id=1, source_target_pairs={{0,1},{1,2},{2,3},{3,7},{7,6},{6,5},{5,4},{4,8},{8,9},{9,10},{10,1... | collective-permute-start | bytes 270344 | tf_op jit(solution)/shard_map/ppermute | solution.py:541
  37.1 18.0 %collective-permute-start.5 = (f32[176,128]{1,0:T(8,128)S(1)}, f32[176,128]{1,0:T(8,128)S(1)}, u32[]{:S(2)}, u32[]{:S(2)}) collective-permute-start(f32[176,128]{1,0:T(8,128)S(1)} %get-tuple-element.21.first_ref), channel_id=1, source_target_pairs={{1,0},{2,1},{3,2},{7,3},{6,7},{5,6},{4,5},{8,4},{9,8},{10,9},{11,1... | collective-permute-start | bytes 270344 | tf_op jit(solution)/shard_map/ppermute | solution.py:542
  55.1 9.8 %copy-start.14 = (f32[9,7]{1,0:T(8,128)S(1)}, f32[9,7]{1,0:T(8,128)}, u32[]{:S(2)}) copy-start(f32[9,7]{1,0:T(8,128)} %constant.108.clone) | copy-start | bytes 760
  55.1 10.5 %copy-start.12 = (f32[256]{0:T(256)S(1)}, f32[256]{0:T(256)}, u32[]{:S(2)}) copy-start(f32[256]{0:T(256)} %constant.103.clone) | copy-start | bytes 3076
  55.1 10.5 %copy-start.13 = (f32[128]{0:T(128)S(1)}, f32[128]{0:T(128)}, u32[]{:S(2)}) copy-start(f32[128]{0:T(128)} %constant.104.clone) | copy-start | bytes 1540
  55.1 10.5 %copy-start.16 = (f32[128,128]{1,0:T(8,128)S(1)}, f32[128,128]{1,0:T(8,128)}, u32[]{:S(2)}) copy-start(f32[128,128]{1,0:T(8,128)} %constant.106.clone) | copy-start | bytes 196612
  60.6 5.4 %copy-start.15 = (f32[128,128]{1,0:T(8,128)S(1)}, f32[128,128]{1,0:T(8,128)}, u32[]{:S(2)}) copy-start(f32[128,128]{1,0:T(8,128)} %constant.105.clone) | copy-start | bytes 196612
  60.6 5.8 %copy-start.17 = (f32[7]{0:T(128)S(1)}, f32[7]{0:T(128)}, u32[]{:S(2)}) copy-start(f32[7]{0:T(128)} %constant.107.clone) | copy-start | bytes 88
  60.6 27.2 %copy-start.2 = (f32[256,256]{1,0:T(8,128)S(1)}, f32[256,256]{1,0:T(8,128)}, u32[]{:S(2)}) copy-start(f32[256,256]{1,0:T(8,128)} %constant.109.clone.cy_ref) | copy-start | bytes 786436
  60.6 27.2 %copy-start.3 = (f32[128,128]{1,0:T(8,128)S(1)}, f32[128,128]{1,0:T(8,128)}, u32[]{:S(2)}) copy-start(f32[128,128]{1,0:T(8,128)} %constant.110.clone.cxt_ref) | copy-start | bytes 196612
  60.6 27.2 %copy-start.5 = (f32[8,128]{1,0:T(8,128)S(1)}, f32[8,128]{1,0:T(8,128)}, u32[]{:S(2)}) copy-start(f32[8,128]{1,0:T(8,128)} %constant.111.clone.ends_of_ref) | copy-start | bytes 12292
  60.6 27.1 %all-to-all-start.1 = ((f32[32,5,8,128]{3,2,1,0:T(8,128)}), f32[32,5,8,128]{3,2,1,0:T(8,128)S(1)}, u32[]{:S(2)}, u32[]{:S(2)}) async-start(f32[32,5,8,128]{3,2,1,0:T(8,128)} %bitcast.13), calls=%async_computation.1 | async-start | bytes 1310720 | tf_op jit(solution)/shard_map/all_to_all | solution.py:548
  66.4 28.5 %copy-start.4 = (f32[128,128]{1,0:T(8,128)S(1)}, f32[128,128]{1,0:T(8,128)}, u32[]{:S(2)}) copy-start(f32[128,128]{1,0:T(8,128)} %constant.112.clone.cx_ref) | copy-start | bytes 196612
  87.8 12.7 %copy-start.1 = (f32[256,256]{1,0:T(8,128)S(1)}, f32[256,256]{1,0:T(8,128)}, u32[]{:S(2)}) copy-start(f32[256,256]{1,0:T(8,128)} %constant.113.clone.cyt_ref) | copy-start | bytes 786436
  91.4 9.1 %all-to-all-start.2 = ((f32[8,16,256]{2,1,0:T(8,128)}), f32[8,16,256]{2,1,0:T(8,128)S(1)}, u32[]{:S(2)}, u32[]{:S(2)}) async-start(f32[8,16,256]{2,1,0:T(8,128)} %get-tuple-element.29), calls=%async_computation.2 | async-start | bytes 262144 | tf_op jit(solution)/shard_map/all_to_all | solution.py:570
  95.6 19.5 %copy-start.6 = (f32[20,64,128]{2,1,0:T(8,128)S(1)}, f32[20,64,128]{2,1,0:T(8,128)}, u32[]{:S(2)}) copy-start(f32[20,64,128]{2,1,0:T(8,128)} %x_ref.1) | copy-start | bytes 1966084
  95.6 19.5 %copy-start.7 = (f32[20,64,128]{2,1,0:T(8,128)S(1)}, f32[20,64,128]{2,1,0:T(8,128)}, u32[]{:S(2)}) copy-start(f32[20,64,128]{2,1,0:T(8,128)} %param.20) | copy-start | bytes 1966084

commit v7 on v6

--- a/solution.py
+++ b/solution.py
@@ -413,34 +413,56 @@
     scaled_ref[...] = scaled
 
 
-def back_kernel(scaled_ref, cx_ref, z_ref):
-    z_ref[...] = jnp.dot(
-        scaled_ref[...], cx_ref[...], precision=HIGHEST, preferred_element_type=jnp.float32
-    )
-
-
-def joined_kernel(z_ref, jump_ref, g_first_ref, g_last_ref, cyt_ref, out_ref):
-    blocks = jump_ref.shape[0]
-    ngy, modes = out_ref.shape[:2]
-    ny, cols = g_first_ref.shape
-    length = ny // ngy
-    total = jump_ref[0]
-    for i in range(1, blocks):
-        total = total + jump_ref[i]
-    both = jnp.concatenate([total, jnp.zeros((LANES - 16, ny), jnp.float32)], axis=0).T
-    x = jnp.concatenate(
-        [
-            z_ref[m * ny : (m + 1) * ny]
-            + g_first_ref[...] * both[:, m : m + 1]
-            - g_last_ref[...] * both[:, 8 + m : 9 + m]
-            for m in range(modes)
-        ],
-        axis=1,
-    )
-    out = jnp.dot(cyt_ref[...], x, precision=HIGHEST, preferred_element_type=jnp.float32)
-    for g in range(ngy):
+def back_kernel(place_ref, scaled_ref, cx_ref, cyt_ref, p0_ref, p1_ref, p2_ref, p3_ref, rows_ref):
+    modes, length, cols = p0_ref.shape
+    ny = cyt_ref.shape[0]
+    ngy = ny // length
+    z = jnp.dot(scaled_ref[...], cx_ref[...], precision=HIGHEST, preferred_element_type=jnp.float32)
+    z = jnp.concatenate([z[m * ny : (m + 1) * ny] for m in range(modes)], axis=1)
+    rows_ref[...] = jnp.dot(cyt_ref[...], z, precision=HIGHEST, preferred_element_type=jnp.float32)
+    for d, out_ref in enumerate((p0_ref, p1_ref, p2_ref, p3_ref)):
+        g = lax.rem(place_ref[0] + d, ngy)
+        span = pl.ds(pl.multiple_of(g * length, 8), length)
         for m in range(modes):
-            out_ref[g, m] = out[g * length : (g + 1) * length, m * cols : (m + 1) * cols]
+            out_ref[m] = rows_ref[span, pl.ds(m * cols, cols)]
+
+
+def final_kernel(
+    place_ref, p0_ref, p1_ref, p2_ref, p3_ref, t0_ref, t1_ref, t2_ref, t3_ref, g_first_ref, g_last_ref,
+    cyt_ref, now_hbm, before_hbm, fresh_ref, update_ref, now_ref, before_ref, sems,
+):
+    modes, length, cols = p0_ref.shape
+    ngy = fresh_ref.shape[0] // modes
+    copies = [
+        pltpu.make_async_copy(now_hbm, now_ref, sems.at[0]),
+        pltpu.make_async_copy(before_hbm, before_ref, sems.at[1]),
+    ]
+    for copy in copies:
+        copy.start()
+    place = place_ref[0]
+    back = cyt_ref[pl.ds(pl.multiple_of(place * length, 8), length), :]
+    right = split(jnp.concatenate([g_first_ref[...], -g_last_ref[...]], axis=0))
+    left = []
+    for t_ref in (t0_ref, t1_ref, t2_ref, t3_ref):
+        for m in range(modes):
+            left.append(
+                jnp.concatenate([back * t_ref[m : m + 1, :], back * t_ref[8 + m : 9 + m, :]], axis=1)
+            )
+    left = split(jnp.concatenate(left, axis=0))
+    jump = jnp.dot(left[0], right[0], preferred_element_type=jnp.float32)
+    jump = jump + jnp.dot(left[1], right[0], preferred_element_type=jnp.float32)
+    jump = jump + jnp.dot(left[0], right[1], preferred_element_type=jnp.float32)
+    for copy in copies:
+        copy.wait()
+    for d, p_ref in enumerate((p0_ref, p1_ref, p2_ref, p3_ref)):
+        g = lax.rem(place + ngy - d, ngy)
+        for m in range(modes):
+            at = (d * modes + m) * length
+            update = p_ref[m] + jump[at : at + length]
+            mode = g * modes + m
+            before = before_ref[mode]
+            fresh_ref[mode] = before + relax_weight * (now_ref[mode] - before + step_length * update)
+            update_ref[mode] = update
 
 
 def solve_tables(mean_perm, ny, cols, blocks, position):
@@ -568,23 +590,35 @@
         name="local_solve",
     )(place[None], part, *pieces, f32(cy), f32(cx.T), f32(ends_of), recip, coef)
     jumps = lax.all_to_all(jumps, "gx", 0, 0, tiled=True)
-    z = pl.pallas_call(
+    smem = pl.BlockSpec(memory_space=pltpu.SMEM)
+    hbm = pl.BlockSpec(memory_space=pl.ANY)
+    sent = pl.pallas_call(
         back_kernel,
-        out_shape=jax.ShapeDtypeStruct((sub * ny, cols), jnp.float32),
+        in_specs=[smem] + [vmem] * 3,
+        out_shape=[jax.ShapeDtypeStruct((sub, length, cols), jnp.float32)] * 4,
+        scratch_shapes=[pltpu.VMEM((ny, sub * cols), jnp.float32)],
         compiler_params=params,
         cost_estimate=pl.CostEstimate(
-            flops=12 * sub * ny * cols * cols, bytes_accessed=2 << 20, transcendentals=0
+            flops=36 * sub * ny * cols * cols, bytes_accessed=2 << 20, transcendentals=0
         ),
         name="back",
-    )(scaled, f32(cx))
-    columns = pl.pallas_call(
-        joined_kernel,
-        out_shape=jax.ShapeDtypeStruct((ngy, sub, length, cols), jnp.float32),
+    )(place[None], scaled, f32(cx), f32(cy.T))
+    got = [sent[0]] + [rotated(sent[d], "gy", d) for d in range(1, ngy)]
+    total = jnp.sum(jumps, axis=0)
+    totals = [total] + [rotated(total, "gy", d) for d in range(1, ngy)]
+    block = jax.ShapeDtypeStruct(field_now.shape, jnp.float32)
+    fresh, update = pl.pallas_call(
+        final_kernel,
+        in_specs=[smem] + [vmem] * 11 + [hbm] * 2,
+        out_shape=[block] * 2,
+        scratch_shapes=[
+            pltpu.VMEM(field_now.shape, jnp.float32),
+            pltpu.VMEM(field_now.shape, jnp.float32),
+            pltpu.SemaphoreType.DMA((2,)),
+        ],
         compiler_params=params,
-        name="joined_solve",
-    )(z, jumps, g_first, g_last, f32(cy.T))
-    update = lax.all_to_all(columns, "gy", 0, 0, tiled=True).reshape(modes, length, cols)
-    fresh = field_before + relax_weight * (field_now - field_before + step_length * update)
+        name="final",
+    )(place[None], *got, *totals, g_first, g_last, f32(cy.T), field_now, field_before)
     return (fresh, update)
 
 

time: 118 us -> 115 us (0.975)
  blocking collectives: 13.5 us -> 0 us
  starting transfers between devices: 35 us -> 44.1 us
  Pallas kernels: 31.5 us -> 35.4 us
  waiting for transfers between devices: 30.4 us -> 28.3 us
    all_to_all x1 -> x0, blocking collectives: 13.5 us -> none  [on_device(): lax.all_to_all(columns, 'gy', 0, 0, tiled=True).reshape(modes, length, cols)]
    ppermute x5 -> x11, starting transfers between devices: 7.55 us -> 16.7 us  [rotated(): return lax.ppermute(x, axis, [(i, (i + by) % count) for i in range(count)])]
    all_to_all x1, waiting for transfers between devices: 4.77 us -> 0.01 us  [on_device(): jumps = lax.all_to_all(jumps, 'gx', 0, 0, tiled=True)]
    pallas_call x2, Pallas kernels: 1.92 us -> 5.86 us  [the longest x1 3.02 us: on_device(): pl.pallas_call(back_kernel, in_specs=[smem] + [vmem] * 3, out_shape=[jax....]
    ppermute x5 -> x11, waiting for transfers between devices: 0.01 us -> 2.71 us  [rotated(): return lax.ppermute(x, axis, [(i, (i + by) % count) for i in range(count)])]
  transfers between devices with their start and end apart: 11 -> 17, of which waited for: 3 -> 5; matrix products, arithmetic and copies ran while one was open for 2% -> 2% of each run, Pallas kernels for 16% -> 19%
where the time goes in v7:
time: 115 us; the launch traced here: 114 us
  starting transfers between devices  44.1 us (38%)
  Pallas kernels  35.4 us (31%)
  waiting for transfers between devices  28.3 us (25%)
  local copies, waits for them, and re-layouts  2.53 us (2%)
  between operations  1.94 us (2%)
  matrix products  1.16 us (1%)
    all_to_all x1, waiting for transfers between devices, on_device(): lax.all_to_all(galerkin.reshape(nsa * ngy, sub, rows, cols), ('sa', 'gy')...  20.7 us
    ppermute x11, starting transfers between devices, rotated(): return lax.ppermute(x, axis, [(i, (i + by) % count) for i in range(count)])  16.7 us
    all_to_all x1, starting transfers between devices, on_device(): lax.all_to_all(outgoing, 'sa', 0, 0, tiled=True).reshape(p * rows, cols)  10.3 us
    pallas_call x1, Pallas kernels, inner_fluxes(): pl.pallas_call(functools.partial(inner_kernel, rows), out_shape=jax.Shape...  10.2 us
    pallas_call x1, Pallas kernels, node_tables(): pl.pallas_call(tables_kernel, grid=((q + pad) // QB,), in_specs=[pl.Block...  7.87 us
    ppermute x1, starting transfers between devices, on_device(): lax.ppermute(first, row_axis, [(b, a) for a, b in ring])  7.81 us
    pallas_call x1, Pallas kernels, outer_fluxes(): pl.pallas_call(functools.partial(outer_kernel, rows), in_specs=[pl.BlockS...  5.43 us
    all_to_all x1, waiting for transfers between devices, on_device(): lax.all_to_all(outgoing, 'sa', 0, 0, tiled=True).reshape(p * rows, cols)  4.91 us
  transfers between devices with their start and end apart: 17, of which 5 were waited for; matrix products, arithmetic and copies ran while one was open for 2% of the time, Pallas kernels for 19%

profile of v7, /device:TPU:32, one launch (start us, length us, event | category | flops | bytes accessed | tf_op | source)
XLA Modules:
  0.0 113.7 jit_solution(9449162337432123359)
XLA Ops:
  0.6 2.0 %dealt.1 = f32[8,20,8,128]{3,2,1,0:T(8,128)} custom-call(f32[20,64,128]{2,1,0:T(8,128)} %now_hbm.1), custom_call_target="tpu_custom_call" | custom-call | tf_op jit(solution)/shard_map/dealt/pallas_call | solution.py:511
  2.7 10.3 %all-to-all-start = ((f32[8,20,8,128]{3,2,1,0:T(8,128)}), f32[8,20,8,128]{3,2,1,0:T(8,128)S(1)}, u32[]{:S(2)}, u32[]{:S(2)}) async-start(f32[8,20,8,128]{3,2,1,0:T(8,128)} %dealt.1), calls=%async_computation | async-start | bytes 1310720 | tf_op jit(solution)/shard_map/all_to_all | solution.py:531
  13.0 0.1 dynamic-slice_bitcast_fusion
  13.1 1.6 %collective-permute-start = (f32[5,64,128]{2,1,0:T(8,128)S(1)}, f32[5,64,128]{2,1,0:T(8,128)S(1)}, u32[]{:S(2)}, u32[]{:S(2)}) collective-permute-start(f32[5,64,128]{2,1,0:T(8,128)S(1)} %get-tuple-element.40), channel_id=1, source_target_pairs={{0,8},{8,16},{16,24},{24,0},{1,9},{9,17},{17,25},{25,1},{2,10},{10... | collective-permute-start | bytes 491528 | tf_op jit(solution)/shard_map/ppermute | solution.py:500
  14.7 2.7 %collective-permute-start.1 = (f32[5,64,128]{2,1,0:T(8,128)S(1)}, f32[5,64,128]{2,1,0:T(8,128)S(1)}, u32[]{:S(2)}, u32[]{:S(2)}) collective-permute-start(f32[5,64,128]{2,1,0:T(8,128)S(1)} %get-tuple-element.39), channel_id=1, source_target_pairs={{0,16},{8,24},{16,0},{24,8},{1,17},{9,25},{17,1},{25,9},{2,18},{10... | collective-permute-start | bytes 491528 | tf_op jit(solution)/shard_map/ppermute | solution.py:500
  17.4 1.4 %collective-permute-start.2 = (f32[5,64,128]{2,1,0:T(8,128)S(1)}, f32[5,64,128]{2,1,0:T(8,128)S(1)}, u32[]{:S(2)}, u32[]{:S(2)}) collective-permute-start(f32[5,64,128]{2,1,0:T(8,128)S(1)} %get-tuple-element.38), channel_id=1, source_target_pairs={{0,24},{8,0},{16,8},{24,16},{1,25},{9,1},{17,9},{25,17},{2,26},{10... | collective-permute-start | bytes 491528 | tf_op jit(solution)/shard_map/ppermute | solution.py:500
  18.8 1.4 %collective-permute-start.3 = (f32[9,8,128]{2,1,0:T(8,128)}, f32[9,8,128]{2,1,0:T(8,128)S(1)}, u32[]{:S(2)}, u32[]{:S(2)}) collective-permute-start(f32[9,8,128]{2,1,0:T(8,128)} %param.23), channel_id=1, source_target_pairs={{0,0},{1,1},{2,2},{3,3},{7,4},{6,5},{5,6},{4,7},{8,8},{9,9},{10,10... | collective-permute-start | bytes 110600 | tf_op jit(solution)/shard_map/ppermute | solution.py:544
  20.2 0.1 add_convert_fusion.open_ref
  20.3 0.1 copy.25.mode_ref
  20.5 7.9 %node_tables.1 = (bf16[1536,480]{1,0:T(8,128)(2,1)S(1)}, bf16[320,1536]{1,0:T(8,128)(2,1)S(1)}, bf16[1536,48]{1,0:T(8,128)(2,1)S(1)}, bf16[160,480]{1,0:T(8,128)(2,1)S(1)}) custom-call(s32[8,1536]{1,0:T(8,128)S(1)} %pad.13.index_ref, s32[160,8]{1,0:T(8,128)S(1)} %copy.25.mode_ref, f32[1,1536]{1,0:T(1,128)S(1)} %broadcast_in_dim.5.weight_ref), custom_call_target="tpu_custom_call" | custom-call | tf_op jit(solution)/shard_map/node_tables/pallas_call | solution.py:116
  28.4 1.2 %copy-done.1 = bf16[1536,480]{1,0:T(8,128)(2,1)} copy-done((bf16[1536,480]{1,0:T(8,128)(2,1)}, bf16[1536,480]{1,0:T(8,128)(2,1)S(1)}, u32[]{:S(2)}) %copy-start.1) | copy-done | bytes 1474584
  29.5 0.0 collective-permute-done.3
  29.6 0.0 collective-permute-done.s1_ref
  29.6 0.0 collective-permute-done.1.s2_ref
  29.6 0.0 collective-permute-done.2.s3_ref
  29.6 4.9 %all-to-all-done = f32[8,20,8,128]{3,2,1,0:T(8,128)S(1)} async-done(((f32[8,20,8,128]{3,2,1,0:T(8,128)}), f32[8,20,8,128]{3,2,1,0:T(8,128)S(1)}, u32[]{:S(2)}, u32[]{:S(2)}) %all-to-all-start) | async-done | bytes 655392 | tf_op jit(solution)/shard_map/all_to_all | solution.py:531
  34.5 0.5 rim_of.1
  35.0 0.1 collective-permute-start.6
  35.1 1.7 %collective-permute-start.7 = (f32[176,128]{1,0:T(8,128)S(1)}, f32[176,128]{1,0:T(8,128)S(1)}, u32[]{:S(2)}, u32[]{:S(2)}) collective-permute-start(f32[176,128]{1,0:T(8,128)S(1)} %get-tuple-element.27.near_ref), channel_id=1, source_target_pairs={{0,224},{32,0},{64,32},{96,64},{128,96},{160,128},{192,160},{224,1... | collective-permute-start | bytes 270344 | tf_op jit(solution)/shard_map/ppermute | solution.py:500
  36.8 0.2 collective-permute-start.4
  37.1 7.8 %collective-permute-start.5 = (f32[176,128]{1,0:T(8,128)S(1)}, f32[176,128]{1,0:T(8,128)S(1)}, u32[]{:S(2)}, u32[]{:S(2)}) collective-permute-start(f32[176,128]{1,0:T(8,128)S(1)} %get-tuple-element.25.first_ref), channel_id=1, source_target_pairs={{1,0},{2,1},{3,2},{7,3},{6,7},{5,6},{4,5},{8,4},{9,8},{10,9},{11,1... | collective-permute-start | bytes 270344 | tf_op jit(solution)/shard_map/ppermute | solution.py:564
  44.9 10.2 %inner_fluxes.1.g_ref = f32[8,160,128]{2,1,0:T(8,128)S(1)} custom-call(f32[1280,128]{1,0:T(8,128)S(1)} %bitcast.38, bf16[48,1024]{1,0:T(8,128)(2,1)S(1)} %pad_maximum_fusion.log_ref, bf16[1536,480]{1,0:T(8,128)(2,1)} %copy-done.1, bf16[1536,48]{1,0:T(8,128)(2,1)S(1)} %get-tuple-element.22.germ_ref, bf16[320,1536]{1,0:T(8,128)(2,1)S(1)} %get-tuple-element.23.w_ref, ...), custom_call_target="tpu_custom_call" | custom-call | flops 5662310400 | bytes 8388608 | tf_op jit(solution)/shard_map/inner_fluxes/pallas_call | solution.py:268
  55.1 0.0 copy-start.15
  55.1 0.0 copy-start.13
  55.1 0.0 copy-start.14
  55.1 0.0 copy-start.17
  55.1 0.0 collective-permute-done.4.up_ref
  55.1 0.0 collective-permute-done.5.down_ref
  55.1 0.0 collective-permute-done.6.left_ref
  55.1 0.0 collective-permute-done.7.right_ref
  55.1 5.4 %outer_fluxes.1 = f32[1280,128]{1,0:T(8,128)} custom-call(f32[4]{0:T(128)S(1)} %add_convert_fusion.open_ref, f32[8,160,128]{2,1,0:T(8,128)S(1)} %inner_fluxes.1.g_ref, f32[176,128]{1,0:T(8,128)S(1)} %get-tuple-element.25.first_ref, f32[176,128]{1,0:T(8,128)S(1)} %get-tuple-element.26.last_ref, f32[176,128]{1,0:T(8,128)S(1)} %get-tuple-element.27.near_ref, ...), custom_call_target="tpu_custom_call" | custom-call | flops 1132462080 | bytes 8388608 | tf_op jit(solution)/shard_map/outer_fluxes/pallas_call | solution.py:359
  60.6 0.0 copy-start.6
  60.6 4.3 %all-to-all-start.1 = ((f32[32,5,8,128]{3,2,1,0:T(8,128)}), f32[32,5,8,128]{3,2,1,0:T(8,128)S(1)}, u32[]{:S(2)}, u32[]{:S(2)}) async-start(f32[32,5,8,128]{3,2,1,0:T(8,128)} %bitcast.13), calls=%async_computation.1 | async-start | bytes 1310720 | tf_op jit(solution)/shard_map/all_to_all | solution.py:570
  64.9 0.0 copy-done.15
  65.6 0.4 fusion.1
  66.0 0.0 copy-start.4
  66.0 0.0 copy-start.7
  66.1 0.4 fusion.2
  66.5 0.2 convolution_bitcast_fusion
  66.7 0.2 convolution_bitcast_fusion.1
  66.9 0.1 add_divide_fusion.recip_ref
  67.0 20.7 %all-to-all-done.1.part_ref = f32[32,5,8,128]{3,2,1,0:T(8,128)S(1)} async-done(((f32[32,5,8,128]{3,2,1,0:T(8,128)}), f32[32,5,8,128]{3,2,1,0:T(8,128)S(1)}, u32[]{:S(2)}, u32[]{:S(2)}) %all-to-all-start.1) | async-done | bytes 655392 | tf_op jit(solution)/shard_map/all_to_all | solution.py:570
  87.8 3.6 %local_solve.1 = (f32[1280,128]{1,0:T(8,128)S(1)}, f32[8,16,256]{2,1,0:T(8,128)}) custom-call(s32[1]{0:T(128)} %bitcast.place_ref, f32[32,5,8,128]{3,2,1,0:T(8,128)S(1)} %all-to-all-done.1.part_ref, f32[5,64,128]{2,1,0:T(8,128)S(1)} %get-tuple-element.28.s0_ref, f32[5,64,128]{2,1,0:T(8,128)S(1)} %collective-permute-done.s1_ref, ...), custom_call_target="tpu_custom_call" | custom-call | tf_op jit(solution)/shard_map/local_solve/pallas_call | solution.py:581
  91.3 3.4 %all-to-all-start.2 = ((f32[8,16,256]{2,1,0:T(8,128)}), f32[8,16,256]{2,1,0:T(8,128)S(1)}, u32[]{:S(2)}, u32[]{:S(2)}) async-start(f32[8,16,256]{2,1,0:T(8,128)} %get-tuple-element.37), calls=%async_computation.2 | async-start | bytes 262144 | tf_op jit(solution)/shard_map/all_to_all | solution.py:592
  94.7 0.0 copy-done.4
  94.7 0.0 copy-start
  94.7 0.0 copy-start.2
  94.7 3.0 %back.1 = (f32[5,64,128]{2,1,0:T(8,128)S(1)}, f32[5,64,128]{2,1,0:T(8,128)}, f32[5,64,128]{2,1,0:T(8,128)S(1)}, f32[5,64,128]{2,1,0:T(8,128)S(1)}) custom-call(s32[1]{0:T(128)} %bitcast.place_ref, f32[1280,128]{1,0:T(8,128)S(1)} %get-tuple-element.32.scaled_ref, f32[128,128]{1,0:T(8,128)S(1)} %copy-done.7, f32[256,256]{1,0:T(8,128)S(1)} %copy-done.4), custom_call_target="tpu_custom_call" | custom-call | flops 754974720 | bytes 2097152 | tf_op jit(solution)/shard_map/back/pallas_call | solution.py:595
  97.8 1.3 %collective-permute-start.10 = (f32[5,64,128]{2,1,0:T(8,128)S(1)}, f32[5,64,128]{2,1,0:T(8,128)S(1)}, u32[]{:S(2)}, u32[]{:S(2)}) collective-permute-start(f32[5,64,128]{2,1,0:T(8,128)S(1)} %get-tuple-element.36), channel_id=1, source_target_pairs={{0,24},{8,0},{16,8},{24,16},{1,25},{9,1},{17,9},{25,17},{2,26},{10... | collective-permute-start | bytes 491528 | tf_op jit(solution)/shard_map/ppermute | solution.py:500
  99.1 0.7 collective-permute-start.8
  99.8 1.7 %collective-permute-start.9 = (f32[5,64,128]{2,1,0:T(8,128)S(1)}, f32[5,64,128]{2,1,0:T(8,128)S(1)}, u32[]{:S(2)}, u32[]{:S(2)}) collective-permute-start(f32[5,64,128]{2,1,0:T(8,128)S(1)} %get-tuple-element.35), channel_id=1, source_target_pairs={{0,16},{8,24},{16,0},{24,8},{1,17},{9,25},{17,1},{25,9},{2,18},{10... | collective-permute-start | bytes 491528 | tf_op jit(solution)/shard_map/ppermute | solution.py:500
  101.5 0.0 all-to-all-done.2
  101.5 1.7 %collective-permute-start.11 = (f32[16,256]{1,0:T(8,128)S(1)}, f32[16,256]{1,0:T(8,128)S(1)}, u32[]{:S(2)}, u32[]{:S(2)}) collective-permute-start(f32[16,256]{1,0:T(8,128)S(1)} %reduce_sum.9.t0_ref), channel_id=1, source_target_pairs={{0,8},{8,16},{16,24},{24,0},{1,9},{9,17},{17,25},{25,1},{2,10},{10... | collective-permute-start | bytes 49160 | tf_op jit(solution)/shard_map/ppermute | solution.py:500
  103.3 1.3 %collective-permute-start.12 = (f32[16,256]{1,0:T(8,128)S(1)}, f32[16,256]{1,0:T(8,128)S(1)}, u32[]{:S(2)}, u32[]{:S(2)}) collective-permute-start(f32[16,256]{1,0:T(8,128)S(1)} %reduce_sum.9.t0_ref), channel_id=1, source_target_pairs={{0,16},{8,24},{16,0},{24,8},{1,17},{9,25},{17,1},{25,9},{2,18},{10... | collective-permute-start | bytes 49160 | tf_op jit(solution)/shard_map/ppermute | solution.py:500
  104.5 0.1 collective-permute-done.10.p3_ref
  104.6 2.4 %collective-permute-start.13 = (f32[16,256]{1,0:T(8,128)S(1)}, f32[16,256]{1,0:T(8,128)S(1)}, u32[]{:S(2)}, u32[]{:S(2)}) collective-permute-start(f32[16,256]{1,0:T(8,128)S(1)} %reduce_sum.9.t0_ref), channel_id=1, source_target_pairs={{0,24},{8,0},{16,8},{24,16},{1,25},{9,1},{17,9},{25,17},{2,26},{10... | collective-permute-start | bytes 49160 | tf_op jit(solution)/shard_map/ppermute | solution.py:500
  107.0 0.1 copy.26.g_first_ref
  107.1 1.0 copy.27.g_last_ref
  108.1 2.4 %collective-permute-done.8.p1_ref = f32[5,64,128]{2,1,0:T(8,128)S(1)} collective-permute-done((f32[5,64,128]{2,1,0:T(8,128)}, f32[5,64,128]{2,1,0:T(8,128)S(1)}, u32[]{:S(2)}, u32[]{:S(2)}) %collective-permute-start.8) | collective-permute-done | bytes 163872 | tf_op jit(solution)/shard_map/ppermute | solution.py:500
  110.5 0.0 collective-permute-done.9.p2_ref
  110.5 0.2 collective-permute-done.11.t1_ref
  110.7 0.0 collective-permute-done.12.t2_ref
  110.7 0.0 collective-permute-done.13.t3_ref
  110.7 2.8 %final.1 = (f32[20,64,128]{2,1,0:T(8,128)}, f32[20,64,128]{2,1,0:T(8,128)}) custom-call(s32[1]{0:T(128)} %bitcast.place_ref, f32[5,64,128]{2,1,0:T(8,128)S(1)} %get-tuple-element.33.p0_ref, f32[5,64,128]{2,1,0:T(8,128)S(1)} %collective-permute-done.8.p1_ref, f32[5,64,128]{2,1,0:T(8,128)S(1)} %collective-permute-done.9.p2_ref, ...), custom_call_target="tpu_custom_call" | custom-call | tf_op jit(solution)/shard_map/final/pallas_call | solution.py:610
  (37 shorter events, 0.2 us)
Async XLA Ops:
  0.6 12.4 %copy-start.8 = (f32[20,64,128]{2,1,0:T(8,128)S(1)}, f32[20,64,128]{2,1,0:T(8,128)}, u32[]{:S(2)}) copy-start(f32[20,64,128]{2,1,0:T(8,128)} %param.22) | copy-start | bytes 1966084
  2.7 17.6 %copy-start.12 = (s32[160,8]{0,1:T(8,128)S(1)}, s32[160,8]{0,1:T(8,128)}, u32[]{:S(2)}) copy-start(s32[160,8]{0,1:T(8,128)} %param.27) | copy-start | bytes 15364
  2.7 17.7 %copy-start.10 = (s32[1500,8]{0,1:T(8,128)S(1)}, s32[1500,8]{0,1:T(8,128)}, u32[]{:S(2)}) copy-start(s32[1500,8]{0,1:T(8,128)} %param.26) | copy-start | bytes 144004
  2.7 17.8 %copy-start.11 = (f32[1500]{0:T(1024)S(1)}, f32[1500]{0:T(1024)}, u32[]{:S(2)}) copy-start(f32[1500]{0:T(1024)} %param.24) | copy-start | bytes 18004
  2.7 31.9 %all-to-all-start = ((f32[8,20,8,128]{3,2,1,0:T(8,128)}), f32[8,20,8,128]{3,2,1,0:T(8,128)S(1)}, u32[]{:S(2)}, u32[]{:S(2)}) async-start(f32[8,20,8,128]{3,2,1,0:T(8,128)} %dealt.1), calls=%async_computation | async-start | bytes 1310720 | tf_op jit(solution)/shard_map/all_to_all | solution.py:531
  13.1 16.5 %collective-permute-start = (f32[5,64,128]{2,1,0:T(8,128)S(1)}, f32[5,64,128]{2,1,0:T(8,128)S(1)}, u32[]{:S(2)}, u32[]{:S(2)}) collective-permute-start(f32[5,64,128]{2,1,0:T(8,128)S(1)} %get-tuple-element.40), channel_id=1, source_target_pairs={{0,8},{8,16},{16,24},{24,0},{1,9},{9,17},{17,25},{25,1},{2,10},{10... | collective-permute-start | bytes 491528 | tf_op jit(solution)/shard_map/ppermute | solution.py:500
  14.7 15.0 %collective-permute-start.1 = (f32[5,64,128]{2,1,0:T(8,128)S(1)}, f32[5,64,128]{2,1,0:T(8,128)S(1)}, u32[]{:S(2)}, u32[]{:S(2)}) collective-permute-start(f32[5,64,128]{2,1,0:T(8,128)S(1)} %get-tuple-element.39), channel_id=1, source_target_pairs={{0,16},{8,24},{16,0},{24,8},{1,17},{9,25},{17,1},{25,9},{2,18},{10... | collective-permute-start | bytes 491528 | tf_op jit(solution)/shard_map/ppermute | solution.py:500
  17.4 12.2 %collective-permute-start.2 = (f32[5,64,128]{2,1,0:T(8,128)S(1)}, f32[5,64,128]{2,1,0:T(8,128)S(1)}, u32[]{:S(2)}, u32[]{:S(2)}) collective-permute-start(f32[5,64,128]{2,1,0:T(8,128)S(1)} %get-tuple-element.38), channel_id=1, source_target_pairs={{0,24},{8,0},{16,8},{24,16},{1,25},{9,1},{17,9},{25,17},{2,26},{10... | collective-permute-start | bytes 491528 | tf_op jit(solution)/shard_map/ppermute | solution.py:500
  18.8 10.7 %collective-permute-start.3 = (f32[9,8,128]{2,1,0:T(8,128)}, f32[9,8,128]{2,1,0:T(8,128)S(1)}, u32[]{:S(2)}, u32[]{:S(2)}) collective-permute-start(f32[9,8,128]{2,1,0:T(8,128)} %param.23), channel_id=1, source_target_pairs={{0,0},{1,1},{2,2},{3,3},{7,4},{6,5},{5,6},{4,7},{8,8},{9,9},{10,10... | collective-permute-start | bytes 110600 | tf_op jit(solution)/shard_map/ppermute | solution.py:544
  28.4 1.2 %copy-start.1 = (bf16[1536,480]{1,0:T(8,128)(2,1)}, bf16[1536,480]{1,0:T(8,128)(2,1)S(1)}, u32[]{:S(2)}) copy-start(bf16[1536,480]{1,0:T(8,128)(2,1)S(1)} %get-tuple-element.21.basis_ref) | copy-start | bytes 4423684
  35.0 20.1 %collective-permute-start.6 = (f32[176,128]{1,0:T(8,128)S(1)}, f32[176,128]{1,0:T(8,128)S(1)}, u32[]{:S(2)}, u32[]{:S(2)}) collective-permute-start(f32[176,128]{1,0:T(8,128)S(1)} %get-tuple-element.27.near_ref), channel_id=1, source_target_pairs={{0,32},{32,64},{64,96},{96,128},{128,160},{160,192},{192,224},{224... | collective-permute-start | bytes 270344 | tf_op jit(solution)/shard_map/ppermute | solution.py:500
  35.1 20.0 %collective-permute-start.7 = (f32[176,128]{1,0:T(8,128)S(1)}, f32[176,128]{1,0:T(8,128)S(1)}, u32[]{:S(2)}, u32[]{:S(2)}) collective-permute-start(f32[176,128]{1,0:T(8,128)S(1)} %get-tuple-element.27.near_ref), channel_id=1, source_target_pairs={{0,224},{32,0},{64,32},{96,64},{128,96},{160,128},{192,160},{224,1... | collective-permute-start | bytes 270344 | tf_op jit(solution)/shard_map/ppermute | solution.py:500
  36.8 18.3 %collective-permute-start.4 = (f32[176,128]{1,0:T(8,128)S(1)}, f32[176,128]{1,0:T(8,128)S(1)}, u32[]{:S(2)}, u32[]{:S(2)}) collective-permute-start(f32[176,128]{1,0:T(8,128)S(1)} %get-tuple-element.26.last_ref), channel_id=1, source_target_pairs={{0,1},{1,2},{2,3},{3,7},{7,6},{6,5},{5,4},{4,8},{8,9},{9,10},{10,1... | collective-permute-start | bytes 270344 | tf_op jit(solution)/shard_map/ppermute | solution.py:563
  37.1 18.0 %collective-permute-start.5 = (f32[176,128]{1,0:T(8,128)S(1)}, f32[176,128]{1,0:T(8,128)S(1)}, u32[]{:S(2)}, u32[]{:S(2)}) collective-permute-start(f32[176,128]{1,0:T(8,128)S(1)} %get-tuple-element.25.first_ref), channel_id=1, source_target_pairs={{1,0},{2,1},{3,2},{7,3},{6,7},{5,6},{4,5},{8,4},{9,8},{10,9},{11,1... | collective-permute-start | bytes 270344 | tf_op jit(solution)/shard_map/ppermute | solution.py:564
  55.1 9.8 %copy-start.15 = (f32[9,7]{1,0:T(8,128)S(1)}, f32[9,7]{1,0:T(8,128)}, u32[]{:S(2)}) copy-start(f32[9,7]{1,0:T(8,128)} %constant.105.clone) | copy-start | bytes 760
  55.1 10.5 %copy-start.13 = (f32[256]{0:T(256)S(1)}, f32[256]{0:T(256)}, u32[]{:S(2)}) copy-start(f32[256]{0:T(256)} %constant.100.clone) | copy-start | bytes 3076
  55.1 10.5 %copy-start.14 = (f32[128]{0:T(128)S(1)}, f32[128]{0:T(128)}, u32[]{:S(2)}) copy-start(f32[128]{0:T(128)} %constant.101.clone) | copy-start | bytes 1540
  55.1 10.5 %copy-start.17 = (f32[128,128]{1,0:T(8,128)S(1)}, f32[128,128]{1,0:T(8,128)}, u32[]{:S(2)}) copy-start(f32[128,128]{1,0:T(8,128)} %constant.103.clone) | copy-start | bytes 196612
  60.6 5.4 %copy-start.16 = (f32[128,128]{1,0:T(8,128)S(1)}, f32[128,128]{1,0:T(8,128)}, u32[]{:S(2)}) copy-start(f32[128,128]{1,0:T(8,128)} %constant.102.clone) | copy-start | bytes 196612
  60.6 5.9 %copy-start.18 = (f32[7]{0:T(128)S(1)}, f32[7]{0:T(128)}, u32[]{:S(2)}) copy-start(f32[7]{0:T(128)} %constant.104.clone) | copy-start | bytes 88
  60.6 27.2 %copy-start.3 = (f32[256,256]{1,0:T(8,128)S(1)}, f32[256,256]{1,0:T(8,128)}, u32[]{:S(2)}) copy-start(f32[256,256]{1,0:T(8,128)} %constant.106.clone.cy_ref) | copy-start | bytes 786436
  60.6 27.2 %copy-start.5 = (f32[128,128]{1,0:T(8,128)S(1)}, f32[128,128]{1,0:T(8,128)}, u32[]{:S(2)}) copy-start(f32[128,128]{1,0:T(8,128)} %constant.107.clone.cxt_ref) | copy-start | bytes 196612
  60.6 27.2 %copy-start.6 = (f32[8,128]{1,0:T(8,128)S(1)}, f32[8,128]{1,0:T(8,128)}, u32[]{:S(2)}) copy-start(f32[8,128]{1,0:T(8,128)} %constant.108.clone.ends_of_ref) | copy-start | bytes 12292
  60.6 27.1 %all-to-all-start.1 = ((f32[32,5,8,128]{3,2,1,0:T(8,128)}), f32[32,5,8,128]{3,2,1,0:T(8,128)S(1)}, u32[]{:S(2)}, u32[]{:S(2)}) async-start(f32[32,5,8,128]{3,2,1,0:T(8,128)} %bitcast.13), calls=%async_computation.1 | async-start | bytes 1310720 | tf_op jit(solution)/shard_map/all_to_all | solution.py:570
  66.0 0.9 copy-start.9
  66.0 28.7 %copy-start.4 = (f32[256,256]{1,0:T(8,128)S(1)}, f32[256,256]{1,0:T(8,128)}, u32[]{:S(2)}) copy-start(f32[256,256]{1,0:T(8,128)} %constant.110.clone.cyt_ref) | copy-start | bytes 786436
  66.0 28.7 %copy-start.7 = (f32[128,128]{1,0:T(8,128)S(1)}, f32[128,128]{1,0:T(8,128)}, u32[]{:S(2)}) copy-start(f32[128,128]{1,0:T(8,128)} %constant.109.clone.cx_ref) | copy-start | bytes 196612
  91.3 10.2 %all-to-all-start.2 = ((f32[8,16,256]{2,1,0:T(8,128)}), f32[8,16,256]{2,1,0:T(8,128)S(1)}, u32[]{:S(2)}, u32[]{:S(2)}) async-start(f32[8,16,256]{2,1,0:T(8,128)} %get-tuple-element.37), calls=%async_computation.2 | async-start | bytes 262144 | tf_op jit(solution)/shard_map/all_to_all | solution.py:592
  94.7 16.0 %copy-start = (f32[20,64,128]{2,1,0:T(8,128)S(1)}, f32[20,64,128]{2,1,0:T(8,128)}, u32[]{:S(2)}) copy-start(f32[20,64,128]{2,1,0:T(8,128)} %now_hbm.1) | copy-start | bytes 1966084
  94.7 16.0 %copy-start.2 = (f32[20,64,128]{2,1,0:T(8,128)S(1)}, f32[20,64,128]{2,1,0:T(8,128)}, u32[]{:S(2)}) copy-start(f32[20,64,128]{2,1,0:T(8,128)} %before_hbm.1) | copy-start | bytes 1966084
  97.8 6.9 %collective-permute-start.10 = (f32[5,64,128]{2,1,0:T(8,128)S(1)}, f32[5,64,128]{2,1,0:T(8,128)S(1)}, u32[]{:S(2)}, u32[]{:S(2)}) collective-permute-start(f32[5,64,128]{2,1,0:T(8,128)S(1)} %get-tuple-element.36), channel_id=1, source_target_pairs={{0,24},{8,0},{16,8},{24,16},{1,25},{9,1},{17,9},{25,17},{2,26},{10... | collective-permute-start | bytes 491528 | tf_op jit(solution)/shard_map/ppermute | solution.py:500
  99.1 11.4 %collective-permute-start.8 = (f32[5,64,128]{2,1,0:T(8,128)}, f32[5,64,128]{2,1,0:T(8,128)S(1)}, u32[]{:S(2)}, u32[]{:S(2)}) collective-permute-start(f32[5,64,128]{2,1,0:T(8,128)} %get-tuple-element.34), channel_id=1, source_target_pairs={{0,8},{8,16},{16,24},{24,0},{1,9},{9,17},{17,25},{25,1},{2,10},{10... | collective-permute-start | bytes 491528 | tf_op jit(solution)/shard_map/ppermute | solution.py:500
  99.8 10.7 %collective-permute-start.9 = (f32[5,64,128]{2,1,0:T(8,128)S(1)}, f32[5,64,128]{2,1,0:T(8,128)S(1)}, u32[]{:S(2)}, u32[]{:S(2)}) collective-permute-start(f32[5,64,128]{2,1,0:T(8,128)S(1)} %get-tuple-element.35), channel_id=1, source_target_pairs={{0,16},{8,24},{16,0},{24,8},{1,17},{9,25},{17,1},{25,9},{2,18},{10... | collective-permute-start | bytes 491528 | tf_op jit(solution)/shard_map/ppermute | solution.py:500
  101.5 9.2 %collective-permute-start.11 = (f32[16,256]{1,0:T(8,128)S(1)}, f32[16,256]{1,0:T(8,128)S(1)}, u32[]{:S(2)}, u32[]{:S(2)}) collective-permute-start(f32[16,256]{1,0:T(8,128)S(1)} %reduce_sum.9.t0_ref), channel_id=1, source_target_pairs={{0,8},{8,16},{16,24},{24,0},{1,9},{9,17},{17,25},{25,1},{2,10},{10... | collective-permute-start | bytes 49160 | tf_op jit(solution)/shard_map/ppermute | solution.py:500
  103.3 7.4 %collective-permute-start.12 = (f32[16,256]{1,0:T(8,128)S(1)}, f32[16,256]{1,0:T(8,128)S(1)}, u32[]{:S(2)}, u32[]{:S(2)}) collective-permute-start(f32[16,256]{1,0:T(8,128)S(1)} %reduce_sum.9.t0_ref), channel_id=1, source_target_pairs={{0,16},{8,24},{16,0},{24,8},{1,17},{9,25},{17,1},{25,9},{2,18},{10... | collective-permute-start | bytes 49160 | tf_op jit(solution)/shard_map/ppermute | solution.py:500
  104.6 6.1 %collective-permute-start.13 = (f32[16,256]{1,0:T(8,128)S(1)}, f32[16,256]{1,0:T(8,128)S(1)}, u32[]{:S(2)}, u32[]{:S(2)}) collective-permute-start(f32[16,256]{1,0:T(8,128)S(1)} %reduce_sum.9.t0_ref), channel_id=1, source_target_pairs={{0,24},{8,0},{16,8},{24,16},{1,25},{9,1},{17,9},{25,17},{2,26},{10... | collective-permute-start | bytes 49160 | tf_op jit(solution)/shard_map/ppermute | solution.py:500

commit v8 on v7

--- a/solution.py
+++ b/solution.py
@@ -413,13 +413,20 @@
     scaled_ref[...] = scaled
 
 
+def dot_in_halves(a, b):
+    a, b = split(a), split(b)
+    out = jnp.dot(a[0], b[0], preferred_element_type=jnp.float32)
+    out = out + jnp.dot(a[1], b[0], preferred_element_type=jnp.float32)
+    return out + jnp.dot(a[0], b[1], preferred_element_type=jnp.float32)
+
+
 def back_kernel(place_ref, scaled_ref, cx_ref, cyt_ref, p0_ref, p1_ref, p2_ref, p3_ref, rows_ref):
     modes, length, cols = p0_ref.shape
     ny = cyt_ref.shape[0]
     ngy = ny // length
-    z = jnp.dot(scaled_ref[...], cx_ref[...], precision=HIGHEST, preferred_element_type=jnp.float32)
+    z = dot_in_halves(scaled_ref[...], cx_ref[...])
     z = jnp.concatenate([z[m * ny : (m + 1) * ny] for m in range(modes)], axis=1)
-    rows_ref[...] = jnp.dot(cyt_ref[...], z, precision=HIGHEST, preferred_element_type=jnp.float32)
+    rows_ref[...] = dot_in_halves(cyt_ref[...], z)
     for d, out_ref in enumerate((p0_ref, p1_ref, p2_ref, p3_ref)):
         g = lax.rem(place_ref[0] + d, ngy)
         span = pl.ds(pl.multiple_of(g * length, 8), length)
@@ -500,6 +507,15 @@
     return lax.ppermute(x, axis, [(i, (i + by) % count) for i in range(count)])
 
 
+def pairs(chain, shift):
+    chain = list(chain)
+    found = [(d, d) for d in chain[:shift]]
+    for k in range(shift, len(chain), 2):
+        two = chain[k : k + 2]
+        found += list(zip(two, two[::-1]))
+    return found
+
+
 def dealt_kernel(order, x_ref, out_ref):
     rows = out_ref.shape[2]
     for k, block in enumerate(order):
@@ -545,7 +561,6 @@
         log_fields, row_axis, [(g * nsa + order[i], g * nsa + i) for g in range(ngy) for i in range(nsa)]
     )
     chain = [g * nsa + order.index(k) for g in range(ngy) for k in range(nsa)]
-    ring = [(a, b) for a, b in zip(chain, chain[1:] + chain[:1])]
     col_index = lax.axis_index("gx")
     opened = jnp.stack(
         [row_index > 0, row_index < ngy * nsa - 1, col_index > 0, col_index < ngx - 1]
@@ -559,11 +574,15 @@
     field, *pieces = lax.optimization_barrier((field, *pieces))
     rims = rim_of(rows, field, scaled_logs.reshape(SLOT * rows, cols))
     first, last, near = rims
+    even_row, even_col = row_index % 2 == 0, col_index % 2 == 0
+    sent = jnp.where(even_row, last, first), jnp.where(even_row, first, last)
+    rows_got = [lax.ppermute(x, row_axis, pairs(chain, k)) for k, x in enumerate(sent)]
+    cols_got = [lax.ppermute(near, "gx", pairs(range(ngx), k)) for k in range(2)]
     halos = (
-        lax.ppermute(last, row_axis, ring),
-        lax.ppermute(first, row_axis, [(b, a) for a, b in ring]),
-        rotated(near, "gx", 1),
-        rotated(near, "gx", -1),
+        jnp.where(even_row, rows_got[1], rows_got[0]),
+        jnp.where(even_row, rows_got[0], rows_got[1]),
+        jnp.where(even_col, cols_got[1], cols_got[0]),
+        jnp.where(even_col, cols_got[0], cols_got[1]),
     )
     inner = inner_fluxes(rows, field, logs, basis_cat, weight_cat, germ_cat, mass_cat)
     galerkin = outer_fluxes(rows, opened, inner, rims, halos, basis_cat, weight_cat, germ_cat)

time: 115 us -> 117 us (1.017)
  waiting for transfers between devices: 28.3 us -> 30.2 us
  starting transfers between devices: 44.1 us -> 45.8 us
    all_to_all x1, starting transfers between devices: 4.27 us -> 13.2 us  [on_device(): lax.all_to_all(galerkin.reshape(nsa * ngy, sub, rows, cols), ('sa', 'gy')...]
    ppermute x2 -> x4, starting transfers between devices: 8.04 us -> 3.16 us  [the longest x2 2.01 us: on_device(): lax.ppermute(near, 'gx', pairs(range(ngx), k))]
    ppermute x11 -> x9, waiting for transfers between devices: 2.71 us -> 7.02 us  [rotated(): return lax.ppermute(x, axis, [(i, (i + by) % count) for i in range(count)])]
    ppermute x11 -> x9, starting transfers between devices: 16.7 us -> 12.6 us  [rotated(): return lax.ppermute(x, axis, [(i, (i + by) % count) for i in range(count)])]
    all_to_all x1, waiting for transfers between devices: 20.7 us -> 18.3 us  [on_device(): lax.all_to_all(galerkin.reshape(nsa * ngy, sub, rows, cols), ('sa', 'gy')...]
    all_to_all x1, starting transfers between devices: 3.36 us -> 5.11 us  [on_device(): jumps = lax.all_to_all(jumps, 'gx', 0, 0, tiled=True)]
  transfers between devices with their start and end apart: 17 -> 17, of which waited for: 5 -> 4; matrix products, arithmetic and copies ran while one was open for 2% -> 2% of each run, Pallas kernels for 19% -> 17%
where the time goes in v8:
time: 117 us; the launch traced here: 116 us
  starting transfers between devices  45.8 us (39%)
  Pallas kernels  34.4 us (29%)
  waiting for transfers between devices  30.2 us (26%)
  local copies, waits for them, and re-layouts  2.53 us (2%)
  between operations  2.01 us (2%)
    all_to_all x1, waiting for transfers between devices, on_device(): lax.all_to_all(galerkin.reshape(nsa * ngy, sub, rows, cols), ('sa', 'gy')...  18.3 us
    all_to_all x1, starting transfers between devices, on_device(): lax.all_to_all(galerkin.reshape(nsa * ngy, sub, rows, cols), ('sa', 'gy')...  13.2 us
    ppermute x9, starting transfers between devices, rotated(): return lax.ppermute(x, axis, [(i, (i + by) % count) for i in range(count)])  12.6 us
    all_to_all x1, starting transfers between devices, on_device(): lax.all_to_all(outgoing, 'sa', 0, 0, tiled=True).reshape(p * rows, cols)  10.3 us
    pallas_call x1, Pallas kernels, inner_fluxes(): pl.pallas_call(functools.partial(inner_kernel, rows), out_shape=jax.Shape...  10.2 us
    pallas_call x1, Pallas kernels, node_tables(): pl.pallas_call(tables_kernel, grid=((q + pad) // QB,), in_specs=[pl.Block...  7.87 us
    ppermute x9, waiting for transfers between devices, rotated(): return lax.ppermute(x, axis, [(i, (i + by) % count) for i in range(count)])  7.02 us
    pallas_call x1, Pallas kernels, outer_fluxes(): pl.pallas_call(functools.partial(outer_kernel, rows), in_specs=[pl.BlockS...  5.46 us
  transfers between devices with their start and end apart: 17, of which 4 were waited for; matrix products, arithmetic and copies ran while one was open for 2% of the time, Pallas kernels for 17%

profile of v8, /device:TPU:32, one launch (start us, length us, event | category | flops | bytes accessed | tf_op | source)
XLA Modules:
  0.0 116.4 jit_solution(13205861143333495576)
XLA Ops:
  0.6 2.0 %dealt.1 = f32[8,20,8,128]{3,2,1,0:T(8,128)} custom-call(f32[20,64,128]{2,1,0:T(8,128)} %now_hbm.1), custom_call_target="tpu_custom_call" | custom-call | tf_op jit(solution)/shard_map/dealt/pallas_call | solution.py:527
  2.7 10.3 %all-to-all-start = ((f32[8,20,8,128]{3,2,1,0:T(8,128)}), f32[8,20,8,128]{3,2,1,0:T(8,128)S(1)}, u32[]{:S(2)}, u32[]{:S(2)}) async-start(f32[8,20,8,128]{3,2,1,0:T(8,128)} %dealt.1), calls=%async_computation | async-start | bytes 1310720 | tf_op jit(solution)/shard_map/all_to_all | solution.py:547
  13.0 0.1 dynamic-slice_bitcast_fusion
  13.1 1.6 %collective-permute-start = (f32[5,64,128]{2,1,0:T(8,128)S(1)}, f32[5,64,128]{2,1,0:T(8,128)S(1)}, u32[]{:S(2)}, u32[]{:S(2)}) collective-permute-start(f32[5,64,128]{2,1,0:T(8,128)S(1)} %get-tuple-element.40), channel_id=1, source_target_pairs={{0,8},{8,16},{16,24},{24,0},{1,9},{9,17},{17,25},{25,1},{2,10},{10... | collective-permute-start | bytes 491528 | tf_op jit(solution)/shard_map/ppermute | solution.py:507
  14.7 2.7 %collective-permute-start.1 = (f32[5,64,128]{2,1,0:T(8,128)S(1)}, f32[5,64,128]{2,1,0:T(8,128)S(1)}, u32[]{:S(2)}, u32[]{:S(2)}) collective-permute-start(f32[5,64,128]{2,1,0:T(8,128)S(1)} %get-tuple-element.39), channel_id=1, source_target_pairs={{0,16},{8,24},{16,0},{24,8},{1,17},{9,25},{17,1},{25,9},{2,18},{10... | collective-permute-start | bytes 491528 | tf_op jit(solution)/shard_map/ppermute | solution.py:507
  17.4 1.4 %collective-permute-start.2 = (f32[5,64,128]{2,1,0:T(8,128)S(1)}, f32[5,64,128]{2,1,0:T(8,128)S(1)}, u32[]{:S(2)}, u32[]{:S(2)}) collective-permute-start(f32[5,64,128]{2,1,0:T(8,128)S(1)} %get-tuple-element.38), channel_id=1, source_target_pairs={{0,24},{8,0},{16,8},{24,16},{1,25},{9,1},{17,9},{25,17},{2,26},{10... | collective-permute-start | bytes 491528 | tf_op jit(solution)/shard_map/ppermute | solution.py:507
  18.8 1.4 %collective-permute-start.3 = (f32[9,8,128]{2,1,0:T(8,128)}, f32[9,8,128]{2,1,0:T(8,128)S(1)}, u32[]{:S(2)}, u32[]{:S(2)}) collective-permute-start(f32[9,8,128]{2,1,0:T(8,128)} %param.23), channel_id=1, source_target_pairs={{0,0},{1,1},{2,2},{3,3},{7,4},{6,5},{5,6},{4,7},{8,8},{9,9},{10,10... | collective-permute-start | bytes 110600 | tf_op jit(solution)/shard_map/ppermute | solution.py:560
  20.2 0.1 add_convert_fusion.open_ref
  20.3 0.1 copy.25.mode_ref
  20.5 7.9 %node_tables.1 = (bf16[1536,480]{1,0:T(8,128)(2,1)S(1)}, bf16[320,1536]{1,0:T(8,128)(2,1)S(1)}, bf16[1536,48]{1,0:T(8,128)(2,1)S(1)}, bf16[160,480]{1,0:T(8,128)(2,1)S(1)}) custom-call(s32[8,1536]{1,0:T(8,128)S(1)} %pad.13.index_ref, s32[160,8]{1,0:T(8,128)S(1)} %copy.25.mode_ref, f32[1,1536]{1,0:T(1,128)S(1)} %broadcast_in_dim.5.weight_ref), custom_call_target="tpu_custom_call" | custom-call | tf_op jit(solution)/shard_map/node_tables/pallas_call | solution.py:116
  28.4 1.2 copy-done.1
  29.6 0.0 collective-permute-done.3
  29.6 0.0 collective-permute-done.s1_ref
  29.6 0.0 collective-permute-done.1.s2_ref
  29.6 0.0 collective-permute-done.2.s3_ref
  29.7 4.9 %all-to-all-done = f32[8,20,8,128]{3,2,1,0:T(8,128)S(1)} async-done(((f32[8,20,8,128]{3,2,1,0:T(8,128)}), f32[8,20,8,128]{3,2,1,0:T(8,128)S(1)}, u32[]{:S(2)}, u32[]{:S(2)}) %all-to-all-start) | async-done | bytes 655392 | tf_op jit(solution)/shard_map/all_to_all | solution.py:547
  34.5 0.5 rim_of.1
  35.0 0.1 collective-permute-start.7
  35.1 1.9 %collective-permute-start.6 = (f32[176,128]{1,0:T(8,128)S(1)}, f32[176,128]{1,0:T(8,128)S(1)}, u32[]{:S(2)}, u32[]{:S(2)}) collective-permute-start(f32[176,128]{1,0:T(8,128)S(1)} %get-tuple-element.27.near_ref), channel_id=1, source_target_pairs={{0,0},{32,64},{64,32},{96,128},{128,96},{160,192},{192,160},{224,2... | collective-permute-start | bytes 270344 | tf_op jit(solution)/shard_map/ppermute | solution.py:580
  37.1 0.3 collective-permute-start.5
  37.4 0.8 collective-permute-start.4
  38.2 10.2 %inner_fluxes.1.g_ref = f32[8,160,128]{2,1,0:T(8,128)S(1)} custom-call(f32[1280,128]{1,0:T(8,128)S(1)} %bitcast.38, bf16[48,1024]{1,0:T(8,128)(2,1)S(1)} %pad_maximum_fusion.log_ref, bf16[1536,480]{1,0:T(8,128)(2,1)} %copy-done.1, bf16[1536,48]{1,0:T(8,128)(2,1)S(1)} %get-tuple-element.22.germ_ref, bf16[320,1536]{1,0:T(8,128)(2,1)S(1)} %get-tuple-element.23.w_ref, ...), custom_call_target="tpu_custom_call" | custom-call | flops 5662310400 | bytes 8388608 | tf_op jit(solution)/shard_map/inner_fluxes/pallas_call | solution.py:268
  48.4 0.0 collective-permute-done.5
  48.4 0.0 collective-permute-done.4
  48.4 0.0 collective-permute-done.7
  48.5 0.0 collective-permute-done.6
  48.5 0.0 copy-start.15
  48.5 0.0 copy-start.13
  48.5 0.0 copy-start.14
  48.5 0.0 copy-start.17
  48.5 5.5 %outer_fluxes.1 = f32[1280,128]{1,0:T(8,128)} custom-call(f32[4]{0:T(128)S(1)} %add_convert_fusion.open_ref, f32[8,160,128]{2,1,0:T(8,128)S(1)} %inner_fluxes.1.g_ref, f32[176,128]{1,0:T(8,128)S(1)} %get-tuple-element.25.first_ref, f32[176,128]{1,0:T(8,128)S(1)} %get-tuple-element.26.last_ref, f32[176,128]{1,0:T(8,128)S(1)} %get-tuple-element.27.near_ref, ...), custom_call_target="tpu_custom_call" | custom-call | flops 1132462080 | bytes 8388608 | tf_op jit(solution)/shard_map/outer_fluxes/pallas_call | solution.py:359
  54.0 0.0 copy-start.6
  54.0 13.2 %all-to-all-start.1 = ((f32[32,5,8,128]{3,2,1,0:T(8,128)}), f32[32,5,8,128]{3,2,1,0:T(8,128)S(1)}, u32[]{:S(2)}, u32[]{:S(2)}) async-start(f32[32,5,8,128]{3,2,1,0:T(8,128)} %bitcast.13), calls=%async_computation.1 | async-start | bytes 1310720 | tf_op jit(solution)/shard_map/all_to_all | solution.py:589
  68.0 0.4 fusion.1
  68.4 0.0 copy-start.4
  68.4 0.0 copy-start.7
  68.4 0.4 fusion.2
  68.8 0.0 copy-done.18
  68.8 0.2 convolution_bitcast_fusion
  69.0 0.2 convolution_bitcast_fusion.1
  69.3 0.1 add_divide_fusion.recip_ref
  69.4 18.3 %all-to-all-done.1.part_ref = f32[32,5,8,128]{3,2,1,0:T(8,128)S(1)} async-done(((f32[32,5,8,128]{3,2,1,0:T(8,128)}), f32[32,5,8,128]{3,2,1,0:T(8,128)S(1)}, u32[]{:S(2)}, u32[]{:S(2)}) %all-to-all-start.1) | async-done | bytes 655392 | tf_op jit(solution)/shard_map/all_to_all | solution.py:589
  87.6 0.0 copy-done.3
  87.6 3.6 %local_solve.1 = (f32[1280,128]{1,0:T(8,128)S(1)}, f32[8,16,256]{2,1,0:T(8,128)}) custom-call(s32[1]{0:T(128)} %bitcast.place_ref, f32[32,5,8,128]{3,2,1,0:T(8,128)S(1)} %all-to-all-done.1.part_ref, f32[5,64,128]{2,1,0:T(8,128)S(1)} %get-tuple-element.28.s0_ref, f32[5,64,128]{2,1,0:T(8,128)S(1)} %collective-permute-done.s1_ref, ...), custom_call_target="tpu_custom_call" | custom-call | tf_op jit(solution)/shard_map/local_solve/pallas_call | solution.py:600
  91.2 5.1 %all-to-all-start.2 = ((f32[8,16,256]{2,1,0:T(8,128)}), f32[8,16,256]{2,1,0:T(8,128)S(1)}, u32[]{:S(2)}, u32[]{:S(2)}) async-start(f32[8,16,256]{2,1,0:T(8,128)} %get-tuple-element.37), calls=%async_computation.2 | async-start | bytes 262144 | tf_op jit(solution)/shard_map/all_to_all | solution.py:611
  96.4 0.0 copy-start
  96.4 0.0 copy-start.2
  96.4 1.9 %back.1 = (f32[5,64,128]{2,1,0:T(8,128)S(1)}, f32[5,64,128]{2,1,0:T(8,128)S(1)}, f32[5,64,128]{2,1,0:T(8,128)}, f32[5,64,128]{2,1,0:T(8,128)S(1)}) custom-call(s32[1]{0:T(128)} %bitcast.place_ref, f32[1280,128]{1,0:T(8,128)S(1)} %get-tuple-element.32.scaled_ref, f32[128,128]{1,0:T(8,128)S(1)} %copy-done.7, f32[256,256]{1,0:T(8,128)S(1)} %copy-done.4), custom_call_target="tpu_custom_call" | custom-call | flops 754974720 | bytes 2097152 | tf_op jit(solution)/shard_map/back/pallas_call | solution.py:614
  98.3 0.9 collective-permute-start.8
  99.2 2.2 %collective-permute-start.9 = (f32[5,64,128]{2,1,0:T(8,128)}, f32[5,64,128]{2,1,0:T(8,128)S(1)}, u32[]{:S(2)}, u32[]{:S(2)}) collective-permute-start(f32[5,64,128]{2,1,0:T(8,128)} %get-tuple-element.35), channel_id=1, source_target_pairs={{0,16},{8,24},{16,0},{24,8},{1,17},{9,25},{17,1},{25,9},{2,18},{10... | collective-permute-start | bytes 491528 | tf_op jit(solution)/shard_map/ppermute | solution.py:507
  101.4 1.6 %collective-permute-start.10 = (f32[5,64,128]{2,1,0:T(8,128)S(1)}, f32[5,64,128]{2,1,0:T(8,128)S(1)}, u32[]{:S(2)}, u32[]{:S(2)}) collective-permute-start(f32[5,64,128]{2,1,0:T(8,128)S(1)} %get-tuple-element.36), channel_id=1, source_target_pairs={{0,24},{8,0},{16,8},{24,16},{1,25},{9,1},{17,9},{25,17},{2,26},{10... | collective-permute-start | bytes 491528 | tf_op jit(solution)/shard_map/ppermute | solution.py:507
  103.0 0.0 all-to-all-done.2
  103.1 0.5 collective-permute-start.11
  103.5 1.7 %collective-permute-start.12 = (f32[16,256]{1,0:T(8,128)S(1)}, f32[16,256]{1,0:T(8,128)S(1)}, u32[]{:S(2)}, u32[]{:S(2)}) collective-permute-start(f32[16,256]{1,0:T(8,128)S(1)} %reduce_sum.9.t0_ref), channel_id=1, source_target_pairs={{0,16},{8,24},{16,0},{24,8},{1,17},{9,25},{17,1},{25,9},{2,18},{10... | collective-permute-start | bytes 49160 | tf_op jit(solution)/shard_map/ppermute | solution.py:507
  105.2 4.4 %collective-permute-done.8.p1_ref = f32[5,64,128]{2,1,0:T(8,128)S(1)} collective-permute-done((f32[5,64,128]{2,1,0:T(8,128)S(1)}, f32[5,64,128]{2,1,0:T(8,128)S(1)}, u32[]{:S(2)}, u32[]{:S(2)}) %collective-permute-start.8) | collective-permute-done | bytes 163872 | tf_op jit(solution)/shard_map/ppermute | solution.py:507
  109.6 0.0 collective-permute-start.13
  109.6 0.1 copy.26.g_first_ref
  109.7 1.0 copy.27.g_last_ref
  110.7 0.0 collective-permute-done.9.p2_ref
  110.7 0.0 collective-permute-done.10.p3_ref
  110.7 0.0 collective-permute-done.11.t1_ref
  110.8 0.0 collective-permute-done.12.t2_ref
  110.8 2.6 %collective-permute-done.13.t3_ref = f32[16,256]{1,0:T(8,128)S(1)} collective-permute-done((f32[16,256]{1,0:T(8,128)S(1)}, f32[16,256]{1,0:T(8,128)S(1)}, u32[]{:S(2)}, u32[]{:S(2)}) %collective-permute-start.13) | collective-permute-done | bytes 16416 | tf_op jit(solution)/shard_map/ppermute | solution.py:507
  113.4 2.8 %final.1 = (f32[20,64,128]{2,1,0:T(8,128)}, f32[20,64,128]{2,1,0:T(8,128)}) custom-call(s32[1]{0:T(128)} %bitcast.place_ref, f32[5,64,128]{2,1,0:T(8,128)S(1)} %get-tuple-element.33.p0_ref, f32[5,64,128]{2,1,0:T(8,128)S(1)} %collective-permute-done.8.p1_ref, f32[5,64,128]{2,1,0:T(8,128)S(1)} %collective-permute-done.9.p2_ref, ...), custom_call_target="tpu_custom_call" | custom-call | tf_op jit(solution)/shard_map/final/pallas_call | solution.py:629
  (40 shorter events, 0.2 us)
Async XLA Ops:
  0.6 12.4 %copy-start.8 = (f32[20,64,128]{2,1,0:T(8,128)S(1)}, f32[20,64,128]{2,1,0:T(8,128)}, u32[]{:S(2)}) copy-start(f32[20,64,128]{2,1,0:T(8,128)} %param.22) | copy-start | bytes 1966084
  2.7 17.6 %copy-start.10 = (s32[1500,8]{0,1:T(8,128)S(1)}, s32[1500,8]{0,1:T(8,128)}, u32[]{:S(2)}) copy-start(s32[1500,8]{0,1:T(8,128)} %param.26) | copy-start | bytes 144004
  2.7 17.7 %copy-start.12 = (s32[160,8]{0,1:T(8,128)S(1)}, s32[160,8]{0,1:T(8,128)}, u32[]{:S(2)}) copy-start(s32[160,8]{0,1:T(8,128)} %param.27) | copy-start | bytes 15364
  2.7 17.8 %copy-start.11 = (f32[1500]{0:T(1024)S(1)}, f32[1500]{0:T(1024)}, u32[]{:S(2)}) copy-start(f32[1500]{0:T(1024)} %param.24) | copy-start | bytes 18004
  2.7 31.9 %all-to-all-start = ((f32[8,20,8,128]{3,2,1,0:T(8,128)}), f32[8,20,8,128]{3,2,1,0:T(8,128)S(1)}, u32[]{:S(2)}, u32[]{:S(2)}) async-start(f32[8,20,8,128]{3,2,1,0:T(8,128)} %dealt.1), calls=%async_computation | async-start | bytes 1310720 | tf_op jit(solution)/shard_map/all_to_all | solution.py:547
  13.1 16.5 %collective-permute-start = (f32[5,64,128]{2,1,0:T(8,128)S(1)}, f32[5,64,128]{2,1,0:T(8,128)S(1)}, u32[]{:S(2)}, u32[]{:S(2)}) collective-permute-start(f32[5,64,128]{2,1,0:T(8,128)S(1)} %get-tuple-element.40), channel_id=1, source_target_pairs={{0,8},{8,16},{16,24},{24,0},{1,9},{9,17},{17,25},{25,1},{2,10},{10... | collective-permute-start | bytes 491528 | tf_op jit(solution)/shard_map/ppermute | solution.py:507
  14.7 15.0 %collective-permute-start.1 = (f32[5,64,128]{2,1,0:T(8,128)S(1)}, f32[5,64,128]{2,1,0:T(8,128)S(1)}, u32[]{:S(2)}, u32[]{:S(2)}) collective-permute-start(f32[5,64,128]{2,1,0:T(8,128)S(1)} %get-tuple-element.39), channel_id=1, source_target_pairs={{0,16},{8,24},{16,0},{24,8},{1,17},{9,25},{17,1},{25,9},{2,18},{10... | collective-permute-start | bytes 491528 | tf_op jit(solution)/shard_map/ppermute | solution.py:507
  17.4 12.3 %collective-permute-start.2 = (f32[5,64,128]{2,1,0:T(8,128)S(1)}, f32[5,64,128]{2,1,0:T(8,128)S(1)}, u32[]{:S(2)}, u32[]{:S(2)}) collective-permute-start(f32[5,64,128]{2,1,0:T(8,128)S(1)} %get-tuple-element.38), channel_id=1, source_target_pairs={{0,24},{8,0},{16,8},{24,16},{1,25},{9,1},{17,9},{25,17},{2,26},{10... | collective-permute-start | bytes 491528 | tf_op jit(solution)/shard_map/ppermute | solution.py:507
  18.8 10.7 %collective-permute-start.3 = (f32[9,8,128]{2,1,0:T(8,128)}, f32[9,8,128]{2,1,0:T(8,128)S(1)}, u32[]{:S(2)}, u32[]{:S(2)}) collective-permute-start(f32[9,8,128]{2,1,0:T(8,128)} %param.23), channel_id=1, source_target_pairs={{0,0},{1,1},{2,2},{3,3},{7,4},{6,5},{5,6},{4,7},{8,8},{9,9},{10,10... | collective-permute-start | bytes 110600 | tf_op jit(solution)/shard_map/ppermute | solution.py:560
  28.4 1.2 %copy-start.1 = (bf16[1536,480]{1,0:T(8,128)(2,1)}, bf16[1536,480]{1,0:T(8,128)(2,1)S(1)}, u32[]{:S(2)}) copy-start(bf16[1536,480]{1,0:T(8,128)(2,1)S(1)} %get-tuple-element.21.basis_ref) | copy-start | bytes 4423684
  35.0 13.4 %collective-permute-start.7 = (f32[176,128]{1,0:T(8,128)S(1)}, f32[176,128]{1,0:T(8,128)S(1)}, u32[]{:S(2)}, u32[]{:S(2)}) collective-permute-start(f32[176,128]{1,0:T(8,128)S(1)} %get-tuple-element.27.near_ref), channel_id=1, source_target_pairs={{0,32},{32,0},{64,96},{96,64},{128,160},{160,128},{192,224},{224,1... | collective-permute-start | bytes 270344 | tf_op jit(solution)/shard_map/ppermute | solution.py:580
  35.1 13.3 %collective-permute-start.6 = (f32[176,128]{1,0:T(8,128)S(1)}, f32[176,128]{1,0:T(8,128)S(1)}, u32[]{:S(2)}, u32[]{:S(2)}) collective-permute-start(f32[176,128]{1,0:T(8,128)S(1)} %get-tuple-element.27.near_ref), channel_id=1, source_target_pairs={{0,0},{32,64},{64,32},{96,128},{128,96},{160,192},{192,160},{224,2... | collective-permute-start | bytes 270344 | tf_op jit(solution)/shard_map/ppermute | solution.py:580
  37.1 11.3 %collective-permute-start.5 = (f32[176,128]{1,0:T(8,128)S(1)}, f32[176,128]{1,0:T(8,128)S(1)}, u32[]{:S(2)}, u32[]{:S(2)}) collective-permute-start(f32[176,128]{1,0:T(8,128)S(1)} %get-tuple-element.46), channel_id=1, source_target_pairs={{0,1},{1,0},{2,3},{3,2},{7,6},{6,7},{5,4},{4,5},{8,9},{9,8},{10,11... | collective-permute-start | bytes 270344 | tf_op jit(solution)/shard_map/ppermute | solution.py:579
  37.4 11.0 %collective-permute-start.4 = (f32[176,128]{1,0:T(8,128)S(1)}, f32[176,128]{1,0:T(8,128)S(1)}, u32[]{:S(2)}, u32[]{:S(2)}) collective-permute-start(f32[176,128]{1,0:T(8,128)S(1)} %get-tuple-element.47), channel_id=1, source_target_pairs={{0,0},{1,2},{2,1},{3,7},{7,3},{6,5},{5,6},{4,8},{8,4},{9,10},{10,9... | collective-permute-start | bytes 270344 | tf_op jit(solution)/shard_map/ppermute | solution.py:579
  48.5 18.7 %copy-start.15 = (f32[9,7]{1,0:T(8,128)S(1)}, f32[9,7]{1,0:T(8,128)}, u32[]{:S(2)}) copy-start(f32[9,7]{1,0:T(8,128)} %constant.116.clone) | copy-start | bytes 760
  48.5 19.4 %copy-start.13 = (f32[256]{0:T(256)S(1)}, f32[256]{0:T(256)}, u32[]{:S(2)}) copy-start(f32[256]{0:T(256)} %constant.111.clone) | copy-start | bytes 3076
  48.5 19.4 %copy-start.14 = (f32[128]{0:T(128)S(1)}, f32[128]{0:T(128)}, u32[]{:S(2)}) copy-start(f32[128]{0:T(128)} %constant.112.clone) | copy-start | bytes 1540
  48.5 19.4 %copy-start.17 = (f32[128,128]{1,0:T(8,128)S(1)}, f32[128,128]{1,0:T(8,128)}, u32[]{:S(2)}) copy-start(f32[128,128]{1,0:T(8,128)} %constant.114.clone) | copy-start | bytes 196612
  54.0 14.3 %copy-start.16 = (f32[128,128]{1,0:T(8,128)S(1)}, f32[128,128]{1,0:T(8,128)}, u32[]{:S(2)}) copy-start(f32[128,128]{1,0:T(8,128)} %constant.113.clone) | copy-start | bytes 196612
  54.0 14.8 %copy-start.18 = (f32[7]{0:T(128)S(1)}, f32[7]{0:T(128)}, u32[]{:S(2)}) copy-start(f32[7]{0:T(128)} %constant.115.clone) | copy-start | bytes 88
  54.0 33.6 %copy-start.3 = (f32[256,256]{1,0:T(8,128)S(1)}, f32[256,256]{1,0:T(8,128)}, u32[]{:S(2)}) copy-start(f32[256,256]{1,0:T(8,128)} %constant.117.clone.cy_ref) | copy-start | bytes 786436
  54.0 33.6 %copy-start.5 = (f32[128,128]{1,0:T(8,128)S(1)}, f32[128,128]{1,0:T(8,128)}, u32[]{:S(2)}) copy-start(f32[128,128]{1,0:T(8,128)} %constant.118.clone.cxt_ref) | copy-start | bytes 196612
  54.0 33.6 %copy-start.6 = (f32[8,128]{1,0:T(8,128)S(1)}, f32[8,128]{1,0:T(8,128)}, u32[]{:S(2)}) copy-start(f32[8,128]{1,0:T(8,128)} %constant.119.clone.ends_of_ref) | copy-start | bytes 12292
  54.0 33.6 %all-to-all-start.1 = ((f32[32,5,8,128]{3,2,1,0:T(8,128)}), f32[32,5,8,128]{3,2,1,0:T(8,128)S(1)}, u32[]{:S(2)}, u32[]{:S(2)}) async-start(f32[32,5,8,128]{3,2,1,0:T(8,128)} %bitcast.13), calls=%async_computation.1 | async-start | bytes 1310720 | tf_op jit(solution)/shard_map/all_to_all | solution.py:589
  68.4 0.9 copy-start.9
  68.4 28.0 %copy-start.4 = (f32[256,256]{1,0:T(8,128)S(1)}, f32[256,256]{1,0:T(8,128)}, u32[]{:S(2)}) copy-start(f32[256,256]{1,0:T(8,128)} %constant.121.clone.cyt_ref) | copy-start | bytes 786436
  68.4 28.0 %copy-start.7 = (f32[128,128]{1,0:T(8,128)S(1)}, f32[128,128]{1,0:T(8,128)}, u32[]{:S(2)}) copy-start(f32[128,128]{1,0:T(8,128)} %constant.120.clone.cx_ref) | copy-start | bytes 196612
  91.2 11.8 %all-to-all-start.2 = ((f32[8,16,256]{2,1,0:T(8,128)}), f32[8,16,256]{2,1,0:T(8,128)S(1)}, u32[]{:S(2)}, u32[]{:S(2)}) async-start(f32[8,16,256]{2,1,0:T(8,128)} %get-tuple-element.37), calls=%async_computation.2 | async-start | bytes 262144 | tf_op jit(solution)/shard_map/all_to_all | solution.py:611
  96.4 17.0 %copy-start = (f32[20,64,128]{2,1,0:T(8,128)S(1)}, f32[20,64,128]{2,1,0:T(8,128)}, u32[]{:S(2)}) copy-start(f32[20,64,128]{2,1,0:T(8,128)} %now_hbm.1) | copy-start | bytes 1966084
  96.4 17.0 %copy-start.2 = (f32[20,64,128]{2,1,0:T(8,128)S(1)}, f32[20,64,128]{2,1,0:T(8,128)}, u32[]{:S(2)}) copy-start(f32[20,64,128]{2,1,0:T(8,128)} %before_hbm.1) | copy-start | bytes 1966084
  98.3 11.3 %collective-permute-start.8 = (f32[5,64,128]{2,1,0:T(8,128)S(1)}, f32[5,64,128]{2,1,0:T(8,128)S(1)}, u32[]{:S(2)}, u32[]{:S(2)}) collective-permute-start(f32[5,64,128]{2,1,0:T(8,128)S(1)} %get-tuple-element.34), channel_id=1, source_target_pairs={{0,8},{8,16},{16,24},{24,0},{1,9},{9,17},{17,25},{25,1},{2,10},{10... | collective-permute-start | bytes 491528 | tf_op jit(solution)/shard_map/ppermute | solution.py:507
  99.2 11.5 %collective-permute-start.9 = (f32[5,64,128]{2,1,0:T(8,128)}, f32[5,64,128]{2,1,0:T(8,128)S(1)}, u32[]{:S(2)}, u32[]{:S(2)}) collective-permute-start(f32[5,64,128]{2,1,0:T(8,128)} %get-tuple-element.35), channel_id=1, source_target_pairs={{0,16},{8,24},{16,0},{24,8},{1,17},{9,25},{17,1},{25,9},{2,18},{10... | collective-permute-start | bytes 491528 | tf_op jit(solution)/shard_map/ppermute | solution.py:507
  101.4 9.3 %collective-permute-start.10 = (f32[5,64,128]{2,1,0:T(8,128)S(1)}, f32[5,64,128]{2,1,0:T(8,128)S(1)}, u32[]{:S(2)}, u32[]{:S(2)}) collective-permute-start(f32[5,64,128]{2,1,0:T(8,128)S(1)} %get-tuple-element.36), channel_id=1, source_target_pairs={{0,24},{8,0},{16,8},{24,16},{1,25},{9,1},{17,9},{25,17},{2,26},{10... | collective-permute-start | bytes 491528 | tf_op jit(solution)/shard_map/ppermute | solution.py:507
  103.1 7.7 %collective-permute-start.11 = (f32[16,256]{1,0:T(8,128)S(1)}, f32[16,256]{1,0:T(8,128)S(1)}, u32[]{:S(2)}, u32[]{:S(2)}) collective-permute-start(f32[16,256]{1,0:T(8,128)S(1)} %reduce_sum.9.t0_ref), channel_id=1, source_target_pairs={{0,8},{8,16},{16,24},{24,0},{1,9},{9,17},{17,25},{25,1},{2,10},{10... | collective-permute-start | bytes 49160 | tf_op jit(solution)/shard_map/ppermute | solution.py:507
  103.5 7.2 %collective-permute-start.12 = (f32[16,256]{1,0:T(8,128)S(1)}, f32[16,256]{1,0:T(8,128)S(1)}, u32[]{:S(2)}, u32[]{:S(2)}) collective-permute-start(f32[16,256]{1,0:T(8,128)S(1)} %reduce_sum.9.t0_ref), channel_id=1, source_target_pairs={{0,16},{8,24},{16,0},{24,8},{1,17},{9,25},{17,1},{25,9},{2,18},{10... | collective-permute-start | bytes 49160 | tf_op jit(solution)/shard_map/ppermute | solution.py:507
  109.6 3.7 %collective-permute-start.13 = (f32[16,256]{1,0:T(8,128)S(1)}, f32[16,256]{1,0:T(8,128)S(1)}, u32[]{:S(2)}, u32[]{:S(2)}) collective-permute-start(f32[16,256]{1,0:T(8,128)S(1)} %reduce_sum.9.t0_ref), channel_id=1, source_target_pairs={{0,24},{8,0},{16,8},{24,16},{1,25},{9,1},{17,9},{25,17},{2,26},{10... | collective-permute-start | bytes 49160 | tf_op jit(solution)/shard_map/ppermute | solution.py:507
